TPU v7x, 128 devices: a whole 4x4x4 slice. The times are simulated.
128 devices in a mesh: seq: 32 (over y, z, core), head: 2 (over x_hi), rep: 2 (over x_lo).
Axes of the slice: x: 4 (x_hi: 2, x_lo: 2; x = x_hi * 2 + x_lo), y: 4, z: 4, core: 2. Of those that a mesh axis runs over, the one named last changes fastest.
Arguments:
- queries: bfloat16 [2, 65536, 1024], P('rep', 'seq', 'head'), may hold values from -400 to 400
- key_states: bfloat16 [2, 65536, 1024], P('rep', 'seq', 'head'), may hold values from -6 to 6
- value_states: bfloat16 [2, 65536, 1024], P('rep', 'seq', 'head'), may hold values from -6 to 6
- out_grad: bfloat16 [2, 65536, 1024], P('rep', 'seq', 'head'), may hold values from -4 to 4
- key_mixer: bfloat16 [65536, 256], P('seq'), may hold values from -0.0234375 to 0.0234375
- value_mixer: bfloat16 [65536, 256], P('seq'), may hold values from -0.0234375 to 0.0234375
Outputs:
- query_grad: bfloat16 [2, 65536, 1024], P('rep', 'seq', 'head')
- key_grad: bfloat16 [2, 65536, 1024], P('rep', 'seq', 'head')
- value_grad: bfloat16 [2, 65536, 1024], P('rep', 'seq', 'head')
- key_mixer_grad: float32 [65536, 256], P(('seq', 'head', 'rep'))
- value_mixer_grad: float32 [65536, 256], P(('seq', 'head', 'rep'))
All inputs are finite; a program needn't handle non-finite values.
Results may differ from a plain program's by a relative error of at most 0.015.
Values may be sent and summed in bfloat16 or wider, within the bound.
No kernel may reach another device: no remote copies, remote signals or barrier semaphores. Data moves between devices by JAX's collectives and lax.ppermute only.
A program may use at most 128 MiB of HBM per device.

v0:
```python
import jax
import jax.numpy as jnp
from jax import lax
from jax.sharding import Mesh
from jax.sharding import PartitionSpec as P

DH = 64
KP = 256
SEQ = ("seq_0", "seq_1", "seq_2")
SEQ_HEAD_REP = ("seq_0", "seq_1", "seq_2", "head", "rep")


def cut_along(value, dim, size):
    shape = value.shape
    pieces = value.reshape(*shape[:dim], size, shape[dim] // size, *shape[dim + 1 :])
    return jnp.moveaxis(pieces, dim, 0)


def sent_and_summed(value, axis, dim):
    size = lax.axis_size(axis)
    pieces = lax.all_to_all(cut_along(value, dim, size), axis, 0, 0, tiled=True)
    return jnp.sum(pieces, axis=0)


def sum_in_two_steps(value, axes, dim):
    far, near = axes
    pieces = cut_along(value, dim, lax.axis_size(far))
    nearer = sent_and_summed(pieces, near, dim + 1)
    arrived = lax.all_to_all(nearer, far, split_axis=0, concat_axis=0, tiled=True)
    return arrived.sum(axis=0)


def rows_for(lines, size):
    spare = -len(lines) % size
    return jnp.pad(lines, [(0, spare)] + [(0, 0)] * (lines.ndim - 1))


def copy_for_each(value, axis):
    copies = jnp.broadcast_to(value, (lax.axis_size(axis), *value.shape))
    return lax.all_to_all(copies, axis, split_axis=0, concat_axis=0, tiled=True)


def joined_along(pieces, dim):
    pieces = jnp.moveaxis(pieces, 0, dim)
    shape = pieces.shape
    return pieces.reshape(*shape[:dim], shape[dim] * shape[dim + 1], *shape[dim + 2 :])


def gathered_by_axis(value, axes, dim):
    far, near = axes
    leading = copy_for_each(value, far)
    pieces = jnp.swapaxes(copy_for_each(leading, near), 0, 1)
    return joined_along(pieces.reshape(-1, *value.shape), dim)


def total_of(value, axes):
    own = sum_in_two_steps(
        rows_for(value, lax.axis_size(axes[0]) * lax.axis_size(axes[1])), axes, 0
    )
    whole = gathered_by_axis(own, axes, 0)
    return whole[: len(value)].reshape(value.shape)


def packed_total(arrays, axis):
    ends = [0]
    for a in arrays:
        ends.append(ends[-1] + a.size)
    running = total_of(jnp.concatenate([a.ravel() for a in arrays]), axis)
    return tuple((running[b:e].reshape(a.shape) for a, b, e in zip(arrays, ends, ends[1:])))


def in_one_piece(arrays, axis, dim, along):
    ends, at = ([], 0)
    for a in arrays[:-1]:
        at += a.shape[along]
        ends.append(at)
    both = jnp.concatenate(arrays, axis=along)
    return tuple(
        jnp.split(lax.psum_scatter(both, axis, scatter_dimension=dim, tiled=True), ends, axis=along)
    )


def on_device(queries, key_states, value_states, out_grad, key_mixer, value_mixer):
    tokens = queries.shape[1]
    width = queries.shape[2]
    local_heads = width // DH
    scale = 1.0 / DH**0.5
    query_heads = queries[0].reshape(tokens, local_heads, DH)
    key_flat = key_states[0]
    value_flat = value_states[0]
    key_heads = key_flat.reshape(tokens, local_heads, DH)
    value_heads = value_flat.reshape(tokens, local_heads, DH)
    grad_heads = out_grad[0].reshape(tokens, local_heads, DH)
    part_k = jnp.einsum("nk,nhd->hkd", key_mixer, key_heads, preferred_element_type=jnp.float32)
    part_v = jnp.einsum("nk,nhd->hkd", value_mixer, value_heads, preferred_element_type=jnp.float32)
    proj_k, proj_v = packed_total((part_k, part_v), (("seq_0", "seq_1"), "seq_2"))
    proj_k = proj_k.astype(jnp.bfloat16)
    proj_v = proj_v.astype(jnp.bfloat16)
    scores = (
        jnp.einsum("nhd,hkd->nhk", query_heads, proj_k, preferred_element_type=jnp.float32) * scale
    )
    probs = jax.nn.softmax(scores, axis=-1)
    probs_b = probs.astype(jnp.bfloat16)
    outs = jnp.einsum("nhk,hkd->nhd", probs_b, proj_v, preferred_element_type=jnp.float32)
    delta = jnp.sum(grad_heads.astype(jnp.float32) * outs, axis=2, keepdims=True)
    part_gv = jnp.einsum("nhk,nhd->hkd", probs_b, grad_heads, preferred_element_type=jnp.float32)
    grad_p = jnp.einsum("nhd,hkd->nhk", grad_heads, proj_v, preferred_element_type=jnp.float32)
    grad_s = (probs * (grad_p - delta) * scale).astype(jnp.bfloat16)
    query_grad = jnp.einsum("nhk,hkd->nhd", grad_s, proj_k, preferred_element_type=jnp.float32)
    query_grad = query_grad.astype(jnp.bfloat16).reshape(1, tokens, width)
    part_gk = jnp.einsum("nhk,nhd->hkd", grad_s, query_heads, preferred_element_type=jnp.float32)
    grad_pk, grad_pv = packed_total((part_gk, part_gv), (("seq_0", "seq_1"), "seq_2"))
    grad_pk = grad_pk.astype(jnp.bfloat16)
    grad_pv = grad_pv.astype(jnp.bfloat16)
    key_grad = jnp.einsum("nk,hkd->nhd", key_mixer, grad_pk, preferred_element_type=jnp.float32)
    key_grad = key_grad.astype(jnp.bfloat16).reshape(1, tokens, width)
    value_grad = jnp.einsum("nk,hkd->nhd", value_mixer, grad_pv, preferred_element_type=jnp.float32)
    value_grad = value_grad.astype(jnp.bfloat16).reshape(1, tokens, width)
    pk_cols = grad_pk.transpose(0, 2, 1).reshape(local_heads * DH, KP)
    pv_cols = grad_pv.transpose(0, 2, 1).reshape(local_heads * DH, KP)
    part_e = jnp.dot(key_flat, pk_cols, preferred_element_type=jnp.float32)
    part_f = jnp.dot(value_flat, pv_cols, preferred_element_type=jnp.float32)
    mixer_e, mixer_f = in_one_piece((part_e, part_f), ("head", "rep"), 0, 1)
    return (query_grad, key_grad, value_grad, mixer_e, mixer_f)


def solution(mesh):
    split = Mesh(
        mesh.devices.reshape(4, 4, 2, mesh.shape["head"], mesh.shape["rep"]),
        ("seq_0", "seq_1", "seq_2", "head", "rep"),
    )
    return jax.shard_map(
        on_device,
        mesh=split,
        in_specs=(
            P("rep", SEQ, "head"),
            P("rep", SEQ, "head"),
            P("rep", SEQ, "head"),
            P("rep", SEQ, "head"),
            P(SEQ, None),
            P(SEQ, None),
        ),
        out_specs=(
            P("rep", SEQ, "head"),
            P("rep", SEQ, "head"),
            P("rep", SEQ, "head"),
            P(SEQ_HEAD_REP, None),
            P(SEQ_HEAD_REP, None),
        ),
        check_vma=False,
    )
```

profile of v0, /device:TPU:3, one launch (start us, length us, event | category | flops | bytes accessed | tf_op | source)
XLA Modules:
  0.0 228.4 jit_solution(7260387180678241309)
XLA Ops:
  7.2 3.0 %copy.73 = bf16[1,2048,512]{1,2,0:T(8,128)(2,1)S(1)} copy(bf16[1,2048,512]{2,1,0:T(8,128)(2,1)} %param.7) | data formatting | bytes 4194304 | tf_op args[1]
  10.2 1.5 convolution_bitcast_fusion.3
  11.7 2.5 %copy.74 = f32[8,256,64]{2,1,0:T(8,128)} copy(f32[8,256,64]{1,2,0:T(8,128)} %convolution_bitcast_fusion.3) | data formatting | bytes 1048576 | tf_op jit(solution)/shard_map/nk,nhd->hkd/transpose | solution.py:94
  14.2 2.5 %concatenate.19 = f32[8,2,8192]{2,1,0:T(2,128)} reshape(f32[8,256,64]{2,1,0:T(8,128)} %copy.74) | data formatting | bytes 1048576 | tf_op jit(solution)/shard_map/concatenate | solution.py:68
  16.8 2.4 %copy.75 = bf16[1,2048,512]{1,2,0:T(8,128)(2,1)} copy(bf16[1,2048,512]{2,1,0:T(8,128)(2,1)S(1)} %copy-done.3) | data formatting | bytes 4194304 | tf_op args[2]
  19.1 2.6 %convolution_bitcast_fusion.2 = f32[8,256,64]{1,2,0:T(8,128)S(1)} fusion(bf16[2048,8,64]{0,2,1:T(8,128)(2,1)} %bitcast.111, bf16[2048,256]{1,0:T(8,128)(2,1)} %param.11), kind=kOutput, calls=%fused_computation.24 | convolution fusion | flops 536870912 | bytes 3670016 | tf_op jit(solution)/shard_map/nk,nhd->hkd/dot_general | solution.py:95
  23.9 4.9 %all_to_all.56 = f32[2,16,8192]{2,1,0:T(8,128)S(1)} all-to-all(f32[2,16,8192]{2,1,0:T(8,128)S(1)} %copy.77), channel_id=1, replica_groups=mesh['seq_0'=4,'seq_1'=4,'seq_2'=2,'head'=2,'rep'=2] {'seq_2'}, dimensions={0} | all-to-all | bytes 2097152 | tf_op jit(solution)/shard_map/all_to_all | solution.py:21
  29.4 18.2 %all_to_all.57 = f32[16,1,8192]{2,1,0:T(1,128)} all-to-all(f32[16,1,8192]{2,1,0:T(1,128)S(1)} %all_to_all.37), channel_id=1, replica_groups=mesh['seq_0'=4,'seq_1'=4,'seq_2'=2,'head'=2,'rep'=2] {'seq_0','seq_1'}, dimensions={0} | all-to-all | bytes 1048576 | tf_op jit(solution)/shard_map/all_to_all | solution.py:29
  47.6 1.4 reduce_sum.55
  49.0 1.2 broadcast_in_dim.15
  50.7 3.2 %reduce.2 = bf16[16,8192]{1,0:T(8,128)(2,1)S(1)} reduce(bf16[16,1,8192]{2,1,0:T(2,128)(2,1)} %broadcast_in_dim.15, bf16[]{:T(256)} %broadcast.26), dimensions={1}, to_apply=%broadcast_in_dim.15.reduce_sub_computation | reduce | bytes 524290 | tf_op jit(solution)/shard_map/broadcast_in_dim | solution.py:39
  54.8 3.7 %all-to-all-start.2 = ((bf16[16,2,4096]{2,1,0:T(2,128)(2,1)}), bf16[16,2,4096]{2,1,0:T(2,128)(2,1)S(1)}, u32[]{:S(2)}, u32[]{:S(2)}) async-start(bf16[16,2,4096]{2,1,0:T(2,128)(2,1)} %reshape.75), calls=%async_computation.2 | async-start | bytes 524288 | tf_op jit(solution)/shard_map/all_to_all | solution.py:40
  58.6 2.4 %copy.79 = bf16[1,2048,512]{1,2,0:T(8,128)(2,1)} copy(bf16[1,2048,512]{2,1,0:T(8,128)(2,1)S(1)} %copy-done.6) | data formatting | bytes 4194304 | tf_op args[0]
  61.0 2.9 %copy.82 = bf16[1,2048,512]{1,2,0:T(8,128)(2,1)S(1)} copy(bf16[1,2048,512]{2,1,0:T(8,128)(2,1)} %param.9) | data formatting | bytes 4194304 | tf_op args[3]
  63.9 1.9 all-to-all-done.2
  66.8 1.3 copy.121
  68.2 6.8 %all_to_all.58 = bf16[2,16,8192]{2,1,0:T(8,128)(2,1)S(1)} all-to-all(bf16[2,16,8192]{2,1,0:T(8,128)(2,1)S(1)} %broadcast_in_dim.16), channel_id=1, replica_groups=mesh['seq_0'=4,'seq_1'=4,'seq_2'=2,'head'=2,'rep'=2] {'seq_2'}, dimensions={0} | all-to-all | bytes 1048576 | tf_op jit(solution)/shard_map/all_to_all | solution.py:40
  76.0 1.2 convert_element_type.44
  77.2 1.2 copy.78
  78.4 1.2 convert_element_type.43
  79.6 10.1 %fusion.24 = (f32[2048,8]{0,1:T(8,128)S(1)}, f32[2048,8,256]{0,2,1:T(8,128)}) fusion(bf16[8,256,64]{2,1,0:T(8,128)(2,1)} %convert_element_type.43, bf16[2048,8,64]{0,2,1:T(8,128)(2,1)} %bitcast.108), kind=kOutput, calls=%fused_computation.40 | convolution fusion | flops 549454080 | bytes 19202048 | tf_op jit(solution)/shard_map/sub | solution.py:102
  89.7 7.2 %fusion.10 = bf16[2048,8,256]{0,2,1:T(8,128)(2,1)S(1)} fusion(f32[2048,8,256]{0,2,1:T(8,128)} %get-tuple-element.32, f32[2048,8]{0,1:T(8,128)S(1)} %get-tuple-element.31), kind=kLoop, calls=%fused_computation.12 | loop fusion | flops 8388608 | bytes 25231360 | tf_op jit(solution)/shard_map/convert_element_type | solution.py:103
  96.9 3.3 %fusion.26 = f32[8,256,64]{2,1,0:T(8,128)} fusion(bf16[2048,8,256]{0,2,1:T(8,128)(2,1)S(1)} %fusion.10, bf16[2048,8,64]{0,2,1:T(8,128)(2,1)S(1)} %bitcast.100), kind=kOutput, calls=%fused_computation.42 | convolution fusion | flops 536870912 | bytes 11010048 | tf_op jit(solution)/shard_map/nhk,nhd->hkd/dot_general | solution.py:106
  100.2 1.8 fusion.11
  102.0 7.8 %fusion.3 = bf16[2048,8,256]{0,2,1:T(8,128)(2,1)S(1)} fusion(f32[2048,8]{0,1:T(8,128)S(1)} %fusion.11, f32[2048,8,256]{0,2,1:T(8,128)} %get-tuple-element.32, f32[2048,8]{0,1:T(8,128)S(1)} %get-tuple-element.31, bf16[8,256,64]{2,1,0:T(8,128)(2,1)S(1)} %copy-done.5, bf16[2048,8,64]{0,2,1:T(8,128)(2,1)S(1)} %bitcast.102), kind=kOutput, calls=%fused_computation.4 | convolution fusion | flops 557842432 | bytes 27656192 | tf_op jit(solution)/shard_map/nhd,hkd->nhk/dot_general | solution.py:107
  109.8 3.2 %copy-done.1 = bf16[2048,8,256]{0,2,1:T(8,128)(2,1)} copy-done((bf16[2048,8,256]{0,2,1:T(8,128)(2,1)}, bf16[2048,8,256]{0,2,1:T(8,128)(2,1)S(1)}, u32[]{:S(2)}) %copy-start.1) | copy-done | bytes 8388632
  113.1 3.3 %fusion.25 = f32[8,256,64]{2,1,0:T(8,128)} fusion(bf16[2048,8,256]{0,2,1:T(8,128)(2,1)S(1)} %fusion.3, bf16[2048,8,64]{0,2,1:T(8,128)(2,1)S(1)} %bitcast.109), kind=kOutput, calls=%fused_computation.41 | convolution fusion | flops 536870912 | bytes 11010048 | tf_op jit(solution)/shard_map/nhk,nhd->hkd/dot_general | solution.py:111
  116.3 1.8 concatenate.22
  119.9 4.5 %all_to_all.59 = f32[2,16,8192]{2,1,0:T(8,128)S(1)} all-to-all(f32[2,16,8192]{2,1,0:T(8,128)S(1)} %copy.92), channel_id=1, replica_groups=mesh['seq_0'=4,'seq_1'=4,'seq_2'=2,'head'=2,'rep'=2] {'seq_2'}, dimensions={0} | all-to-all | bytes 2097152 | tf_op jit(solution)/shard_map/all_to_all | solution.py:21
  125.0 14.0 %all_to_all.60 = f32[16,1,8192]{2,1,0:T(1,128)S(1)} all-to-all(f32[16,1,8192]{2,1,0:T(1,128)S(1)} %all_to_all.43), channel_id=1, replica_groups=mesh['seq_0'=4,'seq_1'=4,'seq_2'=2,'head'=2,'rep'=2] {'seq_0','seq_1'}, dimensions={0} | all-to-all | bytes 1048576 | tf_op jit(solution)/shard_map/all_to_all | solution.py:29
  139.8 2.2 reduce.3
  142.2 10.8 %all_to_all.61 = bf16[16,2,4096]{2,1,0:T(2,128)(2,1)S(1)} all-to-all(bf16[16,2,4096]{2,1,0:T(2,128)(2,1)S(1)} %reshape.77), channel_id=1, replica_groups=mesh['seq_0'=4,'seq_1'=4,'seq_2'=2,'head'=2,'rep'=2] {'seq_0','seq_1'}, dimensions={0} | all-to-all | bytes 524288 | tf_op jit(solution)/shard_map/all_to_all | solution.py:40
  153.7 6.9 %all_to_all.62 = bf16[2,16,8192]{2,1,0:T(8,128)(2,1)S(1)} all-to-all(bf16[2,16,8192]{2,1,0:T(8,128)(2,1)S(1)} %broadcast_in_dim.18), channel_id=1, replica_groups=mesh['seq_0'=4,'seq_1'=4,'seq_2'=2,'head'=2,'rep'=2] {'seq_2'}, dimensions={0} | all-to-all | bytes 1048576 | tf_op jit(solution)/shard_map/all_to_all | solution.py:40
  161.5 1.2 convert_element_type.53
  162.7 1.2 copy.98
  163.9 1.9 copy.93
  165.9 2.1 convert_element_type.50
  168.0 1.9 copy.97
  169.9 1.9 convolution_bitcast_fusion.1
  172.6 2.5 %pad_maximum_fusion = f32[2048,512]{0,1:T(8,128)} fusion(f32[2048,256]{0,1:T(8,128)S(1)} %convolution_bitcast_fusion, f32[2048,256]{0,1:T(8,128)S(1)} %convolution_bitcast_fusion.1), kind=kLoop, calls=%fused_computation.13 | loop fusion | flops 1048576 | bytes 8388608 | tf_op jit(solution)/shard_map/concatenate | solution.py:77
  175.1 5.2 %convolution_convert_fusion = bf16[8,64,2048]{2,1,0:T(8,128)(2,1)S(1)} fusion(bf16[8,256,64]{2,1,0:T(8,128)(2,1)} %convert_element_type.43, bf16[2048,8,256]{0,2,1:T(8,128)(2,1)} %copy-done.1), kind=kOutput, calls=%fused_computation.16 | convolution fusion | flops 537919488 | bytes 10747904 | tf_op jit(solution)/shard_map/nhk,hkd->nhd/dot_general | solution.py:109
  180.3 2.5 %copy.99 = bf16[1,2048,512]{2,1,0:T(8,128)(2,1)} copy(bf16[1,2048,512]{1,2,0:T(8,128)(2,1)S(1)} %bitcast.103) | data formatting | bytes 4194304
  182.8 2.4 %convolution_convert_fusion.2 = bf16[8,64,2048]{2,1,0:T(8,128)(2,1)S(1)} fusion(bf16[8,256,64]{2,1,0:T(8,128)(2,1)} %convert_element_type.50, bf16[2048,256]{1,0:T(8,128)(2,1)S(1)} %copy-done), kind=kOutput, calls=%fused_computation.18 | convolution fusion | flops 537919488 | bytes 3407872 | tf_op jit(solution)/shard_map/nk,hkd->nhd/dot_general | solution.py:115
  185.1 2.5 %copy.100 = bf16[1,2048,512]{2,1,0:T(8,128)(2,1)} copy(bf16[1,2048,512]{1,2,0:T(8,128)(2,1)S(1)} %bitcast.104) | data formatting | bytes 4194304
  187.6 2.7 %convolution_convert_fusion.1 = bf16[8,64,2048]{2,1,0:T(8,128)(2,1)S(1)} fusion(bf16[8,256,64]{2,1,0:T(8,128)(2,1)} %convert_element_type.53, bf16[2048,256]{1,0:T(8,128)(2,1)} %param.11), kind=kOutput, calls=%fused_computation.17 | convolution fusion | flops 537919488 | bytes 3407872 | tf_op jit(solution)/shard_map/nk,hkd->nhd/dot_general | solution.py:117
  190.3 2.5 %copy.101 = bf16[1,2048,512]{2,1,0:T(8,128)(2,1)} copy(bf16[1,2048,512]{1,2,0:T(8,128)(2,1)S(1)} %bitcast.105) | data formatting | bytes 4194304
  192.8 25.4 %reduce-scatter.2.cloned.1.call-done = f32[512,512]{0,1:T(8,128)} async-done(((f32[2048,512]{0,1:T(8,128)}), f32[512,512]{0,1:T(8,128)}) %reduce-scatter.2.cloned.1.call-update) | async-done | bytes 1048592 | tf_op jit(solution)/shard_map/reduce_scatter | solution.py:79
  218.3 1.3 fusion.21
  (49 shorter events, 13.9 us)
Async XLA Ops:
  7.2 3.0 %copy-start = (bf16[2048,256]{1,0:T(8,128)(2,1)S(1)}, bf16[2048,256]{1,0:T(8,128)(2,1)}, u32[]{:S(2)}) copy-start(bf16[2048,256]{1,0:T(8,128)(2,1)} %param.10) | copy-start | bytes 3145732
  11.7 5.0 %copy-start.3 = (bf16[1,2048,512]{2,1,0:T(8,128)(2,1)S(1)}, bf16[1,2048,512]{2,1,0:T(8,128)(2,1)}, u32[]{:S(2)}) copy-start(bf16[1,2048,512]{2,1,0:T(8,128)(2,1)} %param.8) | copy-start | bytes 6291460
  21.7 1.0 copy-start.8
  29.4 29.2 %copy-start.6 = (bf16[1,2048,512]{2,1,0:T(8,128)(2,1)S(1)}, bf16[1,2048,512]{2,1,0:T(8,128)(2,1)}, u32[]{:S(2)}) copy-start(bf16[1,2048,512]{2,1,0:T(8,128)(2,1)} %param.6) | copy-start | bytes 6291460
  54.8 11.1 %all-to-all-start.2 = ((bf16[16,2,4096]{2,1,0:T(2,128)(2,1)}), bf16[16,2,4096]{2,1,0:T(2,128)(2,1)S(1)}, u32[]{:S(2)}, u32[]{:S(2)}) async-start(bf16[16,2,4096]{2,1,0:T(2,128)(2,1)} %reshape.75), calls=%async_computation.2 | async-start | bytes 524288 | tf_op jit(solution)/shard_map/all_to_all | solution.py:40
  58.5 159.7 %reduce-scatter.2.cloned.1.call-start = ((), (), s32[]{:S(2)}) async-start(), calls=%async_computation.9 | async-start | bytes 5242880 | tf_op jit(solution)/shard_map/reduce_scatter | solution.py:79
  96.8 3.4 %copy-start.5 = (bf16[8,256,64]{2,1,0:T(8,128)(2,1)S(1)}, bf16[8,256,64]{2,1,0:T(8,128)(2,1)}, u32[]{:S(2)}) copy-start(bf16[8,256,64]{2,1,0:T(8,128)(2,1)} %convert_element_type.44) | copy-start | bytes 786436
  102.0 11.1 %copy-start.7 = (bf16[1,2048,512]{1,2,0:T(8,128)(2,1)S(1)}, bf16[1,2048,512]{1,2,0:T(8,128)(2,1)}, u32[]{:S(2)}) copy-start(bf16[1,2048,512]{1,2,0:T(8,128)(2,1)} %copy.79) | copy-start | bytes 6291460
  109.8 3.2 %copy-start.1 = (bf16[2048,8,256]{0,2,1:T(8,128)(2,1)}, bf16[2048,8,256]{0,2,1:T(8,128)(2,1)S(1)}, u32[]{:S(2)}) copy-start(bf16[2048,8,256]{0,2,1:T(8,128)(2,1)S(1)} %fusion.3) | copy-start | bytes 25165828
  116.3 1.8 copy-start.9
  161.3 8.7 %copy-start.2 = (bf16[1,2048,512]{2,1,0:T(8,128)(2,1)S(1)}, bf16[1,2048,512]{2,1,0:T(8,128)(2,1)}, u32[]{:S(2)}) copy-start(bf16[1,2048,512]{2,1,0:T(8,128)(2,1)} %param.7) | copy-start | bytes 6291460
  169.9 1.9 copy-start.4
Sparse Core Ops, SparseCore 0:
  175.2 43.0 reduce-scatter.1
where the time goes:
time: 232 us; the launch traced here: 228 us
  blocking collectives  66.1 us (28%)
  local copies, waits for them, and re-layouts  55.4 us (24%)
  matrix products  43.2 us (19%)
  waiting for transfers between devices  27.4 us (12%)
  other arithmetic  18 us (8%)
  between operations  14.4 us (6%)
  starting transfers between devices  3.77 us (2%)
    all_to_all x2, blocking collectives, sum_in_two_steps(): lax.all_to_all(nearer, far, split_axis=0, concat_axis=0, tiled=True)  32.2 us
    unnamed x35, local copies, waits for them, and re-layouts  27.5 us
    reduce_scatter x1, waiting for transfers between devices, in_one_piece(): lax.psum_scatter(both, axis, scatter_dimension=dim, tiled=True)  25.4 us
    all_to_all x3, blocking collectives, copy_for_each(): return lax.all_to_all(copies, axis, split_axis=0, concat_axis=0, tiled=True)  24.5 us
    sub x1, matrix products, on_device(): probs = jax.nn.softmax(scores, axis=-1)  10.1 us
    all_to_all x2, blocking collectives, sent_and_summed(): pieces = lax.all_to_all(cut_along(value, dim, size), axis, 0, 0, tiled=True)  9.4 us
    dot_general x1, matrix products, on_device(): jnp.einsum('nhd,hkd->nhk', grad_heads, proj_v, preferred_element_type=jnp...  7.85 us
    convert_element_type x1, other arithmetic, on_device(): probs_b = probs.astype(jnp.bfloat16)  7.17 us
  transfers between devices with their start and end apart: 2, of which 2 were waited for; matrix products, arithmetic and copies ran while one was open for 10% of the time, Pallas kernels for 0%

commit v1 on v0

v1 whole, which is shorter than its diff:
```python
import functools

import jax
import jax.numpy as jnp
from jax import lax
from jax.experimental import pallas as pl
from jax.experimental.pallas import tpu as pltpu
from jax.sharding import Mesh
from jax.sharding import PartitionSpec as P

DH = 64
KP = 256
LOG2E = 1.4426950408889634
SEQ = ("seq_0", "seq_1", "seq_2")
SEQ_HEAD_REP = ("seq_0", "seq_1", "seq_2", "head", "rep")
BF = jnp.bfloat16
F32 = jnp.float32
NT = (((1,), (1,)), ((), ()))
TN = (((0,), (0,)), ((), ()))
VM = pl.BlockSpec(memory_space=pltpu.VMEM)
PARAMS = dict(vmem_limit_bytes=56 * 1024 * 1024)


def shape_of(rows, cols, kind):
    return jax.ShapeDtypeStruct((rows, cols), kind)


def cost(flops, moved):
    return pl.CostEstimate(flops=flops, bytes_accessed=moved, transcendentals=0)


def split_by_core(core, both, keep, send):
    half = KP // 2
    for at, total in enumerate(both):
        out = pl.ds(at * half, half)
        keep[out, :] = total[pl.ds(core * half, half), :].astype(keep.dtype)
        send[out, :] = total[pl.ds((1 - core) * half, half), :].astype(send.dtype)


def project_kernel(k_ref, v_ref, e_ref, f_ref, keep, send, sum_k, sum_v):
    step = pl.program_id(0)
    part_k = lax.dot_general(e_ref[...], k_ref[...], TN, preferred_element_type=F32)
    part_v = lax.dot_general(f_ref[...], v_ref[...], TN, preferred_element_type=F32)

    @pl.when(step == 0)
    def _():
        sum_k[...] = part_k
        sum_v[...] = part_v

    @pl.when(step > 0)
    def _():
        sum_k[...] += part_k
        sum_v[...] += part_v

    @pl.when(step == pl.num_programs(0) - 1)
    def _():
        split_by_core(lax.axis_index("seq_2"), (sum_k, sum_v), keep, send)


def project(k, v, e, f):
    tokens, width = k.shape
    rows = 512
    wide = pl.BlockSpec((rows, width), lambda i: (i, 0))
    thin = pl.BlockSpec((rows, KP), lambda i: (i, 0))
    return pl.pallas_call(
        project_kernel,
        grid=(tokens // rows,),
        in_specs=[wide, wide, thin, thin],
        out_specs=[pl.BlockSpec((KP, width), lambda i: (0, 0))] * 2,
        out_shape=[shape_of(KP, width, F32)] * 2,
        scratch_shapes=[pltpu.VMEM((KP, width), F32)] * 2,
        compiler_params=pltpu.CompilerParams(**PARAMS),
        cost_estimate=cost(4 * tokens * width * KP, 6 << 20),
        name="project",
    )(k, v, e, f)


def core_sum_kernel(keep, got, own, send_1, send_2, send_3):
    size = lax.axis_size("seq_0")
    me = lax.axis_index("seq_0")
    rows = KP // 2 // size
    for step, out in enumerate((own, send_1, send_2, send_3)):
        to = lax.rem(me + step, size)
        for at in range(2):
            cut = pl.ds(at * KP // 2 + to * rows, rows)
            total = keep[cut, :] + got[cut, :].astype(F32)
            out[at * rows : (at + 1) * rows, :] = total.astype(out.dtype)


def y_sum_kernel(own, got_1, got_2, got_3, out):
    total = (own[...] + got_2[...].astype(F32)) + (
        got_1[...].astype(F32) + got_3[...].astype(F32)
    )
    out[...] = total.astype(out.dtype)


def z_sum_kernel(own, got_1, got_2, got_3, out):
    total = (own[...].astype(F32) + got_2[...].astype(F32)) + (
        got_1[...].astype(F32) + got_3[...].astype(F32)
    )
    out[...] = total.astype(out.dtype)


def small(kernel, outs, name, *args):
    return pl.pallas_call(
        kernel,
        in_specs=[VM] * len(args),
        out_specs=[VM] * len(outs),
        out_shape=list(outs),
        compiler_params=pltpu.CompilerParams(**PARAMS),
        cost_estimate=cost(1 << 20, 1 << 20),
        name=name,
    )(*args)


def ring(size, step):
    return [(i, (i + step) % size) for i in range(size)]


def shifted(value, axis, step):
    return lax.ppermute(value, axis, ring(lax.axis_size(axis), step))


def total_over_seq(keep, send, wire):
    width = keep.shape[1]
    rows = KP // lax.axis_size("seq_0")
    got = shifted(send, "seq_2", 1)
    own, *sends = small(
        core_sum_kernel,
        [shape_of(rows, width, F32)] + [shape_of(rows, width, wire)] * 3,
        "core_sum",
        keep,
        got,
    )
    got = [shifted(s, "seq_0", i + 1) for i, s in enumerate(sends)]
    (part,) = small(y_sum_kernel, [shape_of(rows, width, wire)], "y_sum", own, *got)
    got = [shifted(part, "seq_1", i + 1) for i in range(3)]
    (piece,) = small(z_sum_kernel, [shape_of(rows, width, BF)], "z_sum", part, *got)
    pieces = [piece] + [shifted(piece, "seq_0", i + 1) for i in range(3)]
    return pieces + [shifted(p, "seq_2", 1) for p in pieces]


def assemble(pieces, first, second):
    size = lax.axis_size("seq_0")
    me = lax.axis_index("seq_0")
    core = lax.axis_index("seq_2")
    rows = KP // 2 // size
    for at, piece in enumerate(pieces):
        of = lax.rem(me + size - at % size, size)
        half = core if at < size else 1 - core
        out = pl.ds(pl.multiple_of(half * (KP // 2) + of * rows, rows), rows)
        first[out, :] = piece[:rows, :]
        second[out, :] = piece[rows:, :]


def attend_kernel(*refs):
    q_ref, g_ref, *pieces = refs[:10]
    dq_ref, keep, send = refs[10:13]
    pk, pv, pk_t, sum_k, sum_v = refs[13:]
    step = pl.program_id(0)
    width = q_ref.shape[1]
    scale = 1.0 / DH**0.5

    @pl.when(step == 0)
    def _():
        assemble(pieces, pk, pv)
        pk_t[...] = pk[...].T
        sum_k[...] = jnp.zeros_like(sum_k)
        sum_v[...] = jnp.zeros_like(sum_v)

    low = lax.broadcasted_iota(jnp.int32, (KP, 2 * DH), 1) < DH

    def pair(j, carry):
        at = pl.multiple_of(j * 2 * DH, 2 * DH)
        cols = pl.ds(at, 2 * DH)
        q = q_ref[:, cols]
        g = g_ref[:, cols]
        pk_pair = pk[:, cols]
        pv_pair = pv[:, cols]
        none = jnp.zeros_like(pk_pair)
        dpk, dpv, dq_t = [], [], []
        for e in range(2):
            mine = low if e == 0 else jnp.logical_not(low)
            s = lax.dot_general(
                jnp.where(mine, pk_pair, none), q, NT, preferred_element_type=F32
            )
            top = jnp.max(s, axis=0, keepdims=True)
            ex = jnp.exp2((s - top) * (scale * LOG2E))
            share = scale / jnp.sum(ex, axis=0, keepdims=True)
            p = ex * share
            pb = p.astype(BF)
            gp = lax.dot_general(
                jnp.where(mine, pv_pair, none), g, NT, preferred_element_type=F32
            )
            delta = jnp.sum(pb.astype(F32) * gp, axis=0, keepdims=True) * (1.0 / scale)
            ds = (p * (gp - delta)).astype(BF)
            dpv.append(jnp.dot(pb, g, preferred_element_type=F32))
            dpk.append(jnp.dot(ds, q, preferred_element_type=F32))
            rows = pl.ds(pl.multiple_of(at + e * DH, DH), DH)
            dq_t.append(jnp.dot(pk_t[rows, :], ds, preferred_element_type=F32))
        sum_k[:, cols] += jnp.where(low, dpk[0], dpk[1])
        sum_v[:, cols] += jnp.where(low, dpv[0], dpv[1])
        dq_ref[:, cols] = jnp.concatenate(dq_t, axis=0).T.astype(BF)
        return carry

    lax.fori_loop(0, width // (2 * DH), pair, 0)

    @pl.when(step == pl.num_programs(0) - 1)
    def _():
        sum_v[...] = sum_v[...] * (1.0 / scale)
        split_by_core(lax.axis_index("seq_2"), (sum_k, sum_v), keep, send)


def attend(q, g, pieces):
    tokens, width = q.shape
    rows = 512
    wide = pl.BlockSpec((rows, width), lambda i: (i, 0))
    still = pl.BlockSpec((KP, width), lambda i: (0, 0))
    return pl.pallas_call(
        attend_kernel,
        grid=(tokens // rows,),
        in_specs=[wide, wide] + [VM] * len(pieces),
        out_specs=[wide, still, still],
        out_shape=[
            shape_of(tokens, width, BF),
            shape_of(KP, width, F32),
            shape_of(KP, width, BF),
        ],
        scratch_shapes=[
            pltpu.VMEM((KP, width), BF),
            pltpu.VMEM((KP, width), BF),
            pltpu.VMEM((width, KP), BF),
            pltpu.VMEM((KP, width), F32),
            pltpu.VMEM((KP, width), F32),
        ],
        compiler_params=pltpu.CompilerParams(**PARAMS),
        cost_estimate=cost(16 * tokens * width * KP, 8 << 20),
        name="attend",
    )(q, g, *pieces)


def mixer_part_kernel(at_ref, k_ref, v_ref, *refs):
    pieces, (out, dpk, dpv) = refs[:-3], refs[-3:]
    assemble(pieces, dpk, dpv)
    out[:, :KP] = lax.dot_general(
        k_ref[...], dpk[...], NT, preferred_element_type=F32
    ).astype(out.dtype)
    out[:, KP:] = lax.dot_general(
        v_ref[...], dpv[...], NT, preferred_element_type=F32
    ).astype(out.dtype)


def mixer_part(at, k, v, pieces, rows, kind):
    width = k.shape[1]
    wide = pl.BlockSpec((rows, width), lambda i, at: (at[0], 0))
    return pl.pallas_call(
        mixer_part_kernel,
        grid_spec=pltpu.PrefetchScalarGridSpec(
            num_scalar_prefetch=1,
            grid=(1,),
            in_specs=[wide, wide] + [VM] * len(pieces),
            out_specs=pl.BlockSpec((rows, 2 * KP), lambda i, at: (0, 0)),
            scratch_shapes=[pltpu.VMEM((KP, width), BF)] * 2,
        ),
        out_shape=shape_of(rows, 2 * KP, kind),
        compiler_params=pltpu.CompilerParams(**PARAMS),
        cost_estimate=cost(4 * rows * width * KP, 2 << 20),
        name="mixer_part",
    )(at, k, v, *pieces)


def input_grads_kernel(e_ref, f_ref, *refs):
    pieces, (dk, dv, dpk, dpv) = refs[:-4], refs[-4:]

    @pl.when(pl.program_id(0) == 0)
    def _():
        assemble(pieces, dpk, dpv)

    dk[...] = jnp.dot(e_ref[...], dpk[...], preferred_element_type=F32).astype(BF)
    dv[...] = jnp.dot(f_ref[...], dpv[...], preferred_element_type=F32).astype(BF)


def input_grads(e, f, pieces):
    tokens, width = e.shape[0], pieces[0].shape[1]
    rows = 512
    wide = pl.BlockSpec((rows, width), lambda i: (i, 0))
    thin = pl.BlockSpec((rows, KP), lambda i: (i, 0))
    return pl.pallas_call(
        input_grads_kernel,
        grid=(tokens // rows,),
        in_specs=[thin, thin] + [VM] * len(pieces),
        out_specs=[wide, wide],
        out_shape=[shape_of(tokens, width, BF)] * 2,
        scratch_shapes=[pltpu.VMEM((KP, width), BF)] * 2,
        compiler_params=pltpu.CompilerParams(**PARAMS),
        cost_estimate=cost(4 * tokens * width * KP, 6 << 20),
        name="input_grads",
    )(e, f, *pieces)


def mixer_sum_kernel(own, got_1, got_2, got_3, de, df):
    total = (own[...] + got_2[...].astype(F32)) + (
        got_1[...].astype(F32) + got_3[...].astype(F32)
    )
    de[...] = total[:, :KP]
    df[...] = total[:, KP:]


def on_device(queries, key_states, value_states, out_grad, key_mixer, value_mixer):
    q, k, v, g = queries[0], key_states[0], value_states[0], out_grad[0]
    tokens, width = q.shape
    across = ("head", "rep")
    keep, send = project(k, v, key_mixer, value_mixer)
    pieces = total_over_seq(keep, send, F32)
    query_grad, keep, send = attend(q, g, pieces)
    pieces = total_over_seq(keep, send, BF)
    me = lax.axis_index(across)
    near = lax.axis_size(across)
    rows = tokens // near
    got = {}
    for step in (2, 1, 3):
        at = lax.rem(me + step, near).reshape(1)
        got[step] = shifted(mixer_part(at, k, v, pieces, rows, BF), across, step)
    own = mixer_part(me.reshape(1), k, v, pieces, rows, F32)
    key_grad, value_grad = input_grads(key_mixer, value_mixer, pieces)
    mixer_e, mixer_f = small(
        mixer_sum_kernel,
        [shape_of(rows, KP, F32)] * 2,
        "mixer_sum",
        own,
        got[1],
        got[2],
        got[3],
    )
    return (query_grad[None], key_grad[None], value_grad[None], mixer_e, mixer_f)


def solution(mesh):
    split = Mesh(
        mesh.devices.reshape(4, 4, 2, mesh.shape["head"], mesh.shape["rep"]),
        ("seq_0", "seq_1", "seq_2", "head", "rep"),
    )
    data = P("rep", SEQ, "head")
    return jax.shard_map(
        on_device,
        mesh=split,
        in_specs=(data, data, data, data, P(SEQ, None), P(SEQ, None)),
        out_specs=(data, data, data, P(SEQ_HEAD_REP, None), P(SEQ_HEAD_REP, None)),
        check_vma=False,
    )
```

time: 232 us -> 148 us (0.64); the launches traced: 228 us -> 148 us
  blocking collectives: 66.1 us -> 0 us
  Pallas kernels: 0 us -> 58.8 us
  local copies, waits for them, and re-layouts: 55.4 us -> 6.14 us
  matrix products: 43.2 us -> 0 us
  starting transfers between devices: 3.77 us -> 40.2 us
  other arithmetic: 18 us -> 0 us
  waiting for transfers between devices: 27.4 us -> 41.6 us
  between operations: 14.4 us -> 0.8 us
    all_to_all x7 -> x0, blocking collectives: 66.1 us -> none  [the longest x2 32.2 us: sum_in_two_steps(): lax.all_to_all(nearer, far, split_axis=0, concat_axis=0, tiled=True)]
    pallas_call x0 -> x14, Pallas kernels: none -> 58.8 us  [the longest x1 24.4 us: attend(): pl.pallas_call(attend_kernel, grid=(tokens // rows,), in_specs=[wide, wid...]
    ppermute x0 -> x31, waiting for transfers between devices: none -> 41.6 us  [shifted(): return lax.ppermute(value, axis, ring(lax.axis_size(axis), step))]
    ppermute x0 -> x31, starting transfers between devices: none -> 40.2 us  [shifted(): return lax.ppermute(value, axis, ring(lax.axis_size(axis), step))]
    dot_general x11 -> x0, matrix products: 33.1 us -> none  [the longest x1 7.85 us: on_device(): jnp.einsum('nhd,hkd->nhk', grad_heads, proj_v, preferred_element_type=jnp...]
    reduce_scatter x1 -> x0, waiting for transfers between devices: 25.4 us -> none  [in_one_piece(): lax.psum_scatter(both, axis, scatter_dimension=dim, tiled=True)]
    unnamed x35 -> x62, local copies, waits for them, and re-layouts: 27.5 us -> 6.14 us
    sub x1 -> x0, matrix products: 10.1 us -> none  [on_device(): probs = jax.nn.softmax(scores, axis=-1)]
  transfers between devices with their start and end apart: 2 -> 31, of which waited for: 2 -> 17; matrix products, arithmetic and copies ran while one was open for 10% -> 0% of each run, Pallas kernels for 0% -> 9%
where the time goes in v1:
time: 148 us
  Pallas kernels  58.8 us (40%)
  waiting for transfers between devices  41.6 us (28%)
  starting transfers between devices  40.2 us (27%)
  local copies, waits for them, and re-layouts  6.14 us (4%)
    ppermute x31, waiting for transfers between devices, shifted(): return lax.ppermute(value, axis, ring(lax.axis_size(axis), step))  41.6 us
    ppermute x31, starting transfers between devices, shifted(): return lax.ppermute(value, axis, ring(lax.axis_size(axis), step))  40.2 us
    pallas_call x1, Pallas kernels, attend(): pl.pallas_call(attend_kernel, grid=(tokens // rows,), in_specs=[wide, wid...  24.4 us
    pallas_call x7, Pallas kernels, small(): pl.pallas_call(kernel, in_specs=[VM] * len(args), out_specs=[VM] * len(ou...  13.3 us
    pallas_call x4, Pallas kernels, mixer_part(): pl.pallas_call(mixer_part_kernel, grid_spec=pltpu.PrefetchScalarGridSpec(...  10.6 us
    unnamed x62, local copies, waits for them, and re-layouts  6.14 us
    pallas_call x1, Pallas kernels, project(): pl.pallas_call(project_kernel, grid=(tokens // rows,), in_specs=[wide, wi...  5.55 us
    pallas_call x1, Pallas kernels, input_grads(): pl.pallas_call(input_grads_kernel, grid=(tokens // rows,), in_specs=[thin...  4.82 us
  transfers between devices with their start and end apart: 31, of which 17 were waited for; matrix products, arithmetic and copies ran while one was open for 0% of the time, Pallas kernels for 9%

profile of v1, /device:TPU:3, one launch (start us, length us, event | category | flops | bytes accessed | tf_op | source)
XLA Modules:
  0.0 147.5 jit_solution(9800470655231539189)
XLA Ops:
  0.6 5.5 %project.1 = (f32[256,512]{1,0:T(8,128)}, f32[256,512]{1,0:T(8,128)}) custom-call(bf16[2048,512]{1,0:T(8,128)(2,1)} %bitcast.11, bf16[2048,512]{1,0:T(8,128)(2,1)} %bitcast.16, bf16[2048,256]{1,0:T(8,128)(2,1)} %e_ref.3, bf16[2048,256]{1,0:T(8,128)(2,1)} %f_ref.3), custom_call_target="tpu_custom_call" | custom-call | flops 1073741824 | bytes 6291456 | tf_op jit(solution)/shard_map/project/pallas_call | solution.py:65
  6.9 1.7 %collective-permute-done.got = f32[256,512]{1,0:T(8,128)S(1)} collective-permute-done((f32[256,512]{1,0:T(8,128)}, f32[256,512]{1,0:T(8,128)S(1)}, u32[]{:S(2)}, u32[]{:S(2)}) %collective-permute-start) | collective-permute-done | bytes 524320 | tf_op jit(solution)/shard_map/ppermute | solution.py:121
  8.6 0.8 copy-done.10
  9.4 2.0 %core_sum.2 = (f32[64,512]{1,0:T(8,128)}, f32[64,512]{1,0:T(8,128)}, f32[64,512]{1,0:T(8,128)}, f32[64,512]{1,0:T(8,128)}) custom-call(f32[256,512]{1,0:T(8,128)} %get-tuple-element.22.keep, f32[256,512]{1,0:T(8,128)} %copy-done.10), custom_call_target="tpu_custom_call" | custom-call | flops 1048576 | bytes 1048576 | tf_op jit(solution)/shard_map/core_sum/pallas_call | solution.py:105
  11.4 1.3 collective-permute-start.1
  12.7 2.6 %collective-permute-start.2 = (f32[64,512]{1,0:T(8,128)}, f32[64,512]{1,0:T(8,128)S(1)}, u32[]{:S(2)}, u32[]{:S(2)}) collective-permute-start(f32[64,512]{1,0:T(8,128)} %get-tuple-element.26), channel_id=1, source_target_pairs={{0,64},{32,96},{64,0},{96,32},{1,65},{33,97},{65,1},{97,33},{2,66}... | collective-permute-start | bytes 393224 | tf_op jit(solution)/shard_map/ppermute | solution.py:121
  15.3 1.1 collective-permute-start.3
  16.4 1.2 collective-permute-done.1.got_1
  17.6 3.9 %collective-permute-done.2.got_2 = f32[64,512]{1,0:T(8,128)S(1)} collective-permute-done((f32[64,512]{1,0:T(8,128)}, f32[64,512]{1,0:T(8,128)S(1)}, u32[]{:S(2)}, u32[]{:S(2)}) %collective-permute-start.2) | collective-permute-done | bytes 131104 | tf_op jit(solution)/shard_map/ppermute | solution.py:121
  22.3 1.8 %y_sum.2.own = f32[64,512]{1,0:T(8,128)} custom-call(f32[64,512]{1,0:T(8,128)} %get-tuple-element.24.own, f32[64,512]{1,0:T(8,128)} %copy-done.12, f32[64,512]{1,0:T(8,128)} %copy-done.13, f32[64,512]{1,0:T(8,128)} %copy-done.14), custom_call_target="tpu_custom_call" | custom-call | flops 1048576 | bytes 1048576 | tf_op jit(solution)/shard_map/y_sum/pallas_call | solution.py:105
  24.1 3.8 %collective-permute-start.6 = (f32[64,512]{1,0:T(8,128)}, f32[64,512]{1,0:T(8,128)S(1)}, u32[]{:S(2)}, u32[]{:S(2)}) collective-permute-start(f32[64,512]{1,0:T(8,128)} %y_sum.2.own), channel_id=1, source_target_pairs={{0,24},{8,0},{16,8},{24,16},{1,25},{9,1},{17,9},{25,17},{2,26},{10... | collective-permute-start | bytes 393224 | tf_op jit(solution)/shard_map/ppermute | solution.py:121
  28.5 5.0 %collective-permute-done.6.got_3 = f32[64,512]{1,0:T(8,128)S(1)} collective-permute-done((f32[64,512]{1,0:T(8,128)}, f32[64,512]{1,0:T(8,128)S(1)}, u32[]{:S(2)}, u32[]{:S(2)}) %collective-permute-start.6) | collective-permute-done | bytes 131104 | tf_op jit(solution)/shard_map/ppermute | solution.py:121
  33.5 3.5 %collective-permute-done.4.got_1 = f32[64,512]{1,0:T(8,128)S(1)} collective-permute-done((f32[64,512]{1,0:T(8,128)}, f32[64,512]{1,0:T(8,128)S(1)}, u32[]{:S(2)}, u32[]{:S(2)}) %collective-permute-start.4) | collective-permute-done | bytes 131104 | tf_op jit(solution)/shard_map/ppermute | solution.py:121
  37.7 1.7 %z_sum.2.refs_2_ = bf16[64,512]{1,0:T(8,128)(2,1)} custom-call(f32[64,512]{1,0:T(8,128)} %y_sum.2.own, f32[64,512]{1,0:T(8,128)} %copy-done.17, f32[64,512]{1,0:T(8,128)} %copy-done.16, f32[64,512]{1,0:T(8,128)} %copy-done.15), custom_call_target="tpu_custom_call" | custom-call | flops 1048576 | bytes 1048576 | tf_op jit(solution)/shard_map/z_sum/pallas_call | solution.py:105
  39.4 2.1 %collective-permute-start.9 = (bf16[64,512]{1,0:T(8,128)(2,1)}, bf16[64,512]{1,0:T(8,128)(2,1)S(1)}, u32[]{:S(2)}, u32[]{:S(2)}) collective-permute-start(bf16[64,512]{1,0:T(8,128)(2,1)} %z_sum.2.refs_2_), channel_id=1, source_target_pairs={{0,96},{32,0},{64,32},{96,64},{1,97},{33,1},{65,33},{97,65},{2,98}... | collective-permute-start | bytes 196616 | tf_op jit(solution)/shard_map/ppermute | solution.py:121
  42.1 2.0 %collective-permute-start.10 = (bf16[64,512]{1,0:T(8,128)(2,1)}, bf16[64,512]{1,0:T(8,128)(2,1)S(1)}, u32[]{:S(2)}, u32[]{:S(2)}) collective-permute-start(bf16[64,512]{1,0:T(8,128)(2,1)} %z_sum.2.refs_2_), channel_id=1, source_target_pairs={{0,4},{4,0},{1,5},{5,1},{2,6},{6,2},{3,7},{7,3},{8,12},{12,8},{9,1... | collective-permute-start | bytes 196616 | tf_op jit(solution)/shard_map/ppermute | solution.py:121
  44.1 1.3 collective-permute-start.13
  45.4 1.1 collective-permute-done.8.refs_4_
  46.4 2.2 %collective-permute-start.12 = (bf16[64,512]{1,0:T(8,128)(2,1)S(1)}, bf16[64,512]{1,0:T(8,128)(2,1)S(1)}, u32[]{:S(2)}, u32[]{:S(2)}) collective-permute-start(bf16[64,512]{1,0:T(8,128)(2,1)S(1)} %collective-permute-done.8.refs_4_), channel_id=1, source_target_pairs={{0,4},{4,0},{1,5},{5,1},{2,6},{6,2},{3,7},{7,3},{8,12},{12,8},{9,1... | collective-permute-start | bytes 196616 | tf_op jit(solution)/shard_map/ppermute | solution.py:121
  49.5 0.7 collective-permute-done.11.refs_7_
  50.8 24.4 %attend.1 = (bf16[2048,512]{1,0:T(8,128)(2,1)}, f32[256,512]{1,0:T(8,128)}, bf16[256,512]{1,0:T(8,128)(2,1)}) custom-call(bf16[2048,512]{1,0:T(8,128)(2,1)} %bitcast.21, bf16[2048,512]{1,0:T(8,128)(2,1)} %bitcast.22, bf16[64,512]{1,0:T(8,128)(2,1)} %z_sum.2.refs_2_, bf16[64,512]{1,0:T(8,128)(2,1)} %copy-done.26, bf16[64,512]{1,0:T(8,128)(2,1)} %copy-done.25, ...), custom_call_target="tpu_custom_call" | custom-call | flops 4294967296 | bytes 8388608 | tf_op jit(solution)/shard_map/attend/pallas_call | solution.py:219
  75.7 1.4 collective-permute-done.14.got
  77.1 0.7 copy-done.11
  77.8 1.8 %core_sum.3 = (f32[64,512]{1,0:T(8,128)}, bf16[64,512]{1,0:T(8,128)(2,1)}, bf16[64,512]{1,0:T(8,128)(2,1)}, bf16[64,512]{1,0:T(8,128)(2,1)}) custom-call(f32[256,512]{1,0:T(8,128)} %get-tuple-element.29.keep, bf16[256,512]{1,0:T(8,128)(2,1)} %copy-done.11), custom_call_target="tpu_custom_call" | custom-call | flops 1048576 | bytes 1048576 | tf_op jit(solution)/shard_map/core_sum/pallas_call | solution.py:105
  79.6 1.5 collective-permute-start.16
  81.1 1.6 %collective-permute-start.17 = (bf16[64,512]{1,0:T(8,128)(2,1)}, bf16[64,512]{1,0:T(8,128)(2,1)S(1)}, u32[]{:S(2)}, u32[]{:S(2)}) collective-permute-start(bf16[64,512]{1,0:T(8,128)(2,1)} %get-tuple-element.34), channel_id=1, source_target_pairs={{0,96},{32,0},{64,32},{96,64},{1,97},{33,1},{65,33},{97,65},{2,98}... | collective-permute-start | bytes 196616 | tf_op jit(solution)/shard_map/ppermute | solution.py:121
  82.7 3.4 %collective-permute-done.15.got_1 = bf16[64,512]{1,0:T(8,128)(2,1)S(1)} collective-permute-done((bf16[64,512]{1,0:T(8,128)(2,1)}, bf16[64,512]{1,0:T(8,128)(2,1)S(1)}, u32[]{:S(2)}, u32[]{:S(2)}) %collective-permute-start.15) | collective-permute-done | bytes 65568 | tf_op jit(solution)/shard_map/ppermute | solution.py:121
  86.8 1.6 %y_sum.3.own = bf16[64,512]{1,0:T(8,128)(2,1)} custom-call(f32[64,512]{1,0:T(8,128)} %get-tuple-element.31.own, bf16[64,512]{1,0:T(8,128)(2,1)} %copy-done.21, bf16[64,512]{1,0:T(8,128)(2,1)} %copy-done.22, bf16[64,512]{1,0:T(8,128)(2,1)} %copy-done.23), custom_call_target="tpu_custom_call" | custom-call | flops 1048576 | bytes 1048576 | tf_op jit(solution)/shard_map/y_sum/pallas_call | solution.py:105
  89.1 0.8 collective-permute-start.18
  89.9 1.9 %collective-permute-done.20.got_3 = bf16[64,512]{1,0:T(8,128)(2,1)S(1)} collective-permute-done((bf16[64,512]{1,0:T(8,128)(2,1)}, bf16[64,512]{1,0:T(8,128)(2,1)S(1)}, u32[]{:S(2)}, u32[]{:S(2)}) %collective-permute-start.20) | collective-permute-done | bytes 65568 | tf_op jit(solution)/shard_map/ppermute | solution.py:121
  91.8 2.2 %collective-permute-done.19.got_2 = bf16[64,512]{1,0:T(8,128)(2,1)S(1)} collective-permute-done((bf16[64,512]{1,0:T(8,128)(2,1)}, bf16[64,512]{1,0:T(8,128)(2,1)S(1)}, u32[]{:S(2)}, u32[]{:S(2)}) %collective-permute-start.19) | collective-permute-done | bytes 65568 | tf_op jit(solution)/shard_map/ppermute | solution.py:121
  95.3 1.6 %z_sum.3.refs_0_ = bf16[64,512]{1,0:T(8,128)(2,1)} custom-call(bf16[64,512]{1,0:T(8,128)(2,1)} %y_sum.3.own, bf16[64,512]{1,0:T(8,128)(2,1)} %copy-done.20, bf16[64,512]{1,0:T(8,128)(2,1)} %copy-done.19, bf16[64,512]{1,0:T(8,128)(2,1)} %copy-done.18), custom_call_target="tpu_custom_call" | custom-call | flops 1048576 | bytes 1048576 | tf_op jit(solution)/shard_map/z_sum/pallas_call | solution.py:105
  96.9 2.7 %collective-permute-start.23 = (bf16[64,512]{1,0:T(8,128)(2,1)}, bf16[64,512]{1,0:T(8,128)(2,1)S(1)}, u32[]{:S(2)}, u32[]{:S(2)}) collective-permute-start(bf16[64,512]{1,0:T(8,128)(2,1)} %z_sum.3.refs_0_), channel_id=1, source_target_pairs={{0,96},{32,0},{64,32},{96,64},{1,97},{33,1},{65,33},{97,65},{2,98}... | collective-permute-start | bytes 196616 | tf_op jit(solution)/shard_map/ppermute | solution.py:121
  100.2 3.3 %collective-permute-start.24 = (bf16[64,512]{1,0:T(8,128)(2,1)}, bf16[64,512]{1,0:T(8,128)(2,1)S(1)}, u32[]{:S(2)}, u32[]{:S(2)}) collective-permute-start(bf16[64,512]{1,0:T(8,128)(2,1)} %z_sum.3.refs_0_), channel_id=1, source_target_pairs={{0,4},{4,0},{1,5},{5,1},{2,6},{6,2},{3,7},{7,3},{8,12},{12,8},{9,1... | collective-permute-start | bytes 196616 | tf_op jit(solution)/shard_map/ppermute | solution.py:121
  103.4 2.0 %collective-permute-start.27 = (bf16[64,512]{1,0:T(8,128)(2,1)S(1)}, bf16[64,512]{1,0:T(8,128)(2,1)S(1)}, u32[]{:S(2)}, u32[]{:S(2)}) collective-permute-start(bf16[64,512]{1,0:T(8,128)(2,1)S(1)} %collective-permute-done.23.refs_3_), channel_id=1, source_target_pairs={{0,4},{4,0},{1,5},{5,1},{2,6},{6,2},{3,7},{7,3},{8,12},{12,8},{9,1... | collective-permute-start | bytes 196616 | tf_op jit(solution)/shard_map/ppermute | solution.py:121
  105.4 3.2 %collective-permute-start.26 = (bf16[64,512]{1,0:T(8,128)(2,1)S(1)}, bf16[64,512]{1,0:T(8,128)(2,1)S(1)}, u32[]{:S(2)}, u32[]{:S(2)}) collective-permute-start(bf16[64,512]{1,0:T(8,128)(2,1)S(1)} %collective-permute-done.22.refs_2_), channel_id=1, source_target_pairs={{0,4},{4,0},{1,5},{5,1},{2,6},{6,2},{3,7},{7,3},{8,12},{12,8},{9,1... | collective-permute-start | bytes 196616 | tf_op jit(solution)/shard_map/ppermute | solution.py:121
  110.8 2.6 %mixer_part.5 = bf16[512,512]{1,0:T(8,128)(2,1)} custom-call(s32[1]{0:T(128)} %bitcast.8.at_ref, bf16[2048,512]{1,0:T(8,128)(2,1)} %bitcast.12, bf16[2048,512]{1,0:T(8,128)(2,1)} %bitcast.17, bf16[64,512]{1,0:T(8,128)(2,1)} %z_sum.3.refs_0_, bf16[64,512]{1,0:T(8,128)(2,1)} %copy-done.2, bf16[64,512]{1,0:T(8,128)(2,1)} %copy-done.1, bf16[64,512]{1,0:T(8,128)(2,1)} %copy-done, ...), custom_call_target="tpu_custom_call" | custom-call | flops 268435456 | bytes 2097152 | tf_op jit(solution)/shard_map/mixer_part/pallas_call | solution.py:256
  113.4 1.2 collective-permute-start.28
  114.6 2.6 %mixer_part.6 = bf16[512,512]{1,0:T(8,128)(2,1)} custom-call(s32[1]{0:T(128)} %bitcast.9.at_ref, bf16[2048,512]{1,0:T(8,128)(2,1)} %bitcast.13, bf16[2048,512]{1,0:T(8,128)(2,1)} %bitcast.18, bf16[64,512]{1,0:T(8,128)(2,1)} %z_sum.3.refs_0_, bf16[64,512]{1,0:T(8,128)(2,1)} %copy-done.2, bf16[64,512]{1,0:T(8,128)(2,1)} %copy-done.1, bf16[64,512]{1,0:T(8,128)(2,1)} %copy-done, ...), custom_call_target="tpu_custom_call" | custom-call | flops 268435456 | bytes 2097152 | tf_op jit(solution)/shard_map/mixer_part/pallas_call | solution.py:256
  117.2 0.8 collective-permute-start.29
  118.0 2.6 %mixer_part.7 = bf16[512,512]{1,0:T(8,128)(2,1)} custom-call(s32[1]{0:T(128)} %bitcast.10.at_ref, bf16[2048,512]{1,0:T(8,128)(2,1)} %bitcast.14, bf16[2048,512]{1,0:T(8,128)(2,1)} %bitcast.19, bf16[64,512]{1,0:T(8,128)(2,1)} %z_sum.3.refs_0_, bf16[64,512]{1,0:T(8,128)(2,1)} %copy-done.2, bf16[64,512]{1,0:T(8,128)(2,1)} %copy-done.1, ...), custom_call_target="tpu_custom_call" | custom-call | flops 268435456 | bytes 2097152 | tf_op jit(solution)/shard_map/mixer_part/pallas_call | solution.py:256
  120.6 1.9 %collective-permute-start.30 = (bf16[512,512]{1,0:T(8,128)(2,1)}, bf16[512,512]{1,0:T(8,128)(2,1)S(1)}, u32[]{:S(2)}, u32[]{:S(2)}) collective-permute-start(bf16[512,512]{1,0:T(8,128)(2,1)} %mixer_part.7), channel_id=1, source_target_pairs={{0,3},{1,0},{2,1},{3,2},{4,7},{5,4},{6,5},{7,6},{8,11},{9,8},{10,9... | collective-permute-start | bytes 1572872 | tf_op jit(solution)/shard_map/ppermute | solution.py:121
  122.5 2.8 %mixer_part.4.own = f32[512,512]{1,0:T(8,128)} custom-call(s32[1]{0:T(128)} %bitcast.7.at_ref, bf16[2048,512]{1,0:T(8,128)(2,1)} %bitcast.15, bf16[2048,512]{1,0:T(8,128)(2,1)} %bitcast.20, bf16[64,512]{1,0:T(8,128)(2,1)} %z_sum.3.refs_0_, bf16[64,512]{1,0:T(8,128)(2,1)} %copy-done.2, bf16[64,512]{1,0:T(8,128)(2,1)} %copy-done.1, bf16[64,512]{1,0:T(8,128)(2,1)} %copy-done, ...), custom_call_target="tpu_custom_call" | custom-call | flops 268435456 | bytes 2097152 | tf_op jit(solution)/shard_map/mixer_part/pallas_call | solution.py:256
  125.3 4.8 %input_grads.1 = (bf16[2048,512]{1,0:T(8,128)(2,1)}, bf16[2048,512]{1,0:T(8,128)(2,1)}) custom-call(bf16[2048,256]{1,0:T(8,128)(2,1)} %e_ref.3, bf16[2048,256]{1,0:T(8,128)(2,1)} %f_ref.3, bf16[64,512]{1,0:T(8,128)(2,1)} %z_sum.3.refs_0_, bf16[64,512]{1,0:T(8,128)(2,1)} %copy-done.2, bf16[64,512]{1,0:T(8,128)(2,1)} %copy-done.1, bf16[64,512]{1,0:T(8,128)(2,1)} %copy-done, ...), custom_call_target="tpu_custom_call" | custom-call | flops 1073741824 | bytes 6291456 | tf_op jit(solution)/shard_map/input_grads/pallas_call | solution.py:288
  130.2 1.6 %collective-permute-done.29.got_2 = bf16[512,512]{1,0:T(8,128)(2,1)S(1)} collective-permute-done((bf16[512,512]{1,0:T(8,128)(2,1)}, bf16[512,512]{1,0:T(8,128)(2,1)S(1)}, u32[]{:S(2)}, u32[]{:S(2)}) %collective-permute-start.29) | collective-permute-done | bytes 524320 | tf_op jit(solution)/shard_map/ppermute | solution.py:121
  131.8 12.2 %collective-permute-done.30.got_3 = bf16[512,512]{1,0:T(8,128)(2,1)S(1)} collective-permute-done((bf16[512,512]{1,0:T(8,128)(2,1)}, bf16[512,512]{1,0:T(8,128)(2,1)S(1)}, u32[]{:S(2)}, u32[]{:S(2)}) %collective-permute-start.30) | collective-permute-done | bytes 524320 | tf_op jit(solution)/shard_map/ppermute | solution.py:121
  144.0 0.8 copy-done.9
  144.8 2.7 %mixer_sum.1 = (f32[512,256]{1,0:T(8,128)}, f32[512,256]{1,0:T(8,128)}) custom-call(f32[512,512]{1,0:T(8,128)} %mixer_part.4.own, bf16[512,512]{1,0:T(8,128)(2,1)} %copy-done.7, bf16[512,512]{1,0:T(8,128)(2,1)} %copy-done.8, bf16[512,512]{1,0:T(8,128)(2,1)} %copy-done.9), custom_call_target="tpu_custom_call" | custom-call | flops 1048576 | bytes 1048576 | tf_op jit(solution)/shard_map/mixer_sum/pallas_call | solution.py:105
  (90 shorter events, 10.6 us)
Async XLA Ops:
  6.2 2.4 %collective-permute-start = (f32[256,512]{1,0:T(8,128)}, f32[256,512]{1,0:T(8,128)S(1)}, u32[]{:S(2)}, u32[]{:S(2)}) collective-permute-start(f32[256,512]{1,0:T(8,128)} %get-tuple-element.23), channel_id=1, source_target_pairs={{0,4},{4,0},{1,5},{5,1},{2,6},{6,2},{3,7},{7,3},{8,12},{12,8},{9,1... | collective-permute-start | bytes 1572872 | tf_op jit(solution)/shard_map/ppermute | solution.py:121
  11.4 6.2 %collective-permute-start.1 = (f32[64,512]{1,0:T(8,128)}, f32[64,512]{1,0:T(8,128)S(1)}, u32[]{:S(2)}, u32[]{:S(2)}) collective-permute-start(f32[64,512]{1,0:T(8,128)} %get-tuple-element.25), channel_id=1, source_target_pairs={{0,32},{32,64},{64,96},{96,0},{1,33},{33,65},{65,97},{97,1},{2,34}... | collective-permute-start | bytes 393224 | tf_op jit(solution)/shard_map/ppermute | solution.py:121
  12.7 8.9 %collective-permute-start.2 = (f32[64,512]{1,0:T(8,128)}, f32[64,512]{1,0:T(8,128)S(1)}, u32[]{:S(2)}, u32[]{:S(2)}) collective-permute-start(f32[64,512]{1,0:T(8,128)} %get-tuple-element.26), channel_id=1, source_target_pairs={{0,64},{32,96},{64,0},{96,32},{1,65},{33,97},{65,1},{97,33},{2,66}... | collective-permute-start | bytes 393224 | tf_op jit(solution)/shard_map/ppermute | solution.py:121
  15.3 6.2 %collective-permute-start.3 = (f32[64,512]{1,0:T(8,128)}, f32[64,512]{1,0:T(8,128)S(1)}, u32[]{:S(2)}, u32[]{:S(2)}) collective-permute-start(f32[64,512]{1,0:T(8,128)} %get-tuple-element.27), channel_id=1, source_target_pairs={{0,96},{32,0},{64,32},{96,64},{1,97},{33,1},{65,33},{97,65},{2,98}... | collective-permute-start | bytes 393224 | tf_op jit(solution)/shard_map/ppermute | solution.py:121
  17.6 3.9 %copy-start.12 = (f32[64,512]{1,0:T(8,128)}, f32[64,512]{1,0:T(8,128)S(1)}, u32[]{:S(2)}) copy-start(f32[64,512]{1,0:T(8,128)S(1)} %collective-permute-done.1.got_1) | copy-start | bytes 393220
  24.1 9.4 %collective-permute-start.6 = (f32[64,512]{1,0:T(8,128)}, f32[64,512]{1,0:T(8,128)S(1)}, u32[]{:S(2)}, u32[]{:S(2)}) collective-permute-start(f32[64,512]{1,0:T(8,128)} %y_sum.2.own), channel_id=1, source_target_pairs={{0,24},{8,0},{16,8},{24,16},{1,25},{9,1},{17,9},{25,17},{2,26},{10... | collective-permute-start | bytes 393224 | tf_op jit(solution)/shard_map/ppermute | solution.py:121
  27.8 5.7 %collective-permute-start.5 = (f32[64,512]{1,0:T(8,128)}, f32[64,512]{1,0:T(8,128)S(1)}, u32[]{:S(2)}, u32[]{:S(2)}) collective-permute-start(f32[64,512]{1,0:T(8,128)} %y_sum.2.own), channel_id=1, source_target_pairs={{0,16},{8,24},{16,0},{24,8},{1,17},{9,25},{17,1},{25,9},{2,18},{10... | collective-permute-start | bytes 393224 | tf_op jit(solution)/shard_map/ppermute | solution.py:121
  27.8 9.2 %collective-permute-start.4 = (f32[64,512]{1,0:T(8,128)}, f32[64,512]{1,0:T(8,128)S(1)}, u32[]{:S(2)}, u32[]{:S(2)}) collective-permute-start(f32[64,512]{1,0:T(8,128)} %y_sum.2.own), channel_id=1, source_target_pairs={{0,8},{8,16},{16,24},{24,0},{1,9},{9,17},{17,25},{25,1},{2,10},{10... | collective-permute-start | bytes 393224 | tf_op jit(solution)/shard_map/ppermute | solution.py:121
  33.5 3.5 %copy-start.15 = (f32[64,512]{1,0:T(8,128)}, f32[64,512]{1,0:T(8,128)S(1)}, u32[]{:S(2)}) copy-start(f32[64,512]{1,0:T(8,128)S(1)} %collective-permute-done.6.got_3) | copy-start | bytes 393220
  33.5 3.5 %copy-start.16 = (f32[64,512]{1,0:T(8,128)}, f32[64,512]{1,0:T(8,128)S(1)}, u32[]{:S(2)}) copy-start(f32[64,512]{1,0:T(8,128)S(1)} %collective-permute-done.5.got_2) | copy-start | bytes 393220
  39.4 4.7 %collective-permute-start.9 = (bf16[64,512]{1,0:T(8,128)(2,1)}, bf16[64,512]{1,0:T(8,128)(2,1)S(1)}, u32[]{:S(2)}, u32[]{:S(2)}) collective-permute-start(bf16[64,512]{1,0:T(8,128)(2,1)} %z_sum.2.refs_2_), channel_id=1, source_target_pairs={{0,96},{32,0},{64,32},{96,64},{1,97},{33,1},{65,33},{97,65},{2,98}... | collective-permute-start | bytes 196616 | tf_op jit(solution)/shard_map/ppermute | solution.py:121
  41.5 4.9 %collective-permute-start.8 = (bf16[64,512]{1,0:T(8,128)(2,1)}, bf16[64,512]{1,0:T(8,128)(2,1)S(1)}, u32[]{:S(2)}, u32[]{:S(2)}) collective-permute-start(bf16[64,512]{1,0:T(8,128)(2,1)} %z_sum.2.refs_2_), channel_id=1, source_target_pairs={{0,64},{32,96},{64,0},{96,32},{1,65},{33,97},{65,1},{97,33},{2,66}... | collective-permute-start | bytes 196616 | tf_op jit(solution)/shard_map/ppermute | solution.py:121
  41.9 6.7 %collective-permute-start.7 = (bf16[64,512]{1,0:T(8,128)(2,1)}, bf16[64,512]{1,0:T(8,128)(2,1)S(1)}, u32[]{:S(2)}, u32[]{:S(2)}) collective-permute-start(bf16[64,512]{1,0:T(8,128)(2,1)} %z_sum.2.refs_2_), channel_id=1, source_target_pairs={{0,32},{32,64},{64,96},{96,0},{1,33},{33,65},{65,97},{97,1},{2,34}... | collective-permute-start | bytes 196616 | tf_op jit(solution)/shard_map/ppermute | solution.py:121
  42.1 7.2 %collective-permute-start.10 = (bf16[64,512]{1,0:T(8,128)(2,1)}, bf16[64,512]{1,0:T(8,128)(2,1)S(1)}, u32[]{:S(2)}, u32[]{:S(2)}) collective-permute-start(bf16[64,512]{1,0:T(8,128)(2,1)} %z_sum.2.refs_2_), channel_id=1, source_target_pairs={{0,4},{4,0},{1,5},{5,1},{2,6},{6,2},{3,7},{7,3},{8,12},{12,8},{9,1... | collective-permute-start | bytes 196616 | tf_op jit(solution)/shard_map/ppermute | solution.py:121
  44.1 6.1 %copy-start.24 = (bf16[64,512]{1,0:T(8,128)(2,1)}, bf16[64,512]{1,0:T(8,128)(2,1)S(1)}, u32[]{:S(2)}) copy-start(bf16[64,512]{1,0:T(8,128)(2,1)S(1)} %collective-permute-done.9.refs_5_) | copy-start | bytes 196612
  44.1 5.2 %collective-permute-start.13 = (bf16[64,512]{1,0:T(8,128)(2,1)S(1)}, bf16[64,512]{1,0:T(8,128)(2,1)S(1)}, u32[]{:S(2)}, u32[]{:S(2)}) collective-permute-start(bf16[64,512]{1,0:T(8,128)(2,1)S(1)} %collective-permute-done.9.refs_5_), channel_id=1, source_target_pairs={{0,4},{4,0},{1,5},{5,1},{2,6},{6,2},{3,7},{7,3},{8,12},{12,8},{9,1... | collective-permute-start | bytes 196616 | tf_op jit(solution)/shard_map/ppermute | solution.py:121
  46.4 3.8 %copy-start.25 = (bf16[64,512]{1,0:T(8,128)(2,1)}, bf16[64,512]{1,0:T(8,128)(2,1)S(1)}, u32[]{:S(2)}) copy-start(bf16[64,512]{1,0:T(8,128)(2,1)S(1)} %collective-permute-done.8.refs_4_) | copy-start | bytes 196612
  46.4 3.1 %collective-permute-start.12 = (bf16[64,512]{1,0:T(8,128)(2,1)S(1)}, bf16[64,512]{1,0:T(8,128)(2,1)S(1)}, u32[]{:S(2)}, u32[]{:S(2)}) collective-permute-start(bf16[64,512]{1,0:T(8,128)(2,1)S(1)} %collective-permute-done.8.refs_4_), channel_id=1, source_target_pairs={{0,4},{4,0},{1,5},{5,1},{2,6},{6,2},{3,7},{7,3},{8,12},{12,8},{9,1... | collective-permute-start | bytes 196616 | tf_op jit(solution)/shard_map/ppermute | solution.py:121
  48.6 1.6 %copy-start.26 = (bf16[64,512]{1,0:T(8,128)(2,1)}, bf16[64,512]{1,0:T(8,128)(2,1)S(1)}, u32[]{:S(2)}) copy-start(bf16[64,512]{1,0:T(8,128)(2,1)S(1)} %collective-permute-done.7.refs_3_) | copy-start | bytes 196612
  48.6 1.6 %collective-permute-start.11 = (bf16[64,512]{1,0:T(8,128)(2,1)S(1)}, bf16[64,512]{1,0:T(8,128)(2,1)S(1)}, u32[]{:S(2)}, u32[]{:S(2)}) collective-permute-start(bf16[64,512]{1,0:T(8,128)(2,1)S(1)} %collective-permute-done.7.refs_3_), channel_id=1, source_target_pairs={{0,4},{4,0},{1,5},{5,1},{2,6},{6,2},{3,7},{7,3},{8,12},{12,8},{9,1... | collective-permute-start | bytes 196616 | tf_op jit(solution)/shard_map/ppermute | solution.py:121
  49.3 0.9 copy-start.27
  49.3 0.9 copy-start.28
  75.2 1.8 %collective-permute-start.14 = (bf16[256,512]{1,0:T(8,128)(2,1)}, bf16[256,512]{1,0:T(8,128)(2,1)S(1)}, u32[]{:S(2)}, u32[]{:S(2)}) collective-permute-start(bf16[256,512]{1,0:T(8,128)(2,1)} %get-tuple-element.30), channel_id=1, source_target_pairs={{0,4},{4,0},{1,5},{5,1},{2,6},{6,2},{3,7},{7,3},{8,12},{12,8},{9,1... | collective-permute-start | bytes 786440 | tf_op jit(solution)/shard_map/ppermute | solution.py:121
  79.6 6.5 %collective-permute-start.15 = (bf16[64,512]{1,0:T(8,128)(2,1)}, bf16[64,512]{1,0:T(8,128)(2,1)S(1)}, u32[]{:S(2)}, u32[]{:S(2)}) collective-permute-start(bf16[64,512]{1,0:T(8,128)(2,1)} %get-tuple-element.32), channel_id=1, source_target_pairs={{0,32},{32,64},{64,96},{96,0},{1,33},{33,65},{65,97},{97,1},{2,34}... | collective-permute-start | bytes 196616 | tf_op jit(solution)/shard_map/ppermute | solution.py:121
  79.6 6.5 %collective-permute-start.16 = (bf16[64,512]{1,0:T(8,128)(2,1)}, bf16[64,512]{1,0:T(8,128)(2,1)S(1)}, u32[]{:S(2)}, u32[]{:S(2)}) collective-permute-start(bf16[64,512]{1,0:T(8,128)(2,1)} %get-tuple-element.33), channel_id=1, source_target_pairs={{0,64},{32,96},{64,0},{96,32},{1,65},{33,97},{65,1},{97,33},{2,66}... | collective-permute-start | bytes 196616 | tf_op jit(solution)/shard_map/ppermute | solution.py:121
  81.1 5.1 %collective-permute-start.17 = (bf16[64,512]{1,0:T(8,128)(2,1)}, bf16[64,512]{1,0:T(8,128)(2,1)S(1)}, u32[]{:S(2)}, u32[]{:S(2)}) collective-permute-start(bf16[64,512]{1,0:T(8,128)(2,1)} %get-tuple-element.34), channel_id=1, source_target_pairs={{0,96},{32,0},{64,32},{96,64},{1,97},{33,1},{65,33},{97,65},{2,98}... | collective-permute-start | bytes 196616 | tf_op jit(solution)/shard_map/ppermute | solution.py:121
  88.4 3.3 %collective-permute-start.20 = (bf16[64,512]{1,0:T(8,128)(2,1)}, bf16[64,512]{1,0:T(8,128)(2,1)S(1)}, u32[]{:S(2)}, u32[]{:S(2)}) collective-permute-start(bf16[64,512]{1,0:T(8,128)(2,1)} %y_sum.3.own), channel_id=1, source_target_pairs={{0,24},{8,0},{16,8},{24,16},{1,25},{9,1},{17,9},{25,17},{2,26},{10... | collective-permute-start | bytes 196616 | tf_op jit(solution)/shard_map/ppermute | solution.py:121
  89.1 4.9 %collective-permute-start.19 = (bf16[64,512]{1,0:T(8,128)(2,1)}, bf16[64,512]{1,0:T(8,128)(2,1)S(1)}, u32[]{:S(2)}, u32[]{:S(2)}) collective-permute-start(bf16[64,512]{1,0:T(8,128)(2,1)} %y_sum.3.own), channel_id=1, source_target_pairs={{0,16},{8,24},{16,0},{24,8},{1,17},{9,25},{17,1},{25,9},{2,18},{10... | collective-permute-start | bytes 196616 | tf_op jit(solution)/shard_map/ppermute | solution.py:121
  89.1 5.5 %collective-permute-start.18 = (bf16[64,512]{1,0:T(8,128)(2,1)}, bf16[64,512]{1,0:T(8,128)(2,1)S(1)}, u32[]{:S(2)}, u32[]{:S(2)}) collective-permute-start(bf16[64,512]{1,0:T(8,128)(2,1)} %y_sum.3.own), channel_id=1, source_target_pairs={{0,8},{8,16},{16,24},{24,0},{1,9},{9,17},{17,25},{25,1},{2,10},{10... | collective-permute-start | bytes 196616 | tf_op jit(solution)/shard_map/ppermute | solution.py:121
  91.8 2.9 %copy-start.18 = (bf16[64,512]{1,0:T(8,128)(2,1)}, bf16[64,512]{1,0:T(8,128)(2,1)S(1)}, u32[]{:S(2)}) copy-start(bf16[64,512]{1,0:T(8,128)(2,1)S(1)} %collective-permute-done.20.got_3) | copy-start | bytes 196612
  96.9 6.6 %collective-permute-start.23 = (bf16[64,512]{1,0:T(8,128)(2,1)}, bf16[64,512]{1,0:T(8,128)(2,1)S(1)}, u32[]{:S(2)}, u32[]{:S(2)}) collective-permute-start(bf16[64,512]{1,0:T(8,128)(2,1)} %z_sum.3.refs_0_), channel_id=1, source_target_pairs={{0,96},{32,0},{64,32},{96,64},{1,97},{33,1},{65,33},{97,65},{2,98}... | collective-permute-start | bytes 196616 | tf_op jit(solution)/shard_map/ppermute | solution.py:121
  99.6 5.8 %collective-permute-start.22 = (bf16[64,512]{1,0:T(8,128)(2,1)}, bf16[64,512]{1,0:T(8,128)(2,1)S(1)}, u32[]{:S(2)}, u32[]{:S(2)}) collective-permute-start(bf16[64,512]{1,0:T(8,128)(2,1)} %z_sum.3.refs_0_), channel_id=1, source_target_pairs={{0,64},{32,96},{64,0},{96,32},{1,65},{33,97},{65,1},{97,33},{2,66}... | collective-permute-start | bytes 196616 | tf_op jit(solution)/shard_map/ppermute | solution.py:121
  99.7 8.9 %collective-permute-start.21 = (bf16[64,512]{1,0:T(8,128)(2,1)}, bf16[64,512]{1,0:T(8,128)(2,1)S(1)}, u32[]{:S(2)}, u32[]{:S(2)}) collective-permute-start(bf16[64,512]{1,0:T(8,128)(2,1)} %z_sum.3.refs_0_), channel_id=1, source_target_pairs={{0,32},{32,64},{64,96},{96,0},{1,33},{33,65},{65,97},{97,1},{2,34}... | collective-permute-start | bytes 196616 | tf_op jit(solution)/shard_map/ppermute | solution.py:121
  100.2 9.1 %collective-permute-start.24 = (bf16[64,512]{1,0:T(8,128)(2,1)}, bf16[64,512]{1,0:T(8,128)(2,1)S(1)}, u32[]{:S(2)}, u32[]{:S(2)}) collective-permute-start(bf16[64,512]{1,0:T(8,128)(2,1)} %z_sum.3.refs_0_), channel_id=1, source_target_pairs={{0,4},{4,0},{1,5},{5,1},{2,6},{6,2},{3,7},{7,3},{8,12},{12,8},{9,1... | collective-permute-start | bytes 196616 | tf_op jit(solution)/shard_map/ppermute | solution.py:121
  103.4 6.7 %copy-start = (bf16[64,512]{1,0:T(8,128)(2,1)}, bf16[64,512]{1,0:T(8,128)(2,1)S(1)}, u32[]{:S(2)}) copy-start(bf16[64,512]{1,0:T(8,128)(2,1)S(1)} %collective-permute-done.23.refs_3_) | copy-start | bytes 196612
  103.4 5.8 %collective-permute-start.27 = (bf16[64,512]{1,0:T(8,128)(2,1)S(1)}, bf16[64,512]{1,0:T(8,128)(2,1)S(1)}, u32[]{:S(2)}, u32[]{:S(2)}) collective-permute-start(bf16[64,512]{1,0:T(8,128)(2,1)S(1)} %collective-permute-done.23.refs_3_), channel_id=1, source_target_pairs={{0,4},{4,0},{1,5},{5,1},{2,6},{6,2},{3,7},{7,3},{8,12},{12,8},{9,1... | collective-permute-start | bytes 196616 | tf_op jit(solution)/shard_map/ppermute | solution.py:121
  105.4 4.8 %copy-start.1 = (bf16[64,512]{1,0:T(8,128)(2,1)}, bf16[64,512]{1,0:T(8,128)(2,1)S(1)}, u32[]{:S(2)}) copy-start(bf16[64,512]{1,0:T(8,128)(2,1)S(1)} %collective-permute-done.22.refs_2_) | copy-start | bytes 196612
  105.4 4.1 %collective-permute-start.26 = (bf16[64,512]{1,0:T(8,128)(2,1)S(1)}, bf16[64,512]{1,0:T(8,128)(2,1)S(1)}, u32[]{:S(2)}, u32[]{:S(2)}) collective-permute-start(bf16[64,512]{1,0:T(8,128)(2,1)S(1)} %collective-permute-done.22.refs_2_), channel_id=1, source_target_pairs={{0,4},{4,0},{1,5},{5,1},{2,6},{6,2},{3,7},{7,3},{8,12},{12,8},{9,1... | collective-permute-start | bytes 196616 | tf_op jit(solution)/shard_map/ppermute | solution.py:121
  108.6 1.6 %copy-start.2 = (bf16[64,512]{1,0:T(8,128)(2,1)}, bf16[64,512]{1,0:T(8,128)(2,1)S(1)}, u32[]{:S(2)}) copy-start(bf16[64,512]{1,0:T(8,128)(2,1)S(1)} %collective-permute-done.21.refs_1_) | copy-start | bytes 196612
  108.6 1.5 %collective-permute-start.25 = (bf16[64,512]{1,0:T(8,128)(2,1)S(1)}, bf16[64,512]{1,0:T(8,128)(2,1)S(1)}, u32[]{:S(2)}, u32[]{:S(2)}) collective-permute-start(bf16[64,512]{1,0:T(8,128)(2,1)S(1)} %collective-permute-done.21.refs_1_), channel_id=1, source_target_pairs={{0,4},{4,0},{1,5},{5,1},{2,6},{6,2},{3,7},{7,3},{8,12},{12,8},{9,1... | collective-permute-start | bytes 196616 | tf_op jit(solution)/shard_map/ppermute | solution.py:121
  109.3 0.9 copy-start.3
  109.3 0.9 copy-start.4
  113.4 16.8 %collective-permute-start.28 = (bf16[512,512]{1,0:T(8,128)(2,1)}, bf16[512,512]{1,0:T(8,128)(2,1)S(1)}, u32[]{:S(2)}, u32[]{:S(2)}) collective-permute-start(bf16[512,512]{1,0:T(8,128)(2,1)} %mixer_part.5), channel_id=1, source_target_pairs={{0,1},{1,2},{2,3},{3,0},{4,5},{5,6},{6,7},{7,4},{8,9},{9,10},{10,1... | collective-permute-start | bytes 1572872 | tf_op jit(solution)/shard_map/ppermute | solution.py:121
  117.2 14.6 %collective-permute-start.29 = (bf16[512,512]{1,0:T(8,128)(2,1)}, bf16[512,512]{1,0:T(8,128)(2,1)S(1)}, u32[]{:S(2)}, u32[]{:S(2)}) collective-permute-start(bf16[512,512]{1,0:T(8,128)(2,1)} %mixer_part.6), channel_id=1, source_target_pairs={{0,2},{1,3},{2,0},{3,1},{4,6},{5,7},{6,4},{7,5},{8,10},{9,11},{10,... | collective-permute-start | bytes 1572872 | tf_op jit(solution)/shard_map/ppermute | solution.py:121
  120.6 23.3 %collective-permute-start.30 = (bf16[512,512]{1,0:T(8,128)(2,1)}, bf16[512,512]{1,0:T(8,128)(2,1)S(1)}, u32[]{:S(2)}, u32[]{:S(2)}) collective-permute-start(bf16[512,512]{1,0:T(8,128)(2,1)} %mixer_part.7), channel_id=1, source_target_pairs={{0,3},{1,0},{2,1},{3,2},{4,7},{5,4},{6,5},{7,6},{8,11},{9,8},{10,9... | collective-permute-start | bytes 1572872 | tf_op jit(solution)/shard_map/ppermute | solution.py:121
  130.1 13.8 %copy-start.7 = (bf16[512,512]{1,0:T(8,128)(2,1)}, bf16[512,512]{1,0:T(8,128)(2,1)S(1)}, u32[]{:S(2)}) copy-start(bf16[512,512]{1,0:T(8,128)(2,1)S(1)} %collective-permute-done.28.got_1) | copy-start | bytes 1572868
  131.8 12.2 %copy-start.8 = (bf16[512,512]{1,0:T(8,128)(2,1)}, bf16[512,512]{1,0:T(8,128)(2,1)S(1)}, u32[]{:S(2)}) copy-start(bf16[512,512]{1,0:T(8,128)(2,1)S(1)} %collective-permute-done.29.got_2) | copy-start | bytes 1572868
  144.0 0.8 copy-start.9
  (14 other events, 9.4 us)

commit v2 on v1

--- a/solution.py
+++ b/solution.py
@@ -1,5 +1,3 @@
-import functools
-
 import jax
 import jax.numpy as jnp
 from jax import lax
@@ -18,7 +16,6 @@
 NT = (((1,), (1,)), ((), ()))
 TN = (((0,), (0,)), ((), ()))
 VM = pl.BlockSpec(memory_space=pltpu.VMEM)
-PARAMS = dict(vmem_limit_bytes=56 * 1024 * 1024)
 
 
 def shape_of(rows, cols, kind):
@@ -69,101 +66,61 @@
         out_specs=[pl.BlockSpec((KP, width), lambda i: (0, 0))] * 2,
         out_shape=[shape_of(KP, width, F32)] * 2,
         scratch_shapes=[pltpu.VMEM((KP, width), F32)] * 2,
-        compiler_params=pltpu.CompilerParams(**PARAMS),
+        compiler_params=pltpu.CompilerParams(vmem_limit_bytes=60 << 20),
         cost_estimate=cost(4 * tokens * width * KP, 6 << 20),
         name="project",
     )(k, v, e, f)
 
 
-def core_sum_kernel(keep, got, own, send_1, send_2, send_3):
-    size = lax.axis_size("seq_0")
-    me = lax.axis_index("seq_0")
-    rows = KP // 2 // size
-    for step, out in enumerate((own, send_1, send_2, send_3)):
-        to = lax.rem(me + step, size)
-        for at in range(2):
-            cut = pl.ds(at * KP // 2 + to * rows, rows)
-            total = keep[cut, :] + got[cut, :].astype(F32)
-            out[at * rows : (at + 1) * rows, :] = total.astype(out.dtype)
-
-
-def y_sum_kernel(own, got_1, got_2, got_3, out):
-    total = (own[...] + got_2[...].astype(F32)) + (
-        got_1[...].astype(F32) + got_3[...].astype(F32)
-    )
-    out[...] = total.astype(out.dtype)
-
-
-def z_sum_kernel(own, got_1, got_2, got_3, out):
-    total = (own[...].astype(F32) + got_2[...].astype(F32)) + (
-        got_1[...].astype(F32) + got_3[...].astype(F32)
-    )
-    out[...] = total.astype(out.dtype)
-
-
-def small(kernel, outs, name, *args):
-    return pl.pallas_call(
-        kernel,
-        in_specs=[VM] * len(args),
-        out_specs=[VM] * len(outs),
-        out_shape=list(outs),
-        compiler_params=pltpu.CompilerParams(**PARAMS),
+def sum_copies_kernel(got, out):
+    total = jnp.sum(got[...].astype(F32), axis=0, keepdims=True)
+    out[...] = jnp.broadcast_to(total.astype(out.dtype), out.shape)
+
+
+def swap(value, axis):
+    size = lax.axis_size(axis)
+    return lax.ppermute(value, axis, [(i, (i + 1) % size) for i in range(size)])
+
+
+def total_over_seq(keep, send, wire):
+    chips = ("seq_0", "seq_1")
+    size = lax.axis_size(chips)
+    rows, width = keep.shape
+    part = keep + swap(send, "seq_2").astype(F32)
+    part = part.astype(wire).reshape(size, rows // size, width)
+    got = lax.all_to_all(part, chips, 0, 0, tiled=True)
+    copies = pl.pallas_call(
+        sum_copies_kernel,
+        in_specs=[VM],
+        out_specs=VM,
+        out_shape=jax.ShapeDtypeStruct(got.shape, BF),
+        compiler_params=pltpu.CompilerParams(vmem_limit_bytes=4 << 20),
         cost_estimate=cost(1 << 20, 1 << 20),
-        name=name,
-    )(*args)
-
-
-def ring(size, step):
-    return [(i, (i + step) % size) for i in range(size)]
-
-
-def shifted(value, axis, step):
-    return lax.ppermute(value, axis, ring(lax.axis_size(axis), step))
-
-
-def total_over_seq(keep, send, wire):
-    width = keep.shape[1]
-    rows = KP // lax.axis_size("seq_0")
-    got = shifted(send, "seq_2", 1)
-    own, *sends = small(
-        core_sum_kernel,
-        [shape_of(rows, width, F32)] + [shape_of(rows, width, wire)] * 3,
-        "core_sum",
-        keep,
-        got,
-    )
-    got = [shifted(s, "seq_0", i + 1) for i, s in enumerate(sends)]
-    (part,) = small(y_sum_kernel, [shape_of(rows, width, wire)], "y_sum", own, *got)
-    got = [shifted(part, "seq_1", i + 1) for i in range(3)]
-    (piece,) = small(z_sum_kernel, [shape_of(rows, width, BF)], "z_sum", part, *got)
-    pieces = [piece] + [shifted(piece, "seq_0", i + 1) for i in range(3)]
-    return pieces + [shifted(p, "seq_2", 1) for p in pieces]
-
-
-def assemble(pieces, first, second):
-    size = lax.axis_size("seq_0")
-    me = lax.axis_index("seq_0")
+        name="sum_copies",
+    )(got)
+    own = lax.all_to_all(copies, chips, 0, 0, tiled=True).reshape(rows, width)
+    return own, swap(own, "seq_2")
+
+
+def assemble(own, other, first, second):
+    half = KP // 2
     core = lax.axis_index("seq_2")
-    rows = KP // 2 // size
-    for at, piece in enumerate(pieces):
-        of = lax.rem(me + size - at % size, size)
-        half = core if at < size else 1 - core
-        out = pl.ds(pl.multiple_of(half * (KP // 2) + of * rows, rows), rows)
-        first[out, :] = piece[:rows, :]
-        second[out, :] = piece[rows:, :]
-
-
-def attend_kernel(*refs):
-    q_ref, g_ref, *pieces = refs[:10]
-    dq_ref, keep, send = refs[10:13]
-    pk, pv, pk_t, sum_k, sum_v = refs[13:]
+    for piece, at in ((own, core), (other, 1 - core)):
+        out = pl.ds(pl.multiple_of(at * half, half), half)
+        first[out, :] = piece[:half, :]
+        second[out, :] = piece[half:, :]
+
+
+def attend_kernel(
+    q_ref, g_ref, own, other, dq_ref, keep, send, pk, pv, pk_t, sum_k, sum_v
+):
     step = pl.program_id(0)
     width = q_ref.shape[1]
     scale = 1.0 / DH**0.5
 
     @pl.when(step == 0)
     def _():
-        assemble(pieces, pk, pv)
+        assemble(own, other, pk, pv)
         pk_t[...] = pk[...].T
         sum_k[...] = jnp.zeros_like(sum_k)
         sum_v[...] = jnp.zeros_like(sum_v)
@@ -219,7 +176,7 @@
     return pl.pallas_call(
         attend_kernel,
         grid=(tokens // rows,),
-        in_specs=[wide, wide] + [VM] * len(pieces),
+        in_specs=[wide, wide, VM, VM],
         out_specs=[wide, still, still],
         out_shape=[
             shape_of(tokens, width, BF),
@@ -233,21 +190,20 @@
             pltpu.VMEM((KP, width), F32),
             pltpu.VMEM((KP, width), F32),
         ],
-        compiler_params=pltpu.CompilerParams(**PARAMS),
+        compiler_params=pltpu.CompilerParams(vmem_limit_bytes=32 << 20),
         cost_estimate=cost(16 * tokens * width * KP, 8 << 20),
         name="attend",
     )(q, g, *pieces)
 
 
-def mixer_part_kernel(at_ref, k_ref, v_ref, *refs):
-    pieces, (out, dpk, dpv) = refs[:-3], refs[-3:]
-    assemble(pieces, dpk, dpv)
-    out[:, :KP] = lax.dot_general(
-        k_ref[...], dpk[...], NT, preferred_element_type=F32
-    ).astype(out.dtype)
-    out[:, KP:] = lax.dot_general(
-        v_ref[...], dpv[...], NT, preferred_element_type=F32
-    ).astype(out.dtype)
+def mixer_part_kernel(at_ref, k_ref, v_ref, own, other, out):
+    half = KP // 2
+    for at, (data, rows) in enumerate(((k_ref, slice(0, half)), (v_ref, slice(half, KP)))):
+        for side, piece in enumerate((own, other)):
+            cols = slice(at * KP + side * half, at * KP + (side + 1) * half)
+            out[:, cols] = lax.dot_general(
+                data[...], piece[rows, :], NT, preferred_element_type=F32
+            ).astype(out.dtype)
 
 
 def mixer_part(at, k, v, pieces, rows, kind):
@@ -258,23 +214,20 @@
         grid_spec=pltpu.PrefetchScalarGridSpec(
             num_scalar_prefetch=1,
             grid=(1,),
-            in_specs=[wide, wide] + [VM] * len(pieces),
+            in_specs=[wide, wide, VM, VM],
             out_specs=pl.BlockSpec((rows, 2 * KP), lambda i, at: (0, 0)),
-            scratch_shapes=[pltpu.VMEM((KP, width), BF)] * 2,
         ),
         out_shape=shape_of(rows, 2 * KP, kind),
-        compiler_params=pltpu.CompilerParams(**PARAMS),
+        compiler_params=pltpu.CompilerParams(vmem_limit_bytes=12 << 20),
         cost_estimate=cost(4 * rows * width * KP, 2 << 20),
         name="mixer_part",
     )(at, k, v, *pieces)
 
 
-def input_grads_kernel(e_ref, f_ref, *refs):
-    pieces, (dk, dv, dpk, dpv) = refs[:-4], refs[-4:]
-
+def input_grads_kernel(e_ref, f_ref, own, other, dk, dv, dpk, dpv):
     @pl.when(pl.program_id(0) == 0)
     def _():
-        assemble(pieces, dpk, dpv)
+        assemble(own, other, dpk, dpv)
 
     dk[...] = jnp.dot(e_ref[...], dpk[...], preferred_element_type=F32).astype(BF)
     dv[...] = jnp.dot(f_ref[...], dpv[...], preferred_element_type=F32).astype(BF)
@@ -288,22 +241,48 @@
     return pl.pallas_call(
         input_grads_kernel,
         grid=(tokens // rows,),
-        in_specs=[thin, thin] + [VM] * len(pieces),
+        in_specs=[thin, thin, VM, VM],
         out_specs=[wide, wide],
         out_shape=[shape_of(tokens, width, BF)] * 2,
         scratch_shapes=[pltpu.VMEM((KP, width), BF)] * 2,
-        compiler_params=pltpu.CompilerParams(**PARAMS),
+        compiler_params=pltpu.CompilerParams(vmem_limit_bytes=16 << 20),
         cost_estimate=cost(4 * tokens * width * KP, 6 << 20),
         name="input_grads",
     )(e, f, *pieces)
 
 
 def mixer_sum_kernel(own, got_1, got_2, got_3, de, df):
+    half = KP // 2
+    core = lax.axis_index("seq_2")
     total = (own[...] + got_2[...].astype(F32)) + (
         got_1[...].astype(F32) + got_3[...].astype(F32)
     )
-    de[...] = total[:, :KP]
-    df[...] = total[:, KP:]
+    for out, at in ((de, 0), (df, KP)):
+        out[:, pl.ds(pl.multiple_of(core * half, half), half)] = total[:, at : at + half]
+        out[:, pl.ds(pl.multiple_of((1 - core) * half, half), half)] = total[
+            :, at + half : at + KP
+        ]
+
+
+def mixer_sum(own, got):
+    rows = own.shape[0]
+    block = 128
+    wide = pl.BlockSpec((block, 2 * KP), lambda i: (i, 0))
+    thin = pl.BlockSpec((block, KP), lambda i: (i, 0))
+    return pl.pallas_call(
+        mixer_sum_kernel,
+        grid=(rows // block,),
+        in_specs=[wide] * 4,
+        out_specs=[thin] * 2,
+        out_shape=[shape_of(rows, KP, F32)] * 2,
+        compiler_params=pltpu.CompilerParams(vmem_limit_bytes=8 << 20),
+        cost_estimate=cost(1 << 20, 3 << 20),
+        name="mixer_sum",
+    )(own, got[1], got[2], got[3])
+
+
+def ring(size, step):
+    return [(i, (i + step) % size) for i in range(size)]
 
 
 def on_device(queries, key_states, value_states, out_grad, key_mixer, value_mixer):
@@ -320,18 +299,12 @@
     got = {}
     for step in (2, 1, 3):
         at = lax.rem(me + step, near).reshape(1)
-        got[step] = shifted(mixer_part(at, k, v, pieces, rows, BF), across, step)
+        got[step] = lax.ppermute(
+            mixer_part(at, k, v, pieces, rows, BF), across, ring(near, step)
+        )
     own = mixer_part(me.reshape(1), k, v, pieces, rows, F32)
     key_grad, value_grad = input_grads(key_mixer, value_mixer, pieces)
-    mixer_e, mixer_f = small(
-        mixer_sum_kernel,
-        [shape_of(rows, KP, F32)] * 2,
-        "mixer_sum",
-        own,
-        got[1],
-        got[2],
-        got[3],
-    )
+    mixer_e, mixer_f = mixer_sum(own, got)
     return (query_grad[None], key_grad[None], value_grad[None], mixer_e, mixer_f)
 
 

time: 148 us -> 126 us (0.85)
  blocking collectives: 0 us -> 50.4 us
  starting transfers between devices: 40.2 us -> 11.1 us
  Pallas kernels: 58.8 us -> 36 us
  waiting for transfers between devices: 41.6 us -> 23.8 us
  local copies, waits for them, and re-layouts: 6.14 us -> 2.44 us
    all_to_all x0 -> x4, blocking collectives: none -> 50.4 us  [the longest x2 28.7 us: total_over_seq(): got = lax.all_to_all(part, chips, 0, 0, tiled=True)]
    ppermute x31 -> x7, starting transfers between devices: 40.2 us -> 11.1 us  [the longest x4 6.94 us: swap(): return lax.ppermute(value, axis, [(i, (i + 1) % size) for i in range(size)])]
    ppermute x31 -> x7, waiting for transfers between devices: 41.6 us -> 23.8 us  [the longest x3 18.5 us: on_device(): lax.ppermute(mixer_part(at, k, v, pieces, rows, BF), across, ring(near, s...]
    pallas_call x7 -> x3, Pallas kernels: 13.3 us -> 1.69 us  [the longest x1 1.61 us: mixer_sum(): pl.pallas_call(mixer_sum_kernel, grid=(rows // block,), in_specs=[wide] *...]
    pallas_call x4, Pallas kernels: 10.6 us -> 2.8 us  [mixer_part(): pl.pallas_call(mixer_part_kernel, grid_spec=pltpu.PrefetchScalarGridSpec(...]
    unnamed x62 -> x12, local copies, waits for them, and re-layouts: 6.14 us -> 2.44 us
    pallas_call x1, Pallas kernels: 4.82 us -> 3.04 us  [input_grads(): pl.pallas_call(input_grads_kernel, grid=(tokens // rows,), in_specs=[thin...]
    pallas_call x1, Pallas kernels: 24.4 us -> 22.8 us  [attend(): pl.pallas_call(attend_kernel, grid=(tokens // rows,), in_specs=[wide, wid...]
  transfers between devices with their start and end apart: 31 -> 7, of which waited for: 17 -> 7; matrix products, arithmetic and copies ran while one was open for 0% -> 0% of each run, Pallas kernels for 9% -> 4%
where the time goes in v2:
time: 126 us
  blocking collectives  50.4 us (40%)
  Pallas kernels  36 us (29%)
  waiting for transfers between devices  23.8 us (19%)
  starting transfers between devices  11.1 us (9%)
  local copies, waits for them, and re-layouts  2.44 us (2%)
    all_to_all x2, blocking collectives, total_over_seq(): got = lax.all_to_all(part, chips, 0, 0, tiled=True)  28.7 us
    pallas_call x1, Pallas kernels, attend(): pl.pallas_call(attend_kernel, grid=(tokens // rows,), in_specs=[wide, wid...  22.8 us
    all_to_all x2, blocking collectives, total_over_seq(): own = lax.all_to_all(copies, chips, 0, 0, tiled=True).reshape(rows, width)  21.7 us
    ppermute x3, waiting for transfers between devices, on_device(): lax.ppermute(mixer_part(at, k, v, pieces, rows, BF), across, ring(near, s...  18.5 us
    ppermute x4, starting transfers between devices, swap(): return lax.ppermute(value, axis, [(i, (i + 1) % size) for i in range(size)])  6.94 us
    pallas_call x1, Pallas kernels, project(): pl.pallas_call(project_kernel, grid=(tokens // rows,), in_specs=[wide, wi...  5.7 us
    ppermute x4, waiting for transfers between devices, swap(): return lax.ppermute(value, axis, [(i, (i + 1) % size) for i in range(size)])  5.23 us
    ppermute x3, starting transfers between devices, on_device(): lax.ppermute(mixer_part(at, k, v, pieces, rows, BF), across, ring(near, s...  4.13 us
  transfers between devices with their start and end apart: 7, of which 7 were waited for; matrix products, arithmetic and copies ran while one was open for 0% of the time, Pallas kernels for 4%

profile of v2, /device:TPU:3, one launch (start us, length us, event | category | flops | bytes accessed | tf_op | source)
XLA Modules:
  0.0 125.6 jit_solution(8567392428214665854)
XLA Ops:
  0.6 0.0 copy-start.5
  0.6 5.7 %project.1 = (f32[256,512]{1,0:T(8,128)}, f32[256,512]{1,0:T(8,128)}) custom-call(bf16[2048,512]{1,0:T(8,128)(2,1)} %bitcast.15, bf16[2048,512]{1,0:T(8,128)(2,1)} %bitcast.20, bf16[2048,256]{1,0:T(8,128)(2,1)} %e_ref.3, bf16[2048,256]{1,0:T(8,128)(2,1)} %f_ref.3), custom_call_target="tpu_custom_call" | custom-call | flops 1073741824 | bytes 6291456 | tf_op jit(solution)/shard_map/project/pallas_call | solution.py:62
  6.3 0.0 copy-start.4
  6.3 0.7 collective-permute-start
  7.0 1.7 %collective-permute-done = f32[256,512]{1,0:T(8,128)S(1)} collective-permute-done((f32[256,512]{1,0:T(8,128)}, f32[256,512]{1,0:T(8,128)S(1)}, u32[]{:S(2)}, u32[]{:S(2)}) %collective-permute-start) | collective-permute-done | bytes 524320 | tf_op jit(solution)/shard_map/ppermute | solution.py:82
  8.8 1.1 add.18
  9.9 17.9 %all_to_all.20.got = f32[16,16,512]{2,1,0:T(8,128)S(1)} all-to-all(f32[16,16,512]{2,1,0:T(8,128)S(1)} %bitcast.35), channel_id=1, replica_groups=mesh['seq_0'=4,'seq_1'=4,'seq_2'=2,'head'=2,'rep'=2] {'seq_0','seq_1'}, dimensions={0} | all-to-all | bytes 1048576 | tf_op jit(solution)/shard_map/all_to_all | solution.py:91
  27.9 10.8 %all_to_all.21 = bf16[16,16,512]{2,1,0:T(8,128)(2,1)S(1)} all-to-all(bf16[16,16,512]{2,1,0:T(8,128)(2,1)S(1)} %sum_copies.2), channel_id=1, replica_groups=mesh['seq_0'=4,'seq_1'=4,'seq_2'=2,'head'=2,'rep'=2] {'seq_0','seq_1'}, dimensions={0} | all-to-all | bytes 524288 | tf_op jit(solution)/shard_map/all_to_all | solution.py:101
  38.7 2.9 %collective-permute-start.1 = (bf16[256,512]{1,0:T(8,128)(2,1)S(1)}, bf16[256,512]{1,0:T(8,128)(2,1)S(1)}, u32[]{:S(2)}, u32[]{:S(2)}) collective-permute-start(bf16[256,512]{1,0:T(8,128)(2,1)S(1)} %bitcast.31), channel_id=1, source_target_pairs={{0,4},{4,0},{1,5},{5,1},{2,6},{6,2},{3,7},{7,3},{8,12},{12,8},{9,1... | collective-permute-start | bytes 786440 | tf_op jit(solution)/shard_map/ppermute | solution.py:82
  41.7 1.2 collective-permute-done.1.other
  42.8 0.0 copy-done.5
  42.8 0.0 copy-done.4
  42.8 22.8 %attend.1 = (bf16[2048,512]{1,0:T(8,128)(2,1)}, f32[256,512]{1,0:T(8,128)S(1)}, bf16[256,512]{1,0:T(8,128)(2,1)S(1)}) custom-call(bf16[2048,512]{1,0:T(8,128)(2,1)S(1)} %bitcast.33, bf16[2048,512]{1,0:T(8,128)(2,1)S(1)} %bitcast.34, bf16[256,512]{1,0:T(8,128)(2,1)S(1)} %bitcast.32, bf16[256,512]{1,0:T(8,128)(2,1)S(1)} %collective-permute-done.1.other), custom_call_target="tpu_custom_call" | custom-call | flops 4294967296 | bytes 8388608 | tf_op jit(solution)/shard_map/attend/pallas_call | solution.py:176
  65.6 0.0 copy-start
  65.6 0.4 collective-permute-start.2
  66.0 1.2 collective-permute-done.2
  67.2 0.1 add_convert_fusion
  67.2 10.8 %all_to_all.22.got = bf16[16,16,512]{2,1,0:T(8,128)(2,1)S(1)} all-to-all(bf16[16,16,512]{2,1,0:T(8,128)(2,1)S(1)} %bitcast.36), channel_id=1, replica_groups=mesh['seq_0'=4,'seq_1'=4,'seq_2'=2,'head'=2,'rep'=2] {'seq_0','seq_1'}, dimensions={0} | all-to-all | bytes 524288 | tf_op jit(solution)/shard_map/all_to_all | solution.py:91
  78.0 10.9 %all_to_all.23 = bf16[16,16,512]{2,1,0:T(8,128)(2,1)S(1)} all-to-all(bf16[16,16,512]{2,1,0:T(8,128)(2,1)S(1)} %sum_copies.3), channel_id=1, replica_groups=mesh['seq_0'=4,'seq_1'=4,'seq_2'=2,'head'=2,'rep'=2] {'seq_0','seq_1'}, dimensions={0} | all-to-all | bytes 524288 | tf_op jit(solution)/shard_map/all_to_all | solution.py:101
  88.9 2.9 %collective-permute-start.3 = (bf16[256,512]{1,0:T(8,128)(2,1)S(1)}, bf16[256,512]{1,0:T(8,128)(2,1)S(1)}, u32[]{:S(2)}, u32[]{:S(2)}) collective-permute-start(bf16[256,512]{1,0:T(8,128)(2,1)S(1)} %bitcast.25), channel_id=1, source_target_pairs={{0,4},{4,0},{1,5},{5,1},{2,6},{6,2},{3,7},{7,3},{8,12},{12,8},{9,1... | collective-permute-start | bytes 786440 | tf_op jit(solution)/shard_map/ppermute | solution.py:82
  91.8 1.2 collective-permute-done.3.other
  93.0 0.0 copy-done
  93.0 0.0 copy-start.1
  93.0 1.6 %copy-done.1 = bf16[1,2048,512]{2,1,0:T(8,128)(2,1)S(1)} copy-done((bf16[1,2048,512]{2,1,0:T(8,128)(2,1)S(1)}, bf16[1,2048,512]{2,1,0:T(8,128)(2,1)}, u32[]{:S(2)}) %copy-start.1) | copy-done | bytes 2097176
  94.6 0.7 mixer_part.5
  95.3 1.3 %collective-permute-start.4 = (bf16[512,512]{1,0:T(8,128)(2,1)S(1)}, bf16[512,512]{1,0:T(8,128)(2,1)S(1)}, u32[]{:S(2)}, u32[]{:S(2)}) collective-permute-start(bf16[512,512]{1,0:T(8,128)(2,1)S(1)} %mixer_part.5), channel_id=1, source_target_pairs={{0,1},{1,2},{2,3},{3,0},{4,5},{5,6},{6,7},{7,4},{8,9},{9,10},{10,1... | collective-permute-start | bytes 1572872 | tf_op jit(solution)/shard_map/ppermute | solution.py:302
  96.6 0.7 mixer_part.6
  97.3 0.9 collective-permute-start.5
  98.2 0.7 mixer_part.7
  98.9 1.9 %collective-permute-start.6 = (bf16[512,512]{1,0:T(8,128)(2,1)S(1)}, bf16[512,512]{1,0:T(8,128)(2,1)S(1)}, u32[]{:S(2)}, u32[]{:S(2)}) collective-permute-start(bf16[512,512]{1,0:T(8,128)(2,1)S(1)} %mixer_part.7), channel_id=1, source_target_pairs={{0,3},{1,0},{2,1},{3,2},{4,7},{5,4},{6,5},{7,6},{8,11},{9,8},{10,9... | collective-permute-start | bytes 1572872 | tf_op jit(solution)/shard_map/ppermute | solution.py:302
  100.8 0.0 copy-start.2
  100.8 0.0 copy-start.3
  100.9 0.7 mixer_part.4.own
  101.6 0.5 copy-done.2
  102.1 0.3 copy-done.3
  102.4 3.0 %input_grads.1 = (bf16[2048,512]{1,0:T(8,128)(2,1)}, bf16[2048,512]{1,0:T(8,128)(2,1)}) custom-call(bf16[2048,256]{1,0:T(8,128)(2,1)S(1)} %copy-done.2, bf16[2048,256]{1,0:T(8,128)(2,1)S(1)} %copy-done.3, bf16[256,512]{1,0:T(8,128)(2,1)S(1)} %bitcast.30, bf16[256,512]{1,0:T(8,128)(2,1)S(1)} %collective-permute-done.3.other), custom_call_target="tpu_custom_call" | custom-call | flops 1073741824 | bytes 6291456 | tf_op jit(solution)/shard_map/input_grads/pallas_call | solution.py:241
  105.4 3.0 %collective-permute-done.4.got_1 = bf16[512,512]{1,0:T(8,128)(2,1)S(1)} collective-permute-done((bf16[512,512]{1,0:T(8,128)(2,1)S(1)}, bf16[512,512]{1,0:T(8,128)(2,1)S(1)}, u32[]{:S(2)}, u32[]{:S(2)}) %collective-permute-start.4) | collective-permute-done | bytes 524320 | tf_op jit(solution)/shard_map/ppermute | solution.py:302
  108.5 3.3 %collective-permute-done.5.got_2 = bf16[512,512]{1,0:T(8,128)(2,1)S(1)} collective-permute-done((bf16[512,512]{1,0:T(8,128)(2,1)S(1)}, bf16[512,512]{1,0:T(8,128)(2,1)S(1)}, u32[]{:S(2)}, u32[]{:S(2)}) %collective-permute-start.5) | collective-permute-done | bytes 524320 | tf_op jit(solution)/shard_map/ppermute | solution.py:302
  111.7 12.2 %collective-permute-done.6.got_3 = bf16[512,512]{1,0:T(8,128)(2,1)S(1)} collective-permute-done((bf16[512,512]{1,0:T(8,128)(2,1)S(1)}, bf16[512,512]{1,0:T(8,128)(2,1)S(1)}, u32[]{:S(2)}, u32[]{:S(2)}) %collective-permute-start.6) | collective-permute-done | bytes 524320 | tf_op jit(solution)/shard_map/ppermute | solution.py:302
  124.0 1.6 %mixer_sum.1 = (f32[512,256]{1,0:T(8,128)}, f32[512,256]{1,0:T(8,128)}) custom-call(f32[512,512]{1,0:T(8,128)S(1)} %mixer_part.4.own, bf16[512,512]{1,0:T(8,128)(2,1)S(1)} %collective-permute-done.4.got_1, bf16[512,512]{1,0:T(8,128)(2,1)S(1)} %collective-permute-done.5.got_2, bf16[512,512]{1,0:T(8,128)(2,1)S(1)} %collective-permute-done.6.got_3), custom_call_target="tpu_custom_call" | custom-call | flops 1048576 | bytes 3145728 | tf_op jit(solution)/shard_map/mixer_sum/pallas_call | solution.py:272
  (2 shorter events, 0.1 us)
Async XLA Ops:
  0.6 42.2 %copy-start.5 = (bf16[1,2048,512]{2,1,0:T(8,128)(2,1)S(1)}, bf16[1,2048,512]{2,1,0:T(8,128)(2,1)}, u32[]{:S(2)}) copy-start(bf16[1,2048,512]{2,1,0:T(8,128)(2,1)} %param.9) | copy-start | bytes 6291460
  6.3 36.5 %copy-start.4 = (bf16[1,2048,512]{2,1,0:T(8,128)(2,1)S(1)}, bf16[1,2048,512]{2,1,0:T(8,128)(2,1)}, u32[]{:S(2)}) copy-start(bf16[1,2048,512]{2,1,0:T(8,128)(2,1)} %param.6) | copy-start | bytes 6291460
  6.3 2.4 %collective-permute-start = (f32[256,512]{1,0:T(8,128)}, f32[256,512]{1,0:T(8,128)S(1)}, u32[]{:S(2)}, u32[]{:S(2)}) collective-permute-start(f32[256,512]{1,0:T(8,128)} %get-tuple-element.15), channel_id=1, source_target_pairs={{0,4},{4,0},{1,5},{5,1},{2,6},{6,2},{3,7},{7,3},{8,12},{12,8},{9,1... | collective-permute-start | bytes 1572872 | tf_op jit(solution)/shard_map/ppermute | solution.py:82
  38.7 4.1 %collective-permute-start.1 = (bf16[256,512]{1,0:T(8,128)(2,1)S(1)}, bf16[256,512]{1,0:T(8,128)(2,1)S(1)}, u32[]{:S(2)}, u32[]{:S(2)}) collective-permute-start(bf16[256,512]{1,0:T(8,128)(2,1)S(1)} %bitcast.31), channel_id=1, source_target_pairs={{0,4},{4,0},{1,5},{5,1},{2,6},{6,2},{3,7},{7,3},{8,12},{12,8},{9,1... | collective-permute-start | bytes 786440 | tf_op jit(solution)/shard_map/ppermute | solution.py:82
  65.6 27.4 %copy-start = (bf16[1,2048,512]{2,1,0:T(8,128)(2,1)S(1)}, bf16[1,2048,512]{2,1,0:T(8,128)(2,1)}, u32[]{:S(2)}) copy-start(bf16[1,2048,512]{2,1,0:T(8,128)(2,1)} %param.7) | copy-start | bytes 6291460
  65.6 1.5 %collective-permute-start.2 = (bf16[256,512]{1,0:T(8,128)(2,1)S(1)}, bf16[256,512]{1,0:T(8,128)(2,1)S(1)}, u32[]{:S(2)}, u32[]{:S(2)}) collective-permute-start(bf16[256,512]{1,0:T(8,128)(2,1)S(1)} %get-tuple-element.18), channel_id=1, source_target_pairs={{0,4},{4,0},{1,5},{5,1},{2,6},{6,2},{3,7},{7,3},{8,12},{12,8},{9,1... | collective-permute-start | bytes 786440 | tf_op jit(solution)/shard_map/ppermute | solution.py:82
  88.9 4.1 %collective-permute-start.3 = (bf16[256,512]{1,0:T(8,128)(2,1)S(1)}, bf16[256,512]{1,0:T(8,128)(2,1)S(1)}, u32[]{:S(2)}, u32[]{:S(2)}) collective-permute-start(bf16[256,512]{1,0:T(8,128)(2,1)S(1)} %bitcast.25), channel_id=1, source_target_pairs={{0,4},{4,0},{1,5},{5,1},{2,6},{6,2},{3,7},{7,3},{8,12},{12,8},{9,1... | collective-permute-start | bytes 786440 | tf_op jit(solution)/shard_map/ppermute | solution.py:82
  93.0 1.6 %copy-start.1 = (bf16[1,2048,512]{2,1,0:T(8,128)(2,1)S(1)}, bf16[1,2048,512]{2,1,0:T(8,128)(2,1)}, u32[]{:S(2)}) copy-start(bf16[1,2048,512]{2,1,0:T(8,128)(2,1)} %param.8) | copy-start | bytes 6291460
  95.3 13.2 %collective-permute-start.4 = (bf16[512,512]{1,0:T(8,128)(2,1)S(1)}, bf16[512,512]{1,0:T(8,128)(2,1)S(1)}, u32[]{:S(2)}, u32[]{:S(2)}) collective-permute-start(bf16[512,512]{1,0:T(8,128)(2,1)S(1)} %mixer_part.5), channel_id=1, source_target_pairs={{0,1},{1,2},{2,3},{3,0},{4,5},{5,6},{6,7},{7,4},{8,9},{9,10},{10,1... | collective-permute-start | bytes 1572872 | tf_op jit(solution)/shard_map/ppermute | solution.py:302
  97.3 14.5 %collective-permute-start.5 = (bf16[512,512]{1,0:T(8,128)(2,1)S(1)}, bf16[512,512]{1,0:T(8,128)(2,1)S(1)}, u32[]{:S(2)}, u32[]{:S(2)}) collective-permute-start(bf16[512,512]{1,0:T(8,128)(2,1)S(1)} %mixer_part.6), channel_id=1, source_target_pairs={{0,2},{1,3},{2,0},{3,1},{4,6},{5,7},{6,4},{7,5},{8,10},{9,11},{10,... | collective-permute-start | bytes 1572872 | tf_op jit(solution)/shard_map/ppermute | solution.py:302
  98.9 25.0 %collective-permute-start.6 = (bf16[512,512]{1,0:T(8,128)(2,1)S(1)}, bf16[512,512]{1,0:T(8,128)(2,1)S(1)}, u32[]{:S(2)}, u32[]{:S(2)}) collective-permute-start(bf16[512,512]{1,0:T(8,128)(2,1)S(1)} %mixer_part.7), channel_id=1, source_target_pairs={{0,3},{1,0},{2,1},{3,2},{4,7},{5,4},{6,5},{7,6},{8,11},{9,8},{10,9... | collective-permute-start | bytes 1572872 | tf_op jit(solution)/shard_map/ppermute | solution.py:302
  100.8 1.2 copy-start.2
  100.8 1.5 %copy-start.3 = (bf16[2048,256]{1,0:T(8,128)(2,1)S(1)}, bf16[2048,256]{1,0:T(8,128)(2,1)}, u32[]{:S(2)}) copy-start(bf16[2048,256]{1,0:T(8,128)(2,1)} %f_ref.3) | copy-start | bytes 3145732

commit v3 on v2

v3 whole, which is shorter than its diff:
```python
import functools

import jax
import jax.numpy as jnp
from jax import lax
from jax.experimental import pallas as pl
from jax.experimental.pallas import tpu as pltpu
from jax.sharding import Mesh
from jax.sharding import PartitionSpec as P

DH = 64
KP = 256
LOG2E = 1.4426950408889634
ACROSS = ("head", "rep")
SEQ = ("seq_0", "seq_1", "seq_2")
SEQ_HEAD_REP = ("seq_0", "seq_1", "seq_2", "head", "rep")
BF = jnp.bfloat16
F32 = jnp.float32
NT = (((1,), (1,)), ((), ()))
TN = (((0,), (0,)), ((), ()))
VM = pl.BlockSpec(memory_space=pltpu.VMEM)


def shape_of(rows, cols, kind):
    return jax.ShapeDtypeStruct((rows, cols), kind)


def cost(flops, moved):
    return pl.CostEstimate(flops=flops, bytes_accessed=moved, transcendentals=0)


def project_kernel(k_ref, v_ref, e_ref, f_ref, keep, send, k, v, e, f, both, sem):
    chunks = sem.shape[1]
    rows = k.shape[0] // chunks
    half = KP // 2
    core = lax.axis_index("seq_2")
    refs = ((e_ref, e), (k_ref, k), (f_ref, f), (v_ref, v))
    copies = [
        [
            pltpu.make_async_copy(
                source.at[pl.ds(c * rows, rows), :],
                target.at[pl.ds(c * rows, rows), :],
                sem.at[at, c],
            )
            for at, (source, target) in enumerate(refs)
        ]
        for c in range(chunks)
    ]
    for chunk in copies:
        for copy in chunk:
            copy.start()
    for c, chunk in enumerate(copies):
        cut = slice(c * rows, (c + 1) * rows)
        for at, (mixer, data) in enumerate(((e, k), (f, v))):
            chunk[2 * at].wait()
            chunk[2 * at + 1].wait()
            part = lax.dot_general(
                mixer[cut, :], data[cut, :], TN, preferred_element_type=F32
            )
            if c == 0:
                both[at] = part
            else:
                both[at] += part
    for at in range(2):
        out = slice(at * half, (at + 1) * half)
        keep[out, :] = both[at, pl.ds(pl.multiple_of(core * half, half), half), :]
        send[out, :] = both[at, pl.ds(pl.multiple_of((1 - core) * half, half), half), :]


def project(k, v, e, f):
    tokens, width = k.shape
    hbm = pl.BlockSpec(memory_space=pltpu.MemorySpace.HBM)
    return pl.pallas_call(
        project_kernel,
        in_specs=[hbm] * 4,
        out_specs=[VM] * 2,
        out_shape=[shape_of(KP, width, F32)] * 2,
        scratch_shapes=[
            pltpu.VMEM((tokens, width), BF),
            pltpu.VMEM((tokens, width), BF),
            pltpu.VMEM((tokens, KP), BF),
            pltpu.VMEM((tokens, KP), BF),
            pltpu.VMEM((2, KP, width), F32),
            pltpu.SemaphoreType.DMA((4, 4)),
        ],
        compiler_params=pltpu.CompilerParams(vmem_limit_bytes=58 << 20),
        cost_estimate=cost(4 * tokens * width * KP, 6 << 20),
        name="project",
    )(k, v, e, f)


def sum_copies_kernel(got, out):
    total = jnp.sum(got[...].astype(F32), axis=0, keepdims=True)
    out[...] = jnp.broadcast_to(total.astype(out.dtype), out.shape)


def swap(value, axis):
    size = lax.axis_size(axis)
    return lax.ppermute(value, axis, [(i, (i + 1) % size) for i in range(size)])


def total_over_seq(keep, send, wire):
    chips = ("seq_0", "seq_1")
    size = lax.axis_size(chips)
    rows, width = keep.shape
    part = keep + swap(send, "seq_2").astype(F32)
    part = part.astype(wire).reshape(size, rows // size, width)
    got = lax.all_to_all(part, chips, 0, 0, tiled=True)
    copies = pl.pallas_call(
        sum_copies_kernel,
        in_specs=[VM],
        out_specs=VM,
        out_shape=jax.ShapeDtypeStruct(got.shape, BF),
        compiler_params=pltpu.CompilerParams(vmem_limit_bytes=4 << 20),
        cost_estimate=cost(1 << 20, 1 << 20),
        name="sum_copies",
    )(got)
    own = lax.all_to_all(copies, chips, 0, 0, tiled=True).reshape(rows, width)
    return own, swap(own, "seq_2")


def attend_kernel(q_ref, g_ref, own, other, dq_ref, keep, send, sum_k, sum_v):
    step = pl.program_id(0)
    width = q_ref.shape[1]
    half = KP // 2
    scale = 1.0 / DH**0.5
    heads = 4
    lanes = heads * DH

    @pl.when(step == 0)
    def _():
        sum_k[...] = jnp.zeros_like(sum_k)
        sum_v[...] = jnp.zeros_like(sum_v)

    head_of = lax.broadcasted_iota(jnp.int32, (KP, lanes), 1) // DH

    def stacked(piece):
        none = jnp.zeros_like(piece)
        return jnp.concatenate(
            [jnp.where(head_of == h, piece, none) for h in range(heads)], axis=0
        )

    def diagonal(total):
        out = total[:KP]
        for h in range(1, heads):
            out = jnp.where(head_of == h, total[h * KP : (h + 1) * KP], out)
        return out

    def group(j, carry):
        cols = pl.ds(pl.multiple_of(j * lanes, lanes), lanes)
        q = q_ref[:, cols]
        g = g_ref[:, cols]
        pk = stacked(jnp.concatenate([own[:half, cols], other[:half, cols]], axis=0))
        pv = stacked(jnp.concatenate([own[half:, cols], other[half:, cols]], axis=0))
        s_all = lax.dot_general(pk, q, NT, preferred_element_type=F32)
        gp_all = lax.dot_general(pv, g, NT, preferred_element_type=F32)
        pbs, dss = [], []
        for h in range(heads):
            s = s_all[h * KP : (h + 1) * KP]
            gp = gp_all[h * KP : (h + 1) * KP]
            top = jnp.max(s, axis=0, keepdims=True)
            ex = jnp.exp2((s - top) * (scale * LOG2E))
            share = scale / jnp.sum(ex, axis=0, keepdims=True)
            p = ex * share
            pb = p.astype(BF)
            delta = jnp.sum(pb.astype(F32) * gp, axis=0, keepdims=True) * (1.0 / scale)
            pbs.append(pb)
            dss.append((p * (gp - delta)).astype(BF))
        pb = jnp.concatenate(pbs, axis=0)
        ds = jnp.concatenate(dss, axis=0)
        sum_v[:, cols] += diagonal(jnp.dot(pb, g, preferred_element_type=F32))
        sum_k[:, cols] += diagonal(jnp.dot(ds, q, preferred_element_type=F32))
        dq_ref[:, cols] = lax.dot_general(
            ds, pk, TN, preferred_element_type=F32
        ).astype(BF)
        return carry

    lax.fori_loop(0, width // lanes, group, 0)

    @pl.when(step == pl.num_programs(0) - 1)
    def _():
        keep[:half, :] = sum_k[:half, :]
        keep[half:, :] = sum_v[:half, :] * (1.0 / scale)
        send[:half, :] = sum_k[half:, :].astype(send.dtype)
        send[half:, :] = (sum_v[half:, :] * (1.0 / scale)).astype(send.dtype)


def attend(q, g, pieces):
    tokens, width = q.shape
    rows = 1024
    wide = pl.BlockSpec((rows, width), lambda i: (i, 0))
    still = pl.BlockSpec((KP, width), lambda i: (0, 0))
    return pl.pallas_call(
        attend_kernel,
        grid=(tokens // rows,),
        in_specs=[wide, wide, VM, VM],
        out_specs=[wide, still, still],
        out_shape=[
            shape_of(tokens, width, BF),
            shape_of(KP, width, F32),
            shape_of(KP, width, BF),
        ],
        scratch_shapes=[pltpu.VMEM((KP, width), F32)] * 2,
        compiler_params=pltpu.CompilerParams(vmem_limit_bytes=44 << 20),
        cost_estimate=cost(16 * tokens * width * KP, 8 << 20),
        name="attend",
    )(q, g, *pieces)


def mixer_part_kernel(steps, k_ref, v_ref, own, other, *refs):
    extra, (de, df) = refs[:-2], refs[-2:]
    half = KP // 2
    core = lax.axis_index("seq_2")
    size = lax.axis_size(ACROSS)
    rows = de.shape[0]
    for at, (data, out) in enumerate(((k_ref, de), (v_ref, df))):
        to = lax.rem(lax.axis_index(ACROSS) + steps[at], size)
        block = data[pl.ds(pl.multiple_of(to * rows, rows), rows), :]
        for piece, side in ((own, core), (other, 1 - core)):
            part = lax.dot_general(
                block,
                piece[at * half : (at + 1) * half, :],
                NT,
                preferred_element_type=F32,
            )
            cols = pl.ds(pl.multiple_of(side * half, half), half)
            if extra:
                part += extra[at][:, cols].astype(F32)
            out[:, cols] = part.astype(out.dtype)


def mixer_part(steps, k, v, pieces, kind, *extra):
    tokens, width = k.shape
    rows = tokens // lax.axis_size(ACROSS)
    return pl.pallas_call(
        functools.partial(mixer_part_kernel, steps),
        in_specs=[VM] * (4 + len(extra)),
        out_specs=[VM] * 2,
        out_shape=[shape_of(rows, KP, kind)] * 2,
        compiler_params=pltpu.CompilerParams(vmem_limit_bytes=12 << 20),
        cost_estimate=cost(4 * rows * width * KP, 2 << 20),
        name="mixer_part",
    )(k, v, *pieces, *extra)


def input_grads_kernel(e_ref, f_ref, own, other, dk, dv, dpk, dpv):
    @pl.when(pl.program_id(0) == 0)
    def _():
        half = KP // 2
        core = lax.axis_index("seq_2")
        for piece, at in ((own, core), (other, 1 - core)):
            out = pl.ds(pl.multiple_of(at * half, half), half)
            dpk[out, :] = piece[:half, :]
            dpv[out, :] = piece[half:, :]

    dk[...] = jnp.dot(e_ref[...], dpk[...], preferred_element_type=F32).astype(BF)
    dv[...] = jnp.dot(f_ref[...], dpv[...], preferred_element_type=F32).astype(BF)


def input_grads(e, f, pieces):
    tokens, width = e.shape[0], pieces[0].shape[1]
    rows = 512
    wide = pl.BlockSpec((rows, width), lambda i: (i, 0))
    thin = pl.BlockSpec((rows, KP), lambda i: (i, 0))
    return pl.pallas_call(
        input_grads_kernel,
        grid=(tokens // rows,),
        in_specs=[thin, thin, VM, VM],
        out_specs=[wide, wide],
        out_shape=[shape_of(tokens, width, BF)] * 2,
        scratch_shapes=[pltpu.VMEM((KP, width), BF)] * 2,
        compiler_params=pltpu.CompilerParams(vmem_limit_bytes=16 << 20),
        cost_estimate=cost(4 * tokens * width * KP, 6 << 20),
        name="input_grads",
    )(e, f, *pieces)


def along(value, step):
    size = lax.axis_size(ACROSS)
    pairs = [(i, (i + step) % size) for i in range(size)]
    return lax.ppermute(value, ACROSS, pairs)


def mixer_grads(k, v, pieces):
    far_e, far_f = mixer_part((2, 2), k, v, pieces, BF)
    far_e, far_f = along(far_e, 1), along(far_f, -1)
    down_e, up_f = mixer_part((3, 1), k, v, pieces, BF)
    down_e, up_f = along(down_e, -1), along(up_f, 1)
    own_e, own_f = mixer_part((0, 0), k, v, pieces, F32)
    up_e, down_f = mixer_part((1, 3), k, v, pieces, BF, far_e, far_f)
    up_e, down_f = along(up_e, 1), along(down_f, -1)
    return (
        own_e + (down_e.astype(F32) + up_e.astype(F32)),
        own_f + (down_f.astype(F32) + up_f.astype(F32)),
    )


def on_device(queries, key_states, value_states, out_grad, key_mixer, value_mixer):
    q, g = queries[0], out_grad[0]
    k, v = key_states[0], value_states[0]
    keep, send = project(k, v, key_mixer, value_mixer)
    pieces = total_over_seq(keep, send, F32)
    query_grad, keep, send = attend(q, g, pieces)
    pieces = total_over_seq(keep, send, BF)
    mixer_e, mixer_f = mixer_grads(k, v, pieces)
    key_grad, value_grad = input_grads(key_mixer, value_mixer, pieces)
    return (query_grad[None], key_grad[None], value_grad[None], mixer_e, mixer_f)


def solution(mesh):
    split = Mesh(
        mesh.devices.reshape(4, 4, 2, mesh.shape["head"], mesh.shape["rep"]),
        ("seq_0", "seq_1", "seq_2", "head", "rep"),
    )
    data = P("rep", SEQ, "head")
    return jax.shard_map(
        on_device,
        mesh=split,
        in_specs=(data, data, data, data, P(SEQ, None), P(SEQ, None)),
        out_specs=(data, data, data, P(SEQ_HEAD_REP, None), P(SEQ_HEAD_REP, None)),
        check_vma=False,
    )
```

time: 126 us -> 112 us (0.89)
  the two profiles are of different devices: /device:TPU:3 before, /device:TPU:6 now
where the time goes in v3:
time: 112 us
  blocking collectives  55.5 us (50%)
  Pallas kernels  27 us (24%)
  waiting for transfers between devices  19.5 us (17%)
  starting transfers between devices  6.08 us (5%)
  other arithmetic  2.93 us (3%)
    all_to_all x2, blocking collectives, total_over_seq(): got = lax.all_to_all(part, chips, 0, 0, tiled=True)  31.9 us
    all_to_all x2, blocking collectives, total_over_seq(): own = lax.all_to_all(copies, chips, 0, 0, tiled=True).reshape(rows, width)  23.6 us
    pallas_call x1, Pallas kernels, attend(): pl.pallas_call(attend_kernel, grid=(tokens // rows,), in_specs=[wide, wid...  16.6 us
    ppermute x6, waiting for transfers between devices, along(): return lax.ppermute(value, ACROSS, pairs)  12.9 us
    ppermute x4, waiting for transfers between devices, swap(): return lax.ppermute(value, axis, [(i, (i + 1) % size) for i in range(size)])  6.58 us
    ppermute x6, starting transfers between devices, along(): return lax.ppermute(value, ACROSS, pairs)  5.86 us
    pallas_call x1, Pallas kernels, project(): pl.pallas_call(project_kernel, in_specs=[hbm] * 4, out_specs=[VM] * 2, ou...  4.52 us
    pallas_call x1, Pallas kernels, input_grads(): pl.pallas_call(input_grads_kernel, grid=(tokens // rows,), in_specs=[thin...  3.07 us
  transfers between devices with their start and end apart: 10, of which 9 were waited for; matrix products, arithmetic and copies ran while one was open for 1% of the time, Pallas kernels for 5%

profile of v3, /device:TPU:6, one launch (start us, length us, event | category | flops | bytes accessed | tf_op | source)
XLA Modules:
  0.0 111.8 jit_solution(1062906591467562921)
XLA Ops:
  0.6 0.0 copy-start.5
  0.6 4.5 %project.1 = (f32[256,512]{1,0:T(8,128)}, f32[256,512]{1,0:T(8,128)}) custom-call(bf16[2048,512]{1,0:T(8,128)(2,1)} %bitcast.11, bf16[2048,512]{1,0:T(8,128)(2,1)} %bitcast.16, bf16[2048,256]{1,0:T(8,128)(2,1)} %e_ref.3, bf16[2048,256]{1,0:T(8,128)(2,1)} %f_ref.3), custom_call_target="tpu_custom_call" | custom-call | flops 1073741824 | bytes 6291456 | tf_op jit(solution)/shard_map/project/pallas_call | solution.py:73
  5.2 0.0 copy-start.4
  5.2 0.1 collective-permute-start
  5.3 2.1 %collective-permute-done = f32[256,512]{1,0:T(8,128)S(1)} collective-permute-done((f32[256,512]{1,0:T(8,128)}, f32[256,512]{1,0:T(8,128)S(1)}, u32[]{:S(2)}, u32[]{:S(2)}) %collective-permute-start) | collective-permute-done | bytes 524320 | tf_op jit(solution)/shard_map/ppermute | solution.py:99
  7.4 1.1 %add.18 = f32[256,512]{1,0:T(8,128)S(1)} add(f32[256,512]{1,0:T(8,128)} %get-tuple-element.20, f32[256,512]{1,0:T(8,128)S(1)} %collective-permute-done) | non-fusion elementwise | flops 131072 | bytes 1572864 | tf_op jit(solution)/shard_map/add | solution.py:106
  8.5 19.6 %all_to_all.20.got = f32[16,16,512]{2,1,0:T(8,128)S(1)} all-to-all(f32[16,16,512]{2,1,0:T(8,128)S(1)} %bitcast.31), channel_id=1, replica_groups=mesh['seq_0'=4,'seq_1'=4,'seq_2'=2,'head'=2,'rep'=2] {'seq_0','seq_1'}, dimensions={0} | all-to-all | bytes 1048576 | tf_op jit(solution)/shard_map/all_to_all | solution.py:108
  28.2 11.7 %all_to_all.21 = bf16[16,16,512]{2,1,0:T(8,128)(2,1)S(1)} all-to-all(bf16[16,16,512]{2,1,0:T(8,128)(2,1)S(1)} %sum_copies.2), channel_id=1, replica_groups=mesh['seq_0'=4,'seq_1'=4,'seq_2'=2,'head'=2,'rep'=2] {'seq_0','seq_1'}, dimensions={0} | all-to-all | bytes 524288 | tf_op jit(solution)/shard_map/all_to_all | solution.py:118
  39.9 0.0 collective-permute-start.1
  39.9 1.5 %collective-permute-done.1.other = bf16[256,512]{1,0:T(8,128)(2,1)S(1)} collective-permute-done((bf16[256,512]{1,0:T(8,128)(2,1)S(1)}, bf16[256,512]{1,0:T(8,128)(2,1)S(1)}, u32[]{:S(2)}, u32[]{:S(2)}) %collective-permute-start.1) | collective-permute-done | bytes 262176 | tf_op jit(solution)/shard_map/ppermute | solution.py:99
  41.4 0.0 copy-done.5
  41.5 0.0 copy-done.4
  41.5 0.0 copy-start.1
  41.5 16.6 %attend.1 = (bf16[2048,512]{1,0:T(8,128)(2,1)}, f32[256,512]{1,0:T(8,128)S(1)}, bf16[256,512]{1,0:T(8,128)(2,1)S(1)}) custom-call(bf16[2048,512]{1,0:T(8,128)(2,1)S(1)} %bitcast.29, bf16[2048,512]{1,0:T(8,128)(2,1)S(1)} %bitcast.30, bf16[256,512]{1,0:T(8,128)(2,1)S(1)} %bitcast.28, bf16[256,512]{1,0:T(8,128)(2,1)S(1)} %collective-permute-done.1.other), custom_call_target="tpu_custom_call" | custom-call | flops 4294967296 | bytes 8388608 | tf_op jit(solution)/shard_map/attend/pallas_call | solution.py:193
  58.0 0.0 copy-start
  58.0 0.1 collective-permute-start.2
  58.1 1.4 %collective-permute-done.2 = bf16[256,512]{1,0:T(8,128)(2,1)S(1)} collective-permute-done((bf16[256,512]{1,0:T(8,128)(2,1)S(1)}, bf16[256,512]{1,0:T(8,128)(2,1)S(1)}, u32[]{:S(2)}, u32[]{:S(2)}) %collective-permute-start.2) | collective-permute-done | bytes 262176 | tf_op jit(solution)/shard_map/ppermute | solution.py:99
  59.5 0.1 add_convert_fusion
  59.6 12.3 %all_to_all.22.got = bf16[16,16,512]{2,1,0:T(8,128)(2,1)S(1)} all-to-all(bf16[16,16,512]{2,1,0:T(8,128)(2,1)S(1)} %bitcast.32), channel_id=1, replica_groups=mesh['seq_0'=4,'seq_1'=4,'seq_2'=2,'head'=2,'rep'=2] {'seq_0','seq_1'}, dimensions={0} | all-to-all | bytes 524288 | tf_op jit(solution)/shard_map/all_to_all | solution.py:108
  72.0 11.9 %all_to_all.23 = bf16[16,16,512]{2,1,0:T(8,128)(2,1)S(1)} all-to-all(bf16[16,16,512]{2,1,0:T(8,128)(2,1)S(1)} %sum_copies.3), channel_id=1, replica_groups=mesh['seq_0'=4,'seq_1'=4,'seq_2'=2,'head'=2,'rep'=2] {'seq_0','seq_1'}, dimensions={0} | all-to-all | bytes 524288 | tf_op jit(solution)/shard_map/all_to_all | solution.py:118
  83.9 0.0 collective-permute-start.3
  83.9 1.5 %collective-permute-done.3.other = bf16[256,512]{1,0:T(8,128)(2,1)S(1)} collective-permute-done((bf16[256,512]{1,0:T(8,128)(2,1)S(1)}, bf16[256,512]{1,0:T(8,128)(2,1)S(1)}, u32[]{:S(2)}, u32[]{:S(2)}) %collective-permute-start.3) | collective-permute-done | bytes 262176 | tf_op jit(solution)/shard_map/ppermute | solution.py:99
  85.4 0.0 copy-done.1
  85.4 0.0 copy-done
  85.4 0.7 mixer_part.6
  86.1 0.5 collective-permute-start.5
  86.7 1.5 %collective-permute-start.6 = (bf16[512,256]{1,0:T(8,128)(2,1)S(1)}, bf16[512,256]{1,0:T(8,128)(2,1)S(1)}, u32[]{:S(2)}, u32[]{:S(2)}) collective-permute-start(bf16[512,256]{1,0:T(8,128)(2,1)S(1)} %get-tuple-element.30), channel_id=1, source_target_pairs={{0,3},{1,0},{2,1},{3,2},{4,7},{5,4},{6,5},{7,6},{8,11},{9,8},{10,9... | collective-permute-start | bytes 786440 | tf_op jit(solution)/shard_map/ppermute | solution.py:281
  88.2 0.7 mixer_part.5
  88.9 0.9 collective-permute-start.4
  89.8 4.7 %collective-permute-done.5.refs_0_ = bf16[512,256]{1,0:T(8,128)(2,1)S(1)} collective-permute-done((bf16[512,256]{1,0:T(8,128)(2,1)S(1)}, bf16[512,256]{1,0:T(8,128)(2,1)S(1)}, u32[]{:S(2)}, u32[]{:S(2)}) %collective-permute-start.5) | collective-permute-done | bytes 262176 | tf_op jit(solution)/shard_map/ppermute | solution.py:281
  94.5 2.5 %collective-permute-done.6.refs_1_ = bf16[512,256]{1,0:T(8,128)(2,1)S(1)} collective-permute-done((bf16[512,256]{1,0:T(8,128)(2,1)S(1)}, bf16[512,256]{1,0:T(8,128)(2,1)S(1)}, u32[]{:S(2)}, u32[]{:S(2)}) %collective-permute-start.6) | collective-permute-done | bytes 262176 | tf_op jit(solution)/shard_map/ppermute | solution.py:281
  97.0 0.7 mixer_part.7
  97.8 0.3 collective-permute-start.7
  98.1 0.0 copy-start.2
  98.1 0.0 copy-start.3
  98.1 1.5 %collective-permute-start.9 = (bf16[512,256]{1,0:T(8,128)(2,1)S(1)}, bf16[512,256]{1,0:T(8,128)(2,1)S(1)}, u32[]{:S(2)}, u32[]{:S(2)}) collective-permute-start(bf16[512,256]{1,0:T(8,128)(2,1)S(1)} %get-tuple-element.34), channel_id=1, source_target_pairs={{0,1},{1,2},{2,3},{3,0},{4,5},{5,6},{6,7},{7,4},{8,9},{9,10},{10,1... | collective-permute-start | bytes 786440 | tf_op jit(solution)/shard_map/ppermute | solution.py:281
  99.6 0.7 mixer_part.4
  100.3 0.0 copy-done.2
  100.3 0.0 copy-done.3
  100.3 3.1 %input_grads.1 = (bf16[2048,512]{1,0:T(8,128)(2,1)}, bf16[2048,512]{1,0:T(8,128)(2,1)}) custom-call(bf16[2048,256]{1,0:T(8,128)(2,1)S(1)} %copy-done.2, bf16[2048,256]{1,0:T(8,128)(2,1)S(1)} %copy-done.3, bf16[256,512]{1,0:T(8,128)(2,1)S(1)} %bitcast.26, bf16[256,512]{1,0:T(8,128)(2,1)S(1)} %collective-permute-done.3.other), custom_call_target="tpu_custom_call" | custom-call | flops 1073741824 | bytes 6291456 | tf_op jit(solution)/shard_map/input_grads/pallas_call | solution.py:265
  103.4 1.0 collective-permute-start.8
  104.4 0.0 collective-permute-done.4
  104.4 2.3 %collective-permute-done.7 = bf16[512,256]{1,0:T(8,128)(2,1)S(1)} collective-permute-done((bf16[512,256]{1,0:T(8,128)(2,1)S(1)}, bf16[512,256]{1,0:T(8,128)(2,1)S(1)}, u32[]{:S(2)}, u32[]{:S(2)}) %collective-permute-start.7) | collective-permute-done | bytes 262176 | tf_op jit(solution)/shard_map/ppermute | solution.py:281
  106.7 0.9 add_add_fusion.1
  107.6 1.9 %collective-permute-done.9 = bf16[512,256]{1,0:T(8,128)(2,1)S(1)} collective-permute-done((bf16[512,256]{1,0:T(8,128)(2,1)S(1)}, bf16[512,256]{1,0:T(8,128)(2,1)S(1)}, u32[]{:S(2)}, u32[]{:S(2)}) %collective-permute-start.9) | collective-permute-done | bytes 262176 | tf_op jit(solution)/shard_map/ppermute | solution.py:281
  109.5 1.4 %collective-permute-done.8 = bf16[512,256]{1,0:T(8,128)(2,1)S(1)} collective-permute-done((bf16[512,256]{1,0:T(8,128)(2,1)S(1)}, bf16[512,256]{1,0:T(8,128)(2,1)S(1)}, u32[]{:S(2)}, u32[]{:S(2)}) %collective-permute-start.8) | collective-permute-done | bytes 262176 | tf_op jit(solution)/shard_map/ppermute | solution.py:281
  111.0 0.9 add_add_fusion
  (2 shorter events, 0.1 us)
Async XLA Ops:
  0.6 40.8 %copy-start.5 = (bf16[1,2048,512]{2,1,0:T(8,128)(2,1)S(1)}, bf16[1,2048,512]{2,1,0:T(8,128)(2,1)}, u32[]{:S(2)}) copy-start(bf16[1,2048,512]{2,1,0:T(8,128)(2,1)} %param.9) | copy-start | bytes 6291460
  5.2 36.3 %copy-start.4 = (bf16[1,2048,512]{2,1,0:T(8,128)(2,1)S(1)}, bf16[1,2048,512]{2,1,0:T(8,128)(2,1)}, u32[]{:S(2)}) copy-start(bf16[1,2048,512]{2,1,0:T(8,128)(2,1)} %param.6) | copy-start | bytes 6291460
  5.2 2.2 %collective-permute-start = (f32[256,512]{1,0:T(8,128)}, f32[256,512]{1,0:T(8,128)S(1)}, u32[]{:S(2)}, u32[]{:S(2)}) collective-permute-start(f32[256,512]{1,0:T(8,128)} %get-tuple-element.21), channel_id=1, source_target_pairs={{0,4},{4,0},{1,5},{5,1},{2,6},{6,2},{3,7},{7,3},{8,12},{12,8},{9,1... | collective-permute-start | bytes 1572872 | tf_op jit(solution)/shard_map/ppermute | solution.py:99
  39.9 1.5 %collective-permute-start.1 = (bf16[256,512]{1,0:T(8,128)(2,1)S(1)}, bf16[256,512]{1,0:T(8,128)(2,1)S(1)}, u32[]{:S(2)}, u32[]{:S(2)}) collective-permute-start(bf16[256,512]{1,0:T(8,128)(2,1)S(1)} %bitcast.27), channel_id=1, source_target_pairs={{0,4},{4,0},{1,5},{5,1},{2,6},{6,2},{3,7},{7,3},{8,12},{12,8},{9,1... | collective-permute-start | bytes 786440 | tf_op jit(solution)/shard_map/ppermute | solution.py:99
  41.5 43.9 %copy-start.1 = (bf16[1,2048,512]{2,1,0:T(8,128)(2,1)S(1)}, bf16[1,2048,512]{2,1,0:T(8,128)(2,1)}, u32[]{:S(2)}) copy-start(bf16[1,2048,512]{2,1,0:T(8,128)(2,1)} %param.8) | copy-start | bytes 6291460
  58.0 27.4 %copy-start = (bf16[1,2048,512]{2,1,0:T(8,128)(2,1)S(1)}, bf16[1,2048,512]{2,1,0:T(8,128)(2,1)}, u32[]{:S(2)}) copy-start(bf16[1,2048,512]{2,1,0:T(8,128)(2,1)} %param.7) | copy-start | bytes 6291460
  58.0 1.5 %collective-permute-start.2 = (bf16[256,512]{1,0:T(8,128)(2,1)S(1)}, bf16[256,512]{1,0:T(8,128)(2,1)S(1)}, u32[]{:S(2)}, u32[]{:S(2)}) collective-permute-start(bf16[256,512]{1,0:T(8,128)(2,1)S(1)} %get-tuple-element.24), channel_id=1, source_target_pairs={{0,4},{4,0},{1,5},{5,1},{2,6},{6,2},{3,7},{7,3},{8,12},{12,8},{9,1... | collective-permute-start | bytes 786440 | tf_op jit(solution)/shard_map/ppermute | solution.py:99
  83.9 1.5 %collective-permute-start.3 = (bf16[256,512]{1,0:T(8,128)(2,1)S(1)}, bf16[256,512]{1,0:T(8,128)(2,1)S(1)}, u32[]{:S(2)}, u32[]{:S(2)}) collective-permute-start(bf16[256,512]{1,0:T(8,128)(2,1)S(1)} %bitcast.21), channel_id=1, source_target_pairs={{0,4},{4,0},{1,5},{5,1},{2,6},{6,2},{3,7},{7,3},{8,12},{12,8},{9,1... | collective-permute-start | bytes 786440 | tf_op jit(solution)/shard_map/ppermute | solution.py:99
  86.1 8.4 %collective-permute-start.5 = (bf16[512,256]{1,0:T(8,128)(2,1)S(1)}, bf16[512,256]{1,0:T(8,128)(2,1)S(1)}, u32[]{:S(2)}, u32[]{:S(2)}) collective-permute-start(bf16[512,256]{1,0:T(8,128)(2,1)S(1)} %get-tuple-element.29), channel_id=1, source_target_pairs={{0,1},{1,2},{2,3},{3,0},{4,5},{5,6},{6,7},{7,4},{8,9},{9,10},{10,1... | collective-permute-start | bytes 786440 | tf_op jit(solution)/shard_map/ppermute | solution.py:281
  86.7 10.4 %collective-permute-start.6 = (bf16[512,256]{1,0:T(8,128)(2,1)S(1)}, bf16[512,256]{1,0:T(8,128)(2,1)S(1)}, u32[]{:S(2)}, u32[]{:S(2)}) collective-permute-start(bf16[512,256]{1,0:T(8,128)(2,1)S(1)} %get-tuple-element.30), channel_id=1, source_target_pairs={{0,3},{1,0},{2,1},{3,2},{4,7},{5,4},{6,5},{7,6},{8,11},{9,8},{10,9... | collective-permute-start | bytes 786440 | tf_op jit(solution)/shard_map/ppermute | solution.py:281
  88.9 15.5 %collective-permute-start.4 = (bf16[512,256]{1,0:T(8,128)(2,1)S(1)}, bf16[512,256]{1,0:T(8,128)(2,1)S(1)}, u32[]{:S(2)}, u32[]{:S(2)}) collective-permute-start(bf16[512,256]{1,0:T(8,128)(2,1)S(1)} %get-tuple-element.28), channel_id=1, source_target_pairs={{0,3},{1,0},{2,1},{3,2},{4,7},{5,4},{6,5},{7,6},{8,11},{9,8},{10,9... | collective-permute-start | bytes 786440 | tf_op jit(solution)/shard_map/ppermute | solution.py:281
  97.8 9.0 %collective-permute-start.7 = (bf16[512,256]{1,0:T(8,128)(2,1)S(1)}, bf16[512,256]{1,0:T(8,128)(2,1)S(1)}, u32[]{:S(2)}, u32[]{:S(2)}) collective-permute-start(bf16[512,256]{1,0:T(8,128)(2,1)S(1)} %get-tuple-element.31), channel_id=1, source_target_pairs={{0,1},{1,2},{2,3},{3,0},{4,5},{5,6},{6,7},{7,4},{8,9},{9,10},{10,1... | collective-permute-start | bytes 786440 | tf_op jit(solution)/shard_map/ppermute | solution.py:281
  98.1 2.2 %copy-start.2 = (bf16[2048,256]{1,0:T(8,128)(2,1)S(1)}, bf16[2048,256]{1,0:T(8,128)(2,1)}, u32[]{:S(2)}) copy-start(bf16[2048,256]{1,0:T(8,128)(2,1)} %e_ref.3) | copy-start | bytes 3145732
  98.1 2.2 %copy-start.3 = (bf16[2048,256]{1,0:T(8,128)(2,1)S(1)}, bf16[2048,256]{1,0:T(8,128)(2,1)}, u32[]{:S(2)}) copy-start(bf16[2048,256]{1,0:T(8,128)(2,1)} %f_ref.3) | copy-start | bytes 3145732
  98.1 11.4 %collective-permute-start.9 = (bf16[512,256]{1,0:T(8,128)(2,1)S(1)}, bf16[512,256]{1,0:T(8,128)(2,1)S(1)}, u32[]{:S(2)}, u32[]{:S(2)}) collective-permute-start(bf16[512,256]{1,0:T(8,128)(2,1)S(1)} %get-tuple-element.34), channel_id=1, source_target_pairs={{0,1},{1,2},{2,3},{3,0},{4,5},{5,6},{6,7},{7,4},{8,9},{9,10},{10,1... | collective-permute-start | bytes 786440 | tf_op jit(solution)/shard_map/ppermute | solution.py:281
  103.4 7.6 %collective-permute-start.8 = (bf16[512,256]{1,0:T(8,128)(2,1)S(1)}, bf16[512,256]{1,0:T(8,128)(2,1)S(1)}, u32[]{:S(2)}, u32[]{:S(2)}) collective-permute-start(bf16[512,256]{1,0:T(8,128)(2,1)S(1)} %get-tuple-element.33), channel_id=1, source_target_pairs={{0,3},{1,0},{2,1},{3,2},{4,7},{5,4},{6,5},{7,6},{8,11},{9,8},{10,9... | collective-permute-start | bytes 786440 | tf_op jit(solution)/shard_map/ppermute | solution.py:281

commit v4 on v3

--- a/solution.py
+++ b/solution.py
@@ -10,6 +10,7 @@
 
 DH = 64
 KP = 256
+PLACES = 4
 LOG2E = 1.4426950408889634
 ACROSS = ("head", "rep")
 SEQ = ("seq_0", "seq_1", "seq_2")
@@ -27,6 +28,11 @@
 
 def cost(flops, moved):
     return pl.CostEstimate(flops=flops, bytes_accessed=moved, transcendentals=0)
+
+
+def first_place(core):
+    y, z = lax.axis_index("seq_0"), lax.axis_index("seq_1")
+    return y + core * (z - y)
 
 
 def project_kernel(k_ref, v_ref, e_ref, f_ref, keep, send, k, v, e, f, both, sem):
@@ -61,10 +67,16 @@
                 both[at] = part
             else:
                 both[at] += part
-    for at in range(2):
-        out = slice(at * half, (at + 1) * half)
-        keep[out, :] = both[at, pl.ds(pl.multiple_of(core * half, half), half), :]
-        send[out, :] = both[at, pl.ds(pl.multiple_of((1 - core) * half, half), half), :]
+    rows = half // PLACES
+    for out, side in ((keep, core), (send, 1 - core)):
+        me = first_place(side)
+        for place in range(PLACES):
+            cut = pl.multiple_of(
+                side * half + lax.rem(me + PLACES - place, PLACES) * rows, rows
+            )
+            for at in range(2):
+                to = (2 * place + at) * rows
+                out[to : to + rows, :] = both[at, pl.ds(cut, rows), :]
 
 
 def project(k, v, e, f):
@@ -89,34 +101,48 @@
     )(k, v, e, f)
 
 
-def sum_copies_kernel(got, out):
-    total = jnp.sum(got[...].astype(F32), axis=0, keepdims=True)
-    out[...] = jnp.broadcast_to(total.astype(out.dtype), out.shape)
-
-
-def swap(value, axis):
-    size = lax.axis_size(axis)
-    return lax.ppermute(value, axis, [(i, (i + 1) % size) for i in range(size)])
+def shifts(step, second):
+    pairs = []
+    for y in range(PLACES):
+        for z in range(PLACES):
+            for core in range(2):
+                to = (y, (z + step) % PLACES) if second != core else ((y + step) % PLACES, z)
+                pairs.append(
+                    ((y * PLACES + z) * 2 + core, (to[0] * PLACES + to[1]) * 2 + core)
+                )
+    return pairs
+
+
+def from_all(values, second):
+    return [
+        lax.ppermute(value, SEQ, shifts(step, second))
+        for step, value in zip((1, 2, 3), values)
+    ]
+
+
+def summed(own, got):
+    one, two, three = (g.astype(F32) for g in got)
+    return (own.astype(F32) + two) + (one + three)
+
+
+def swap(value):
+    return lax.ppermute(value, "seq_2", [(0, 1), (1, 0)])
 
 
 def total_over_seq(keep, send, wire):
-    chips = ("seq_0", "seq_1")
-    size = lax.axis_size(chips)
-    rows, width = keep.shape
-    part = keep + swap(send, "seq_2").astype(F32)
-    part = part.astype(wire).reshape(size, rows // size, width)
-    got = lax.all_to_all(part, chips, 0, 0, tiled=True)
-    copies = pl.pallas_call(
-        sum_copies_kernel,
-        in_specs=[VM],
-        out_specs=VM,
-        out_shape=jax.ShapeDtypeStruct(got.shape, BF),
-        compiler_params=pltpu.CompilerParams(vmem_limit_bytes=4 << 20),
-        cost_estimate=cost(1 << 20, 1 << 20),
-        name="sum_copies",
-    )(got)
-    own = lax.all_to_all(copies, chips, 0, 0, tiled=True).reshape(rows, width)
-    return own, swap(own, "seq_2")
+    rows = keep.shape[0] // PLACES
+    total = keep + swap(send).astype(F32)
+    blocks = [total[i * rows : (i + 1) * rows] for i in range(PLACES)]
+    got = from_all([blocks[-step].astype(wire) for step in (1, 2, 3)], False)
+    part = summed(blocks[0], got).astype(wire)
+    piece = summed(part, from_all([part] * 3, True)).astype(BF)
+    own = jnp.concatenate([piece] + from_all([piece] * 3, False), axis=0)
+    return own, swap(own)
+
+
+def halves_of(piece, at):
+    rows = KP // 2 // PLACES
+    return [piece[(2 * i + at) * rows : (2 * i + at + 1) * rows] for i in range(PLACES)]
 
 
 def attend_kernel(q_ref, g_ref, own, other, dq_ref, keep, send, sum_k, sum_v):
@@ -150,8 +176,11 @@
         cols = pl.ds(pl.multiple_of(j * lanes, lanes), lanes)
         q = q_ref[:, cols]
         g = g_ref[:, cols]
-        pk = stacked(jnp.concatenate([own[:half, cols], other[:half, cols]], axis=0))
-        pv = stacked(jnp.concatenate([own[half:, cols], other[half:, cols]], axis=0))
+        mine, theirs = own[:, cols], other[:, cols]
+        pk, pv = (
+            stacked(jnp.concatenate(halves_of(mine, at) + halves_of(theirs, at), axis=0))
+            for at in range(2)
+        )
         s_all = lax.dot_general(pk, q, NT, preferred_element_type=F32)
         gp_all = lax.dot_general(pv, g, NT, preferred_element_type=F32)
         pbs, dss = [], []
@@ -179,10 +208,15 @@
 
     @pl.when(step == pl.num_programs(0) - 1)
     def _():
-        keep[:half, :] = sum_k[:half, :]
-        keep[half:, :] = sum_v[:half, :] * (1.0 / scale)
-        send[:half, :] = sum_k[half:, :].astype(send.dtype)
-        send[half:, :] = (sum_v[half:, :] * (1.0 / scale)).astype(send.dtype)
+        rows = half // PLACES
+        for out, side in ((keep, 0), (send, half)):
+            for place in range(PLACES):
+                cut = slice(side + place * rows, side + (place + 1) * rows)
+                to = 2 * place * rows
+                out[to : to + rows, :] = sum_k[cut, :].astype(out.dtype)
+                out[to + rows : to + 2 * rows, :] = (
+                    sum_v[cut, :] * (1.0 / scale)
+                ).astype(out.dtype)
 
 
 def attend(q, g, pieces):
@@ -207,26 +241,48 @@
     )(q, g, *pieces)
 
 
-def mixer_part_kernel(steps, k_ref, v_ref, own, other, *refs):
+def unpack_kernel(own, other, dpk, dpv):
+    half = KP // 2
+    rows = half // PLACES
+    core = lax.axis_index("seq_2")
+    for piece, side in ((own, core), (other, 1 - core)):
+        me = first_place(side)
+        for place in range(PLACES):
+            cut = pl.multiple_of(
+                side * half + lax.rem(me + PLACES - place, PLACES) * rows, rows
+            )
+            for at, out in enumerate((dpk, dpv)):
+                to = (2 * place + at) * rows
+                out[pl.ds(cut, rows), :] = piece[to : to + rows, :]
+
+
+def unpack(own, other):
+    return pl.pallas_call(
+        unpack_kernel,
+        in_specs=[VM] * 2,
+        out_specs=[VM] * 2,
+        out_shape=[shape_of(*own.shape, BF)] * 2,
+        compiler_params=pltpu.CompilerParams(vmem_limit_bytes=4 << 20),
+        cost_estimate=cost(1 << 20, 1 << 20),
+        name="unpack",
+    )(own, other)
+
+
+def mixer_part_kernel(steps, k_ref, v_ref, dpk, dpv, *refs):
     extra, (de, df) = refs[:-2], refs[-2:]
-    half = KP // 2
-    core = lax.axis_index("seq_2")
     size = lax.axis_size(ACROSS)
     rows = de.shape[0]
-    for at, (data, out) in enumerate(((k_ref, de), (v_ref, df))):
+    for at, (data, grad, out) in enumerate(((k_ref, dpk, de), (v_ref, dpv, df))):
         to = lax.rem(lax.axis_index(ACROSS) + steps[at], size)
-        block = data[pl.ds(pl.multiple_of(to * rows, rows), rows), :]
-        for piece, side in ((own, core), (other, 1 - core)):
-            part = lax.dot_general(
-                block,
-                piece[at * half : (at + 1) * half, :],
-                NT,
-                preferred_element_type=F32,
-            )
-            cols = pl.ds(pl.multiple_of(side * half, half), half)
-            if extra:
-                part += extra[at][:, cols].astype(F32)
-            out[:, cols] = part.astype(out.dtype)
+        part = lax.dot_general(
+            data[pl.ds(pl.multiple_of(to * rows, rows), rows), :],
+            grad[...],
+            NT,
+            preferred_element_type=F32,
+        )
+        if extra:
+            part += extra[at][...].astype(F32)
+        out[...] = part.astype(out.dtype)
 
 
 def mixer_part(steps, k, v, pieces, kind, *extra):
@@ -243,16 +299,7 @@
     )(k, v, *pieces, *extra)
 
 
-def input_grads_kernel(e_ref, f_ref, own, other, dk, dv, dpk, dpv):
-    @pl.when(pl.program_id(0) == 0)
-    def _():
-        half = KP // 2
-        core = lax.axis_index("seq_2")
-        for piece, at in ((own, core), (other, 1 - core)):
-            out = pl.ds(pl.multiple_of(at * half, half), half)
-            dpk[out, :] = piece[:half, :]
-            dpv[out, :] = piece[half:, :]
-
+def input_grads_kernel(e_ref, f_ref, dpk, dpv, dk, dv):
     dk[...] = jnp.dot(e_ref[...], dpk[...], preferred_element_type=F32).astype(BF)
     dv[...] = jnp.dot(f_ref[...], dpv[...], preferred_element_type=F32).astype(BF)
 
@@ -268,7 +315,6 @@
         in_specs=[thin, thin, VM, VM],
         out_specs=[wide, wide],
         out_shape=[shape_of(tokens, width, BF)] * 2,
-        scratch_shapes=[pltpu.VMEM((KP, width), BF)] * 2,
         compiler_params=pltpu.CompilerParams(vmem_limit_bytes=16 << 20),
         cost_estimate=cost(4 * tokens * width * KP, 6 << 20),
         name="input_grads",
@@ -301,7 +347,7 @@
     keep, send = project(k, v, key_mixer, value_mixer)
     pieces = total_over_seq(keep, send, F32)
     query_grad, keep, send = attend(q, g, pieces)
-    pieces = total_over_seq(keep, send, BF)
+    pieces = unpack(*total_over_seq(keep, send, BF))
     mixer_e, mixer_f = mixer_grads(k, v, pieces)
     key_grad, value_grad = input_grads(key_mixer, value_mixer, pieces)
     return (query_grad[None], key_grad[None], value_grad[None], mixer_e, mixer_f)

time: 112 us -> 111 us (level)
  the two profiles are of different devices: /device:TPU:6 before, /device:TPU:0 now
where the time goes in v4:
time: 111 us
  waiting for transfers between devices  46.5 us (42%)
  starting transfers between devices  34.5 us (31%)
  Pallas kernels  26 us (23%)
  other arithmetic  3.12 us (3%)
    ppermute x18, waiting for transfers between devices, from_all(): lax.ppermute(value, SEQ, shifts(step, second))  30.4 us
    ppermute x18, starting transfers between devices, from_all(): lax.ppermute(value, SEQ, shifts(step, second))  24.4 us
    pallas_call x1, Pallas kernels, attend(): pl.pallas_call(attend_kernel, grid=(tokens // rows,), in_specs=[wide, wid...  16.6 us
    ppermute x6, starting transfers between devices, along(): return lax.ppermute(value, ACROSS, pairs)  9.72 us
    ppermute x6, waiting for transfers between devices, along(): return lax.ppermute(value, ACROSS, pairs)  9.46 us
    ppermute x4, waiting for transfers between devices, swap(): return lax.ppermute(value, 'seq_2', [(0, 1), (1, 0)])  6.56 us
    pallas_call x1, Pallas kernels, project(): pl.pallas_call(project_kernel, in_specs=[hbm] * 4, out_specs=[VM] * 2, ou...  4.47 us
    pallas_call x1, Pallas kernels, input_grads(): pl.pallas_call(input_grads_kernel, grid=(tokens // rows,), in_specs=[thin...  3.01 us
  transfers between devices with their start and end apart: 28, of which 23 were waited for; matrix products, arithmetic and copies ran while one was open for 1% of the time, Pallas kernels for 4%

profile of v4, /device:TPU:0, one launch (start us, length us, event | category | flops | bytes accessed | tf_op | source)
XLA Modules:
  0.0 110.9 jit_solution(6299397589949299842)
XLA Ops:
  0.6 4.5 %project.1 = (f32[256,512]{1,0:T(8,128)}, f32[256,512]{1,0:T(8,128)}) custom-call(bf16[2048,512]{1,0:T(8,128)(2,1)} %bitcast.7, bf16[2048,512]{1,0:T(8,128)(2,1)} %bitcast.12, bf16[2048,256]{1,0:T(8,128)(2,1)} %e_ref.3, bf16[2048,256]{1,0:T(8,128)(2,1)} %f_ref.3), custom_call_target="tpu_custom_call" | custom-call | flops 1073741824 | bytes 6291456 | tf_op jit(solution)/shard_map/project/pallas_call | solution.py:85
  5.2 2.1 %collective-permute-done = f32[256,512]{1,0:T(8,128)S(1)} collective-permute-done((f32[256,512]{1,0:T(8,128)}, f32[256,512]{1,0:T(8,128)S(1)}, u32[]{:S(2)}, u32[]{:S(2)}) %collective-permute-start) | collective-permute-done | bytes 524320 | tf_op jit(solution)/shard_map/ppermute | solution.py:129
  7.3 1.1 %add.54 = f32[256,512]{1,0:T(8,128)S(1)} add(f32[256,512]{1,0:T(8,128)} %get-tuple-element.22, f32[256,512]{1,0:T(8,128)S(1)} %collective-permute-done) | non-fusion elementwise | flops 131072 | bytes 1572864 | tf_op jit(solution)/shard_map/add | solution.py:134
  8.5 3.2 %collective-permute-start.3 = (f32[64,512]{1,0:T(8,128)S(1)}, f32[64,512]{1,0:T(8,128)S(1)}, u32[]{:S(2)}, u32[]{:S(2)}) collective-permute-start(f32[64,512]{1,0:T(8,128)S(1)} %get-tuple-element.41), channel_id=1, source_target_pairs={{0,96},{4,28},{8,104},{12,4},{16,112},{20,12},{24,120},{28,20},{32... | collective-permute-start | bytes 393224 | tf_op jit(solution)/shard_map/ppermute | solution.py:118
  11.7 2.2 %collective-permute-start.1 = (f32[64,512]{1,0:T(8,128)S(1)}, f32[64,512]{1,0:T(8,128)S(1)}, u32[]{:S(2)}, u32[]{:S(2)}) collective-permute-start(f32[64,512]{1,0:T(8,128)S(1)} %get-tuple-element.43), channel_id=1, source_target_pairs={{0,64},{4,20},{8,72},{12,28},{16,80},{20,4},{24,88},{28,12},{32,96... | collective-permute-start | bytes 393224 | tf_op jit(solution)/shard_map/ppermute | solution.py:118
  14.2 5.1 %collective-permute-done.2 = f32[64,512]{1,0:T(8,128)S(1)} collective-permute-done((f32[64,512]{1,0:T(8,128)S(1)}, f32[64,512]{1,0:T(8,128)S(1)}, u32[]{:S(2)}, u32[]{:S(2)}) %collective-permute-start.2) | collective-permute-done | bytes 131104 | tf_op jit(solution)/shard_map/ppermute | solution.py:118
  19.3 4.1 %collective-permute-start.6 = (f32[64,512]{1,0:T(8,128)S(1)}, f32[64,512]{1,0:T(8,128)S(1)}, u32[]{:S(2)}, u32[]{:S(2)}) collective-permute-start(f32[64,512]{1,0:T(8,128)S(1)} %fusion.2), channel_id=1, source_target_pairs={{0,24},{4,100},{8,0},{12,108},{16,8},{20,116},{24,16},{28,124},{32... | collective-permute-start | bytes 393224 | tf_op jit(solution)/shard_map/ppermute | solution.py:118
  23.4 1.9 %collective-permute-start.4 = (f32[64,512]{1,0:T(8,128)S(1)}, f32[64,512]{1,0:T(8,128)S(1)}, u32[]{:S(2)}, u32[]{:S(2)}) collective-permute-start(f32[64,512]{1,0:T(8,128)S(1)} %fusion.2), channel_id=1, source_target_pairs={{0,16},{4,68},{8,24},{12,76},{16,0},{20,84},{24,8},{28,92},{32,48}... | collective-permute-start | bytes 393224 | tf_op jit(solution)/shard_map/ppermute | solution.py:118
  25.3 0.7 collective-permute-done.6
  25.9 5.1 %collective-permute-done.5 = f32[64,512]{1,0:T(8,128)S(1)} collective-permute-done((f32[64,512]{1,0:T(8,128)S(1)}, f32[64,512]{1,0:T(8,128)S(1)}, u32[]{:S(2)}, u32[]{:S(2)}) %collective-permute-start.5) | collective-permute-done | bytes 131104 | tf_op jit(solution)/shard_map/ppermute | solution.py:118
  31.0 2.2 %collective-permute-start.9 = (bf16[64,512]{1,0:T(8,128)(2,1)S(1)}, bf16[64,512]{1,0:T(8,128)(2,1)S(1)}, u32[]{:S(2)}, u32[]{:S(2)}) collective-permute-start(bf16[64,512]{1,0:T(8,128)(2,1)S(1)} %add_convert_fusion.1), channel_id=1, source_target_pairs={{0,96},{4,28},{8,104},{12,4},{16,112},{20,12},{24,120},{28,20},{32... | collective-permute-start | bytes 196616 | tf_op jit(solution)/shard_map/ppermute | solution.py:118
  33.2 0.9 collective-permute-start.7
  34.2 1.6 %collective-permute-done.9 = bf16[64,512]{1,0:T(8,128)(2,1)S(1)} collective-permute-done((bf16[64,512]{1,0:T(8,128)(2,1)S(1)}, bf16[64,512]{1,0:T(8,128)(2,1)S(1)}, u32[]{:S(2)}, u32[]{:S(2)}) %collective-permute-start.9) | collective-permute-done | bytes 65568 | tf_op jit(solution)/shard_map/ppermute | solution.py:118
  35.8 3.3 %collective-permute-done.8 = bf16[64,512]{1,0:T(8,128)(2,1)S(1)} collective-permute-done((bf16[64,512]{1,0:T(8,128)(2,1)S(1)}, bf16[64,512]{1,0:T(8,128)(2,1)S(1)}, u32[]{:S(2)}, u32[]{:S(2)}) %collective-permute-start.8) | collective-permute-done | bytes 65568 | tf_op jit(solution)/shard_map/ppermute | solution.py:118
  39.5 1.5 %collective-permute-done.10.other = bf16[256,512]{1,0:T(8,128)(2,1)S(1)} collective-permute-done((bf16[256,512]{1,0:T(8,128)(2,1)S(1)}, bf16[256,512]{1,0:T(8,128)(2,1)S(1)}, u32[]{:S(2)}, u32[]{:S(2)}) %collective-permute-start.10) | collective-permute-done | bytes 262176 | tf_op jit(solution)/shard_map/ppermute | solution.py:129
  41.1 16.6 %attend.1 = (bf16[2048,512]{1,0:T(8,128)(2,1)}, f32[256,512]{1,0:T(8,128)S(1)}, bf16[256,512]{1,0:T(8,128)(2,1)S(1)}) custom-call(bf16[2048,512]{1,0:T(8,128)(2,1)S(1)} %bitcast.17, bf16[2048,512]{1,0:T(8,128)(2,1)S(1)} %bitcast.18, bf16[256,512]{1,0:T(8,128)(2,1)S(1)} %pad_maximum_fusion.own, bf16[256,512]{1,0:T(8,128)(2,1)S(1)} %collective-permute-done.10.other), custom_call_target="tpu_custom_call" | custom-call | flops 4294967296 | bytes 8388608 | tf_op jit(solution)/shard_map/attend/pallas_call | solution.py:227
  57.8 1.4 %collective-permute-done.11 = bf16[256,512]{1,0:T(8,128)(2,1)S(1)} collective-permute-done((bf16[256,512]{1,0:T(8,128)(2,1)S(1)}, bf16[256,512]{1,0:T(8,128)(2,1)S(1)}, u32[]{:S(2)}, u32[]{:S(2)}) %collective-permute-start.11) | collective-permute-done | bytes 262176 | tf_op jit(solution)/shard_map/ppermute | solution.py:129
  59.3 1.7 %collective-permute-start.12 = (bf16[64,512]{1,0:T(8,128)(2,1)S(1)}, bf16[64,512]{1,0:T(8,128)(2,1)S(1)}, u32[]{:S(2)}, u32[]{:S(2)}) collective-permute-start(bf16[64,512]{1,0:T(8,128)(2,1)S(1)} %get-tuple-element.44), channel_id=1, source_target_pairs={{0,64},{4,20},{8,72},{12,28},{16,80},{20,4},{24,88},{28,12},{32,96... | collective-permute-start | bytes 196616 | tf_op jit(solution)/shard_map/ppermute | solution.py:118
  61.0 0.6 collective-permute-start.14
  61.5 1.5 %collective-permute-start.13 = (bf16[64,512]{1,0:T(8,128)(2,1)S(1)}, bf16[64,512]{1,0:T(8,128)(2,1)S(1)}, u32[]{:S(2)}, u32[]{:S(2)}) collective-permute-start(bf16[64,512]{1,0:T(8,128)(2,1)S(1)} %get-tuple-element.46), channel_id=1, source_target_pairs={{0,32},{4,12},{8,40},{12,20},{16,48},{20,28},{24,56},{28,4},{32,64... | collective-permute-start | bytes 196616 | tf_op jit(solution)/shard_map/ppermute | solution.py:118
  63.0 2.1 %collective-permute-done.12 = bf16[64,512]{1,0:T(8,128)(2,1)S(1)} collective-permute-done((bf16[64,512]{1,0:T(8,128)(2,1)S(1)}, bf16[64,512]{1,0:T(8,128)(2,1)S(1)}, u32[]{:S(2)}, u32[]{:S(2)}) %collective-permute-start.12) | collective-permute-done | bytes 65568 | tf_op jit(solution)/shard_map/ppermute | solution.py:118
  65.2 1.8 %collective-permute-done.13 = bf16[64,512]{1,0:T(8,128)(2,1)S(1)} collective-permute-done((bf16[64,512]{1,0:T(8,128)(2,1)S(1)}, bf16[64,512]{1,0:T(8,128)(2,1)S(1)}, u32[]{:S(2)}, u32[]{:S(2)}) %collective-permute-start.13) | collective-permute-done | bytes 65568 | tf_op jit(solution)/shard_map/ppermute | solution.py:118
  67.0 2.2 %collective-permute-start.17 = (bf16[64,512]{1,0:T(8,128)(2,1)S(1)}, bf16[64,512]{1,0:T(8,128)(2,1)S(1)}, u32[]{:S(2)}, u32[]{:S(2)}) collective-permute-start(bf16[64,512]{1,0:T(8,128)(2,1)S(1)} %fusion.1), channel_id=1, source_target_pairs={{0,24},{4,100},{8,0},{12,108},{16,8},{20,116},{24,16},{28,124},{32... | collective-permute-start | bytes 196616 | tf_op jit(solution)/shard_map/ppermute | solution.py:118
  69.2 1.5 %collective-permute-start.15 = (bf16[64,512]{1,0:T(8,128)(2,1)S(1)}, bf16[64,512]{1,0:T(8,128)(2,1)S(1)}, u32[]{:S(2)}, u32[]{:S(2)}) collective-permute-start(bf16[64,512]{1,0:T(8,128)(2,1)S(1)} %fusion.1), channel_id=1, source_target_pairs={{0,16},{4,68},{8,24},{12,76},{16,0},{20,84},{24,8},{28,92},{32,48}... | collective-permute-start | bytes 196616 | tf_op jit(solution)/shard_map/ppermute | solution.py:118
  70.8 0.6 collective-permute-done.17
  71.4 4.0 %collective-permute-done.16 = bf16[64,512]{1,0:T(8,128)(2,1)S(1)} collective-permute-done((bf16[64,512]{1,0:T(8,128)(2,1)S(1)}, bf16[64,512]{1,0:T(8,128)(2,1)S(1)}, u32[]{:S(2)}, u32[]{:S(2)}) %collective-permute-start.16) | collective-permute-done | bytes 65568 | tf_op jit(solution)/shard_map/ppermute | solution.py:118
  75.5 0.8 collective-permute-start.20
  76.2 1.6 %collective-permute-start.19 = (bf16[64,512]{1,0:T(8,128)(2,1)S(1)}, bf16[64,512]{1,0:T(8,128)(2,1)S(1)}, u32[]{:S(2)}, u32[]{:S(2)}) collective-permute-start(bf16[64,512]{1,0:T(8,128)(2,1)S(1)} %add_convert_fusion), channel_id=1, source_target_pairs={{0,64},{4,20},{8,72},{12,28},{16,80},{20,4},{24,88},{28,12},{32,96... | collective-permute-start | bytes 196616 | tf_op jit(solution)/shard_map/ppermute | solution.py:118
  77.9 1.9 %collective-permute-done.20 = bf16[64,512]{1,0:T(8,128)(2,1)S(1)} collective-permute-done((bf16[64,512]{1,0:T(8,128)(2,1)S(1)}, bf16[64,512]{1,0:T(8,128)(2,1)S(1)}, u32[]{:S(2)}, u32[]{:S(2)}) %collective-permute-start.20) | collective-permute-done | bytes 65568 | tf_op jit(solution)/shard_map/ppermute | solution.py:118
  79.8 2.2 %collective-permute-done.19 = bf16[64,512]{1,0:T(8,128)(2,1)S(1)} collective-permute-done((bf16[64,512]{1,0:T(8,128)(2,1)S(1)}, bf16[64,512]{1,0:T(8,128)(2,1)S(1)}, u32[]{:S(2)}, u32[]{:S(2)}) %collective-permute-start.19) | collective-permute-done | bytes 65568 | tf_op jit(solution)/shard_map/ppermute | solution.py:118
  82.0 1.3 %collective-permute-done.18 = bf16[64,512]{1,0:T(8,128)(2,1)S(1)} collective-permute-done((bf16[64,512]{1,0:T(8,128)(2,1)S(1)}, bf16[64,512]{1,0:T(8,128)(2,1)S(1)}, u32[]{:S(2)}, u32[]{:S(2)}) %collective-permute-start.18) | collective-permute-done | bytes 65568 | tf_op jit(solution)/shard_map/ppermute | solution.py:118
  83.4 1.5 %collective-permute-done.21.other = bf16[256,512]{1,0:T(8,128)(2,1)S(1)} collective-permute-done((bf16[256,512]{1,0:T(8,128)(2,1)S(1)}, bf16[256,512]{1,0:T(8,128)(2,1)S(1)}, u32[]{:S(2)}, u32[]{:S(2)}) %collective-permute-start.21) | collective-permute-done | bytes 262176 | tf_op jit(solution)/shard_map/ppermute | solution.py:129
  85.1 0.5 mixer_part.6
  85.5 1.6 %collective-permute-start.23 = (bf16[512,256]{1,0:T(8,128)(2,1)S(1)}, bf16[512,256]{1,0:T(8,128)(2,1)S(1)}, u32[]{:S(2)}, u32[]{:S(2)}) collective-permute-start(bf16[512,256]{1,0:T(8,128)(2,1)S(1)} %get-tuple-element.33), channel_id=1, source_target_pairs={{0,1},{1,2},{2,3},{3,0},{4,5},{5,6},{6,7},{7,4},{8,9},{9,10},{10,1... | collective-permute-start | bytes 786440 | tf_op jit(solution)/shard_map/ppermute | solution.py:327
  87.1 1.7 %collective-permute-start.24 = (bf16[512,256]{1,0:T(8,128)(2,1)S(1)}, bf16[512,256]{1,0:T(8,128)(2,1)S(1)}, u32[]{:S(2)}, u32[]{:S(2)}) collective-permute-start(bf16[512,256]{1,0:T(8,128)(2,1)S(1)} %get-tuple-element.34), channel_id=1, source_target_pairs={{0,3},{1,0},{2,1},{3,2},{4,7},{5,4},{6,5},{7,6},{8,11},{9,8},{10,9... | collective-permute-start | bytes 786440 | tf_op jit(solution)/shard_map/ppermute | solution.py:327
  88.8 0.5 mixer_part.5
  89.3 1.6 %collective-permute-start.22 = (bf16[512,256]{1,0:T(8,128)(2,1)S(1)}, bf16[512,256]{1,0:T(8,128)(2,1)S(1)}, u32[]{:S(2)}, u32[]{:S(2)}) collective-permute-start(bf16[512,256]{1,0:T(8,128)(2,1)S(1)} %get-tuple-element.32), channel_id=1, source_target_pairs={{0,3},{1,0},{2,1},{3,2},{4,7},{5,4},{6,5},{7,6},{8,11},{9,8},{10,9... | collective-permute-start | bytes 786440 | tf_op jit(solution)/shard_map/ppermute | solution.py:327
  90.9 4.2 %collective-permute-done.23.refs_0_ = bf16[512,256]{1,0:T(8,128)(2,1)S(1)} collective-permute-done((bf16[512,256]{1,0:T(8,128)(2,1)S(1)}, bf16[512,256]{1,0:T(8,128)(2,1)S(1)}, u32[]{:S(2)}, u32[]{:S(2)}) %collective-permute-start.23) | collective-permute-done | bytes 262176 | tf_op jit(solution)/shard_map/ppermute | solution.py:327
  95.2 1.1 collective-permute-done.24.refs_1_
  96.3 0.5 mixer_part.7
  96.7 1.6 %collective-permute-start.25 = (bf16[512,256]{1,0:T(8,128)(2,1)S(1)}, bf16[512,256]{1,0:T(8,128)(2,1)S(1)}, u32[]{:S(2)}, u32[]{:S(2)}) collective-permute-start(bf16[512,256]{1,0:T(8,128)(2,1)S(1)} %get-tuple-element.35), channel_id=1, source_target_pairs={{0,1},{1,2},{2,3},{3,0},{4,5},{5,6},{6,7},{7,4},{8,9},{9,10},{10,1... | collective-permute-start | bytes 786440 | tf_op jit(solution)/shard_map/ppermute | solution.py:327
  98.3 1.2 %collective-permute-start.27 = (bf16[512,256]{1,0:T(8,128)(2,1)S(1)}, bf16[512,256]{1,0:T(8,128)(2,1)S(1)}, u32[]{:S(2)}, u32[]{:S(2)}) collective-permute-start(bf16[512,256]{1,0:T(8,128)(2,1)S(1)} %get-tuple-element.38), channel_id=1, source_target_pairs={{0,1},{1,2},{2,3},{3,0},{4,5},{5,6},{6,7},{7,4},{8,9},{9,10},{10,1... | collective-permute-start | bytes 786440 | tf_op jit(solution)/shard_map/ppermute | solution.py:327
  100.0 3.0 %input_grads.1 = (bf16[2048,512]{1,0:T(8,128)(2,1)}, bf16[2048,512]{1,0:T(8,128)(2,1)}) custom-call(bf16[2048,256]{1,0:T(8,128)(2,1)S(1)} %copy-done.2, bf16[2048,256]{1,0:T(8,128)(2,1)S(1)} %copy-done.3, bf16[256,512]{1,0:T(8,128)(2,1)S(1)} %get-tuple-element.27.dpk, bf16[256,512]{1,0:T(8,128)(2,1)S(1)} %get-tuple-element.28.dpv), custom_call_target="tpu_custom_call" | custom-call | flops 1073741824 | bytes 6291456 | tf_op jit(solution)/shard_map/input_grads/pallas_call | solution.py:312
  103.0 2.0 %collective-permute-start.26 = (bf16[512,256]{1,0:T(8,128)(2,1)S(1)}, bf16[512,256]{1,0:T(8,128)(2,1)S(1)}, u32[]{:S(2)}, u32[]{:S(2)}) collective-permute-start(bf16[512,256]{1,0:T(8,128)(2,1)S(1)} %get-tuple-element.37), channel_id=1, source_target_pairs={{0,3},{1,0},{2,1},{3,2},{4,7},{5,4},{6,5},{7,6},{8,11},{9,8},{10,9... | collective-permute-start | bytes 786440 | tf_op jit(solution)/shard_map/ppermute | solution.py:327
  105.1 2.1 %collective-permute-done.25 = bf16[512,256]{1,0:T(8,128)(2,1)S(1)} collective-permute-done((bf16[512,256]{1,0:T(8,128)(2,1)S(1)}, bf16[512,256]{1,0:T(8,128)(2,1)S(1)}, u32[]{:S(2)}, u32[]{:S(2)}) %collective-permute-start.25) | collective-permute-done | bytes 262176 | tf_op jit(solution)/shard_map/ppermute | solution.py:327
  107.2 0.9 add_add_fusion.1
  108.1 2.0 %collective-permute-done.27 = bf16[512,256]{1,0:T(8,128)(2,1)S(1)} collective-permute-done((bf16[512,256]{1,0:T(8,128)(2,1)S(1)}, bf16[512,256]{1,0:T(8,128)(2,1)S(1)}, u32[]{:S(2)}, u32[]{:S(2)}) %collective-permute-start.27) | collective-permute-done | bytes 262176 | tf_op jit(solution)/shard_map/ppermute | solution.py:327
  110.0 0.9 add_add_fusion
  (40 shorter events, 2.0 us)
Async XLA Ops:
  0.6 40.4 %copy-start.5 = (bf16[1,2048,512]{2,1,0:T(8,128)(2,1)S(1)}, bf16[1,2048,512]{2,1,0:T(8,128)(2,1)}, u32[]{:S(2)}) copy-start(bf16[1,2048,512]{2,1,0:T(8,128)(2,1)} %param.9) | copy-start | bytes 6291460
  5.1 35.9 %copy-start.4 = (bf16[1,2048,512]{2,1,0:T(8,128)(2,1)S(1)}, bf16[1,2048,512]{2,1,0:T(8,128)(2,1)}, u32[]{:S(2)}) copy-start(bf16[1,2048,512]{2,1,0:T(8,128)(2,1)} %param.6) | copy-start | bytes 6291460
  5.1 2.2 %collective-permute-start = (f32[256,512]{1,0:T(8,128)}, f32[256,512]{1,0:T(8,128)S(1)}, u32[]{:S(2)}, u32[]{:S(2)}) collective-permute-start(f32[256,512]{1,0:T(8,128)} %get-tuple-element.23), channel_id=1, source_target_pairs={{0,4},{4,0},{1,5},{5,1},{2,6},{6,2},{3,7},{7,3},{8,12},{12,8},{9,1... | collective-permute-start | bytes 1572872 | tf_op jit(solution)/shard_map/ppermute | solution.py:129
  8.5 5.7 %collective-permute-start.3 = (f32[64,512]{1,0:T(8,128)S(1)}, f32[64,512]{1,0:T(8,128)S(1)}, u32[]{:S(2)}, u32[]{:S(2)}) collective-permute-start(f32[64,512]{1,0:T(8,128)S(1)} %get-tuple-element.41), channel_id=1, source_target_pairs={{0,96},{4,28},{8,104},{12,4},{16,112},{20,12},{24,120},{28,20},{32... | collective-permute-start | bytes 393224 | tf_op jit(solution)/shard_map/ppermute | solution.py:118
  11.7 7.6 %collective-permute-start.2 = (f32[64,512]{1,0:T(8,128)S(1)}, f32[64,512]{1,0:T(8,128)S(1)}, u32[]{:S(2)}, u32[]{:S(2)}) collective-permute-start(f32[64,512]{1,0:T(8,128)S(1)} %get-tuple-element.42), channel_id=1, source_target_pairs={{0,32},{4,12},{8,40},{12,20},{16,48},{20,28},{24,56},{28,4},{32,64... | collective-permute-start | bytes 393224 | tf_op jit(solution)/shard_map/ppermute | solution.py:118
  11.7 7.6 %collective-permute-start.1 = (f32[64,512]{1,0:T(8,128)S(1)}, f32[64,512]{1,0:T(8,128)S(1)}, u32[]{:S(2)}, u32[]{:S(2)}) collective-permute-start(f32[64,512]{1,0:T(8,128)S(1)} %get-tuple-element.43), channel_id=1, source_target_pairs={{0,64},{4,20},{8,72},{12,28},{16,80},{20,4},{24,88},{28,12},{32,96... | collective-permute-start | bytes 393224 | tf_op jit(solution)/shard_map/ppermute | solution.py:118
  19.3 6.6 %collective-permute-start.6 = (f32[64,512]{1,0:T(8,128)S(1)}, f32[64,512]{1,0:T(8,128)S(1)}, u32[]{:S(2)}, u32[]{:S(2)}) collective-permute-start(f32[64,512]{1,0:T(8,128)S(1)} %fusion.2), channel_id=1, source_target_pairs={{0,24},{4,100},{8,0},{12,108},{16,8},{20,116},{24,16},{28,124},{32... | collective-permute-start | bytes 393224 | tf_op jit(solution)/shard_map/ppermute | solution.py:118
  23.4 7.6 %collective-permute-start.5 = (f32[64,512]{1,0:T(8,128)S(1)}, f32[64,512]{1,0:T(8,128)S(1)}, u32[]{:S(2)}, u32[]{:S(2)}) collective-permute-start(f32[64,512]{1,0:T(8,128)S(1)} %fusion.2), channel_id=1, source_target_pairs={{0,8},{4,36},{8,16},{12,44},{16,24},{20,52},{24,0},{28,60},{32,40}... | collective-permute-start | bytes 393224 | tf_op jit(solution)/shard_map/ppermute | solution.py:118
  23.4 7.6 %collective-permute-start.4 = (f32[64,512]{1,0:T(8,128)S(1)}, f32[64,512]{1,0:T(8,128)S(1)}, u32[]{:S(2)}, u32[]{:S(2)}) collective-permute-start(f32[64,512]{1,0:T(8,128)S(1)} %fusion.2), channel_id=1, source_target_pairs={{0,16},{4,68},{8,24},{12,76},{16,0},{20,84},{24,8},{28,92},{32,48}... | collective-permute-start | bytes 393224 | tf_op jit(solution)/shard_map/ppermute | solution.py:118
  31.0 4.7 %collective-permute-start.9 = (bf16[64,512]{1,0:T(8,128)(2,1)S(1)}, bf16[64,512]{1,0:T(8,128)(2,1)S(1)}, u32[]{:S(2)}, u32[]{:S(2)}) collective-permute-start(bf16[64,512]{1,0:T(8,128)(2,1)S(1)} %add_convert_fusion.1), channel_id=1, source_target_pairs={{0,96},{4,28},{8,104},{12,4},{16,112},{20,12},{24,120},{28,20},{32... | collective-permute-start | bytes 196616 | tf_op jit(solution)/shard_map/ppermute | solution.py:118
  33.2 5.9 %collective-permute-start.8 = (bf16[64,512]{1,0:T(8,128)(2,1)S(1)}, bf16[64,512]{1,0:T(8,128)(2,1)S(1)}, u32[]{:S(2)}, u32[]{:S(2)}) collective-permute-start(bf16[64,512]{1,0:T(8,128)(2,1)S(1)} %add_convert_fusion.1), channel_id=1, source_target_pairs={{0,64},{4,20},{8,72},{12,28},{16,80},{20,4},{24,88},{28,12},{32,96... | collective-permute-start | bytes 196616 | tf_op jit(solution)/shard_map/ppermute | solution.py:118
  33.2 6.2 %collective-permute-start.7 = (bf16[64,512]{1,0:T(8,128)(2,1)S(1)}, bf16[64,512]{1,0:T(8,128)(2,1)S(1)}, u32[]{:S(2)}, u32[]{:S(2)}) collective-permute-start(bf16[64,512]{1,0:T(8,128)(2,1)S(1)} %add_convert_fusion.1), channel_id=1, source_target_pairs={{0,32},{4,12},{8,40},{12,20},{16,48},{20,28},{24,56},{28,4},{32,64... | collective-permute-start | bytes 196616 | tf_op jit(solution)/shard_map/ppermute | solution.py:118
  39.4 1.6 %collective-permute-start.10 = (bf16[256,512]{1,0:T(8,128)(2,1)S(1)}, bf16[256,512]{1,0:T(8,128)(2,1)S(1)}, u32[]{:S(2)}, u32[]{:S(2)}) collective-permute-start(bf16[256,512]{1,0:T(8,128)(2,1)S(1)} %pad_maximum_fusion.own), channel_id=1, source_target_pairs={{0,4},{4,0},{1,5},{5,1},{2,6},{6,2},{3,7},{7,3},{8,12},{12,8},{9,1... | collective-permute-start | bytes 786440 | tf_op jit(solution)/shard_map/ppermute | solution.py:129
  41.1 44.0 %copy-start.1 = (bf16[1,2048,512]{2,1,0:T(8,128)(2,1)S(1)}, bf16[1,2048,512]{2,1,0:T(8,128)(2,1)}, u32[]{:S(2)}) copy-start(bf16[1,2048,512]{2,1,0:T(8,128)(2,1)} %param.8) | copy-start | bytes 6291460
  57.6 27.4 %copy-start = (bf16[1,2048,512]{2,1,0:T(8,128)(2,1)S(1)}, bf16[1,2048,512]{2,1,0:T(8,128)(2,1)}, u32[]{:S(2)}) copy-start(bf16[1,2048,512]{2,1,0:T(8,128)(2,1)} %param.7) | copy-start | bytes 6291460
  57.6 1.5 %collective-permute-start.11 = (bf16[256,512]{1,0:T(8,128)(2,1)S(1)}, bf16[256,512]{1,0:T(8,128)(2,1)S(1)}, u32[]{:S(2)}, u32[]{:S(2)}) collective-permute-start(bf16[256,512]{1,0:T(8,128)(2,1)S(1)} %get-tuple-element.26), channel_id=1, source_target_pairs={{0,4},{4,0},{1,5},{5,1},{2,6},{6,2},{3,7},{7,3},{8,12},{12,8},{9,1... | collective-permute-start | bytes 786440 | tf_op jit(solution)/shard_map/ppermute | solution.py:129
  59.3 5.8 %collective-permute-start.12 = (bf16[64,512]{1,0:T(8,128)(2,1)S(1)}, bf16[64,512]{1,0:T(8,128)(2,1)S(1)}, u32[]{:S(2)}, u32[]{:S(2)}) collective-permute-start(bf16[64,512]{1,0:T(8,128)(2,1)S(1)} %get-tuple-element.44), channel_id=1, source_target_pairs={{0,64},{4,20},{8,72},{12,28},{16,80},{20,4},{24,88},{28,12},{32,96... | collective-permute-start | bytes 196616 | tf_op jit(solution)/shard_map/ppermute | solution.py:118
  61.0 4.3 %collective-permute-start.14 = (bf16[64,512]{1,0:T(8,128)(2,1)S(1)}, bf16[64,512]{1,0:T(8,128)(2,1)S(1)}, u32[]{:S(2)}, u32[]{:S(2)}) collective-permute-start(bf16[64,512]{1,0:T(8,128)(2,1)S(1)} %get-tuple-element.45), channel_id=1, source_target_pairs={{0,96},{4,28},{8,104},{12,4},{16,112},{20,12},{24,120},{28,20},{32... | collective-permute-start | bytes 196616 | tf_op jit(solution)/shard_map/ppermute | solution.py:118
  61.5 5.5 %collective-permute-start.13 = (bf16[64,512]{1,0:T(8,128)(2,1)S(1)}, bf16[64,512]{1,0:T(8,128)(2,1)S(1)}, u32[]{:S(2)}, u32[]{:S(2)}) collective-permute-start(bf16[64,512]{1,0:T(8,128)(2,1)S(1)} %get-tuple-element.46), channel_id=1, source_target_pairs={{0,32},{4,12},{8,40},{12,20},{16,48},{20,28},{24,56},{28,4},{32,64... | collective-permute-start | bytes 196616 | tf_op jit(solution)/shard_map/ppermute | solution.py:118
  67.0 4.3 %collective-permute-start.17 = (bf16[64,512]{1,0:T(8,128)(2,1)S(1)}, bf16[64,512]{1,0:T(8,128)(2,1)S(1)}, u32[]{:S(2)}, u32[]{:S(2)}) collective-permute-start(bf16[64,512]{1,0:T(8,128)(2,1)S(1)} %fusion.1), channel_id=1, source_target_pairs={{0,24},{4,100},{8,0},{12,108},{16,8},{20,116},{24,16},{28,124},{32... | collective-permute-start | bytes 196616 | tf_op jit(solution)/shard_map/ppermute | solution.py:118
  69.2 6.2 %collective-permute-start.16 = (bf16[64,512]{1,0:T(8,128)(2,1)S(1)}, bf16[64,512]{1,0:T(8,128)(2,1)S(1)}, u32[]{:S(2)}, u32[]{:S(2)}) collective-permute-start(bf16[64,512]{1,0:T(8,128)(2,1)S(1)} %fusion.1), channel_id=1, source_target_pairs={{0,8},{4,36},{8,16},{12,44},{16,24},{20,52},{24,0},{28,60},{32,40}... | collective-permute-start | bytes 196616 | tf_op jit(solution)/shard_map/ppermute | solution.py:118
  69.2 6.2 %collective-permute-start.15 = (bf16[64,512]{1,0:T(8,128)(2,1)S(1)}, bf16[64,512]{1,0:T(8,128)(2,1)S(1)}, u32[]{:S(2)}, u32[]{:S(2)}) collective-permute-start(bf16[64,512]{1,0:T(8,128)(2,1)S(1)} %fusion.1), channel_id=1, source_target_pairs={{0,16},{4,68},{8,24},{12,76},{16,0},{20,84},{24,8},{28,92},{32,48}... | collective-permute-start | bytes 196616 | tf_op jit(solution)/shard_map/ppermute | solution.py:118
  75.5 4.3 %collective-permute-start.20 = (bf16[64,512]{1,0:T(8,128)(2,1)S(1)}, bf16[64,512]{1,0:T(8,128)(2,1)S(1)}, u32[]{:S(2)}, u32[]{:S(2)}) collective-permute-start(bf16[64,512]{1,0:T(8,128)(2,1)S(1)} %add_convert_fusion), channel_id=1, source_target_pairs={{0,96},{4,28},{8,104},{12,4},{16,112},{20,12},{24,120},{28,20},{32... | collective-permute-start | bytes 196616 | tf_op jit(solution)/shard_map/ppermute | solution.py:118
  76.2 5.8 %collective-permute-start.19 = (bf16[64,512]{1,0:T(8,128)(2,1)S(1)}, bf16[64,512]{1,0:T(8,128)(2,1)S(1)}, u32[]{:S(2)}, u32[]{:S(2)}) collective-permute-start(bf16[64,512]{1,0:T(8,128)(2,1)S(1)} %add_convert_fusion), channel_id=1, source_target_pairs={{0,64},{4,20},{8,72},{12,28},{16,80},{20,4},{24,88},{28,12},{32,96... | collective-permute-start | bytes 196616 | tf_op jit(solution)/shard_map/ppermute | solution.py:118
  77.9 5.5 %collective-permute-start.18 = (bf16[64,512]{1,0:T(8,128)(2,1)S(1)}, bf16[64,512]{1,0:T(8,128)(2,1)S(1)}, u32[]{:S(2)}, u32[]{:S(2)}) collective-permute-start(bf16[64,512]{1,0:T(8,128)(2,1)S(1)} %add_convert_fusion), channel_id=1, source_target_pairs={{0,32},{4,12},{8,40},{12,20},{16,48},{20,28},{24,56},{28,4},{32,64... | collective-permute-start | bytes 196616 | tf_op jit(solution)/shard_map/ppermute | solution.py:118
  83.4 1.6 %collective-permute-start.21 = (bf16[256,512]{1,0:T(8,128)(2,1)S(1)}, bf16[256,512]{1,0:T(8,128)(2,1)S(1)}, u32[]{:S(2)}, u32[]{:S(2)}) collective-permute-start(bf16[256,512]{1,0:T(8,128)(2,1)S(1)} %pad_maximum_fusion.1.own), channel_id=1, source_target_pairs={{0,4},{4,0},{1,5},{5,1},{2,6},{6,2},{3,7},{7,3},{8,12},{12,8},{9,1... | collective-permute-start | bytes 786440 | tf_op jit(solution)/shard_map/ppermute | solution.py:129
  85.5 9.6 %collective-permute-start.23 = (bf16[512,256]{1,0:T(8,128)(2,1)S(1)}, bf16[512,256]{1,0:T(8,128)(2,1)S(1)}, u32[]{:S(2)}, u32[]{:S(2)}) collective-permute-start(bf16[512,256]{1,0:T(8,128)(2,1)S(1)} %get-tuple-element.33), channel_id=1, source_target_pairs={{0,1},{1,2},{2,3},{3,0},{4,5},{5,6},{6,7},{7,4},{8,9},{9,10},{10,1... | collective-permute-start | bytes 786440 | tf_op jit(solution)/shard_map/ppermute | solution.py:327
  87.1 9.2 %collective-permute-start.24 = (bf16[512,256]{1,0:T(8,128)(2,1)S(1)}, bf16[512,256]{1,0:T(8,128)(2,1)S(1)}, u32[]{:S(2)}, u32[]{:S(2)}) collective-permute-start(bf16[512,256]{1,0:T(8,128)(2,1)S(1)} %get-tuple-element.34), channel_id=1, source_target_pairs={{0,3},{1,0},{2,1},{3,2},{4,7},{5,4},{6,5},{7,6},{8,11},{9,8},{10,9... | collective-permute-start | bytes 786440 | tf_op jit(solution)/shard_map/ppermute | solution.py:327
  89.3 15.7 %collective-permute-start.22 = (bf16[512,256]{1,0:T(8,128)(2,1)S(1)}, bf16[512,256]{1,0:T(8,128)(2,1)S(1)}, u32[]{:S(2)}, u32[]{:S(2)}) collective-permute-start(bf16[512,256]{1,0:T(8,128)(2,1)S(1)} %get-tuple-element.32), channel_id=1, source_target_pairs={{0,3},{1,0},{2,1},{3,2},{4,7},{5,4},{6,5},{7,6},{8,11},{9,8},{10,9... | collective-permute-start | bytes 786440 | tf_op jit(solution)/shard_map/ppermute | solution.py:327
  96.7 10.5 %collective-permute-start.25 = (bf16[512,256]{1,0:T(8,128)(2,1)S(1)}, bf16[512,256]{1,0:T(8,128)(2,1)S(1)}, u32[]{:S(2)}, u32[]{:S(2)}) collective-permute-start(bf16[512,256]{1,0:T(8,128)(2,1)S(1)} %get-tuple-element.35), channel_id=1, source_target_pairs={{0,1},{1,2},{2,3},{3,0},{4,5},{5,6},{6,7},{7,4},{8,9},{9,10},{10,1... | collective-permute-start | bytes 786440 | tf_op jit(solution)/shard_map/ppermute | solution.py:327
  98.3 1.7 %copy-start.2 = (bf16[2048,256]{1,0:T(8,128)(2,1)S(1)}, bf16[2048,256]{1,0:T(8,128)(2,1)}, u32[]{:S(2)}) copy-start(bf16[2048,256]{1,0:T(8,128)(2,1)} %e_ref.3) | copy-start | bytes 3145732
  98.3 1.7 %copy-start.3 = (bf16[2048,256]{1,0:T(8,128)(2,1)S(1)}, bf16[2048,256]{1,0:T(8,128)(2,1)}, u32[]{:S(2)}) copy-start(bf16[2048,256]{1,0:T(8,128)(2,1)} %f_ref.3) | copy-start | bytes 3145732
  98.3 11.7 %collective-permute-start.27 = (bf16[512,256]{1,0:T(8,128)(2,1)S(1)}, bf16[512,256]{1,0:T(8,128)(2,1)S(1)}, u32[]{:S(2)}, u32[]{:S(2)}) collective-permute-start(bf16[512,256]{1,0:T(8,128)(2,1)S(1)} %get-tuple-element.38), channel_id=1, source_target_pairs={{0,1},{1,2},{2,3},{3,0},{4,5},{5,6},{6,7},{7,4},{8,9},{9,10},{10,1... | collective-permute-start | bytes 786440 | tf_op jit(solution)/shard_map/ppermute | solution.py:327
  103.0 7.0 %collective-permute-start.26 = (bf16[512,256]{1,0:T(8,128)(2,1)S(1)}, bf16[512,256]{1,0:T(8,128)(2,1)S(1)}, u32[]{:S(2)}, u32[]{:S(2)}) collective-permute-start(bf16[512,256]{1,0:T(8,128)(2,1)S(1)} %get-tuple-element.37), channel_id=1, source_target_pairs={{0,3},{1,0},{2,1},{3,2},{4,7},{5,4},{6,5},{7,6},{8,11},{9,8},{10,9... | collective-permute-start | bytes 786440 | tf_op jit(solution)/shard_map/ppermute | solution.py:327

commit v5 on v4

--- a/solution.py
+++ b/solution.py
@@ -95,7 +95,7 @@
             pltpu.VMEM((2, KP, width), F32),
             pltpu.SemaphoreType.DMA((4, 4)),
         ],
-        compiler_params=pltpu.CompilerParams(vmem_limit_bytes=58 << 20),
+        compiler_params=pltpu.CompilerParams(vmem_limit_bytes=52 << 20),
         cost_estimate=cost(4 * tokens * width * KP, 6 << 20),
         name="project",
     )(k, v, e, f)
@@ -114,10 +114,10 @@
 
 
 def from_all(values, second):
-    return [
-        lax.ppermute(value, SEQ, shifts(step, second))
-        for step, value in zip((1, 2, 3), values)
-    ]
+    got = []
+    for step, value in zip((1, 2, 3), values):
+        got.append(lax.ppermute(value, SEQ, shifts(step, second)))
+    return got
 
 
 def summed(own, got):
@@ -347,7 +347,8 @@
     keep, send = project(k, v, key_mixer, value_mixer)
     pieces = total_over_seq(keep, send, F32)
     query_grad, keep, send = attend(q, g, pieces)
-    pieces = unpack(*total_over_seq(keep, send, BF))
+    pieces = total_over_seq(keep, send, BF)
+    pieces = unpack(*pieces)
     mixer_e, mixer_f = mixer_grads(k, v, pieces)
     key_grad, value_grad = input_grads(key_mixer, value_mixer, pieces)
     return (query_grad[None], key_grad[None], value_grad[None], mixer_e, mixer_f)

time: 111 us -> 109 us (0.982)
  no operation moved by 1% of the time
where the time goes in v5:
time: 109 us
  waiting for transfers between devices  46.3 us (42%)
  starting transfers between devices  34.5 us (32%)
  Pallas kernels  25 us (23%)
  other arithmetic  2.08 us (2%)
    ppermute x18, waiting for transfers between devices, from_all(): got.append(lax.ppermute(value, SEQ, shifts(step, second)))  30.4 us
    ppermute x18, starting transfers between devices, from_all(): got.append(lax.ppermute(value, SEQ, shifts(step, second)))  24.4 us
    pallas_call x1, Pallas kernels, attend(): pl.pallas_call(attend_kernel, grid=(tokens // rows,), in_specs=[wide, wid...  16.6 us
    ppermute x6, starting transfers between devices, along(): return lax.ppermute(value, ACROSS, pairs)  9.71 us
    ppermute x6, waiting for transfers between devices, along(): return lax.ppermute(value, ACROSS, pairs)  9.47 us
    ppermute x4, waiting for transfers between devices, swap(): return lax.ppermute(value, 'seq_2', [(0, 1), (1, 0)])  6.35 us
    pallas_call x1, Pallas kernels, project(): pl.pallas_call(project_kernel, in_specs=[hbm] * 4, out_specs=[VM] * 2, ou...  3.54 us
    pallas_call x1, Pallas kernels, input_grads(): pl.pallas_call(input_grads_kernel, grid=(tokens // rows,), in_specs=[thin...  3.01 us
  transfers between devices with their start and end apart: 28, of which 23 were waited for; matrix products, arithmetic and copies ran while one was open for 1% of the time, Pallas kernels for 4%

profile of v5, /device:TPU:0, one launch (start us, length us, event | category | flops | bytes accessed | tf_op | source)
XLA Modules:
  0.0 108.7 jit_solution(1721401996705965653)
XLA Ops:
  0.6 3.5 %project.1 = (f32[256,512]{1,0:T(8,128)S(1)}, f32[256,512]{1,0:T(8,128)S(1)}) custom-call(bf16[2048,512]{1,0:T(8,128)(2,1)} %bitcast.7, bf16[2048,512]{1,0:T(8,128)(2,1)} %bitcast.12, bf16[2048,256]{1,0:T(8,128)(2,1)} %e_ref.3, bf16[2048,256]{1,0:T(8,128)(2,1)} %f_ref.3), custom_call_target="tpu_custom_call" | custom-call | flops 1073741824 | bytes 6291456 | tf_op jit(solution)/shard_map/project/pallas_call | solution.py:85
  4.3 1.9 %collective-permute-done = f32[256,512]{1,0:T(8,128)S(1)} collective-permute-done((f32[256,512]{1,0:T(8,128)S(1)}, f32[256,512]{1,0:T(8,128)S(1)}, u32[]{:S(2)}, u32[]{:S(2)}) %collective-permute-start) | collective-permute-done | bytes 524320 | tf_op jit(solution)/shard_map/ppermute | solution.py:129
  6.3 3.2 %collective-permute-start.3 = (f32[64,512]{1,0:T(8,128)S(1)}, f32[64,512]{1,0:T(8,128)S(1)}, u32[]{:S(2)}, u32[]{:S(2)}) collective-permute-start(f32[64,512]{1,0:T(8,128)S(1)} %get-tuple-element.41), channel_id=1, source_target_pairs={{0,96},{4,28},{8,104},{12,4},{16,112},{20,12},{24,120},{28,20},{32... | collective-permute-start | bytes 393224 | tf_op jit(solution)/shard_map/ppermute | solution.py:119
  9.5 2.2 %collective-permute-start.1 = (f32[64,512]{1,0:T(8,128)S(1)}, f32[64,512]{1,0:T(8,128)S(1)}, u32[]{:S(2)}, u32[]{:S(2)}) collective-permute-start(f32[64,512]{1,0:T(8,128)S(1)} %get-tuple-element.43), channel_id=1, source_target_pairs={{0,64},{4,20},{8,72},{12,28},{16,80},{20,4},{24,88},{28,12},{32,96... | collective-permute-start | bytes 393224 | tf_op jit(solution)/shard_map/ppermute | solution.py:119
  12.0 5.1 %collective-permute-done.2 = f32[64,512]{1,0:T(8,128)S(1)} collective-permute-done((f32[64,512]{1,0:T(8,128)S(1)}, f32[64,512]{1,0:T(8,128)S(1)}, u32[]{:S(2)}, u32[]{:S(2)}) %collective-permute-start.2) | collective-permute-done | bytes 131104 | tf_op jit(solution)/shard_map/ppermute | solution.py:119
  17.1 4.1 %collective-permute-start.6 = (f32[64,512]{1,0:T(8,128)S(1)}, f32[64,512]{1,0:T(8,128)S(1)}, u32[]{:S(2)}, u32[]{:S(2)}) collective-permute-start(f32[64,512]{1,0:T(8,128)S(1)} %fusion.2), channel_id=1, source_target_pairs={{0,24},{4,100},{8,0},{12,108},{16,8},{20,116},{24,16},{28,124},{32... | collective-permute-start | bytes 393224 | tf_op jit(solution)/shard_map/ppermute | solution.py:119
  21.2 1.9 %collective-permute-start.4 = (f32[64,512]{1,0:T(8,128)S(1)}, f32[64,512]{1,0:T(8,128)S(1)}, u32[]{:S(2)}, u32[]{:S(2)}) collective-permute-start(f32[64,512]{1,0:T(8,128)S(1)} %fusion.2), channel_id=1, source_target_pairs={{0,16},{4,68},{8,24},{12,76},{16,0},{20,84},{24,8},{28,92},{32,48}... | collective-permute-start | bytes 393224 | tf_op jit(solution)/shard_map/ppermute | solution.py:119
  23.1 0.7 collective-permute-done.6
  23.8 5.1 %collective-permute-done.5 = f32[64,512]{1,0:T(8,128)S(1)} collective-permute-done((f32[64,512]{1,0:T(8,128)S(1)}, f32[64,512]{1,0:T(8,128)S(1)}, u32[]{:S(2)}, u32[]{:S(2)}) %collective-permute-start.5) | collective-permute-done | bytes 131104 | tf_op jit(solution)/shard_map/ppermute | solution.py:119
  28.9 2.2 %collective-permute-start.9 = (bf16[64,512]{1,0:T(8,128)(2,1)S(1)}, bf16[64,512]{1,0:T(8,128)(2,1)S(1)}, u32[]{:S(2)}, u32[]{:S(2)}) collective-permute-start(bf16[64,512]{1,0:T(8,128)(2,1)S(1)} %add_convert_fusion.1), channel_id=1, source_target_pairs={{0,96},{4,28},{8,104},{12,4},{16,112},{20,12},{24,120},{28,20},{32... | collective-permute-start | bytes 196616 | tf_op jit(solution)/shard_map/ppermute | solution.py:119
  31.1 0.9 collective-permute-start.7
  32.0 1.6 %collective-permute-done.9 = bf16[64,512]{1,0:T(8,128)(2,1)S(1)} collective-permute-done((bf16[64,512]{1,0:T(8,128)(2,1)S(1)}, bf16[64,512]{1,0:T(8,128)(2,1)S(1)}, u32[]{:S(2)}, u32[]{:S(2)}) %collective-permute-start.9) | collective-permute-done | bytes 65568 | tf_op jit(solution)/shard_map/ppermute | solution.py:119
  33.6 3.3 %collective-permute-done.8 = bf16[64,512]{1,0:T(8,128)(2,1)S(1)} collective-permute-done((bf16[64,512]{1,0:T(8,128)(2,1)S(1)}, bf16[64,512]{1,0:T(8,128)(2,1)S(1)}, u32[]{:S(2)}, u32[]{:S(2)}) %collective-permute-start.8) | collective-permute-done | bytes 65568 | tf_op jit(solution)/shard_map/ppermute | solution.py:119
  37.4 1.5 %collective-permute-done.10.other = bf16[256,512]{1,0:T(8,128)(2,1)S(1)} collective-permute-done((bf16[256,512]{1,0:T(8,128)(2,1)S(1)}, bf16[256,512]{1,0:T(8,128)(2,1)S(1)}, u32[]{:S(2)}, u32[]{:S(2)}) %collective-permute-start.10) | collective-permute-done | bytes 262176 | tf_op jit(solution)/shard_map/ppermute | solution.py:129
  38.9 16.6 %attend.1 = (bf16[2048,512]{1,0:T(8,128)(2,1)}, f32[256,512]{1,0:T(8,128)S(1)}, bf16[256,512]{1,0:T(8,128)(2,1)S(1)}) custom-call(bf16[2048,512]{1,0:T(8,128)(2,1)S(1)} %bitcast.17, bf16[2048,512]{1,0:T(8,128)(2,1)S(1)} %bitcast.18, bf16[256,512]{1,0:T(8,128)(2,1)S(1)} %pad_maximum_fusion.own, bf16[256,512]{1,0:T(8,128)(2,1)S(1)} %collective-permute-done.10.other), custom_call_target="tpu_custom_call" | custom-call | flops 4294967296 | bytes 8388608 | tf_op jit(solution)/shard_map/attend/pallas_call | solution.py:227
  55.6 1.4 %collective-permute-done.11 = bf16[256,512]{1,0:T(8,128)(2,1)S(1)} collective-permute-done((bf16[256,512]{1,0:T(8,128)(2,1)S(1)}, bf16[256,512]{1,0:T(8,128)(2,1)S(1)}, u32[]{:S(2)}, u32[]{:S(2)}) %collective-permute-start.11) | collective-permute-done | bytes 262176 | tf_op jit(solution)/shard_map/ppermute | solution.py:129
  57.1 1.7 %collective-permute-start.12 = (bf16[64,512]{1,0:T(8,128)(2,1)S(1)}, bf16[64,512]{1,0:T(8,128)(2,1)S(1)}, u32[]{:S(2)}, u32[]{:S(2)}) collective-permute-start(bf16[64,512]{1,0:T(8,128)(2,1)S(1)} %get-tuple-element.44), channel_id=1, source_target_pairs={{0,64},{4,20},{8,72},{12,28},{16,80},{20,4},{24,88},{28,12},{32,96... | collective-permute-start | bytes 196616 | tf_op jit(solution)/shard_map/ppermute | solution.py:119
  58.8 0.6 collective-permute-start.14
  59.4 1.5 %collective-permute-start.13 = (bf16[64,512]{1,0:T(8,128)(2,1)S(1)}, bf16[64,512]{1,0:T(8,128)(2,1)S(1)}, u32[]{:S(2)}, u32[]{:S(2)}) collective-permute-start(bf16[64,512]{1,0:T(8,128)(2,1)S(1)} %get-tuple-element.46), channel_id=1, source_target_pairs={{0,32},{4,12},{8,40},{12,20},{16,48},{20,28},{24,56},{28,4},{32,64... | collective-permute-start | bytes 196616 | tf_op jit(solution)/shard_map/ppermute | solution.py:119
  60.8 2.1 %collective-permute-done.12 = bf16[64,512]{1,0:T(8,128)(2,1)S(1)} collective-permute-done((bf16[64,512]{1,0:T(8,128)(2,1)S(1)}, bf16[64,512]{1,0:T(8,128)(2,1)S(1)}, u32[]{:S(2)}, u32[]{:S(2)}) %collective-permute-start.12) | collective-permute-done | bytes 65568 | tf_op jit(solution)/shard_map/ppermute | solution.py:119
  63.1 1.8 %collective-permute-done.13 = bf16[64,512]{1,0:T(8,128)(2,1)S(1)} collective-permute-done((bf16[64,512]{1,0:T(8,128)(2,1)S(1)}, bf16[64,512]{1,0:T(8,128)(2,1)S(1)}, u32[]{:S(2)}, u32[]{:S(2)}) %collective-permute-start.13) | collective-permute-done | bytes 65568 | tf_op jit(solution)/shard_map/ppermute | solution.py:119
  64.9 2.2 %collective-permute-start.17 = (bf16[64,512]{1,0:T(8,128)(2,1)S(1)}, bf16[64,512]{1,0:T(8,128)(2,1)S(1)}, u32[]{:S(2)}, u32[]{:S(2)}) collective-permute-start(bf16[64,512]{1,0:T(8,128)(2,1)S(1)} %fusion.1), channel_id=1, source_target_pairs={{0,24},{4,100},{8,0},{12,108},{16,8},{20,116},{24,16},{28,124},{32... | collective-permute-start | bytes 196616 | tf_op jit(solution)/shard_map/ppermute | solution.py:119
  67.0 1.5 %collective-permute-start.15 = (bf16[64,512]{1,0:T(8,128)(2,1)S(1)}, bf16[64,512]{1,0:T(8,128)(2,1)S(1)}, u32[]{:S(2)}, u32[]{:S(2)}) collective-permute-start(bf16[64,512]{1,0:T(8,128)(2,1)S(1)} %fusion.1), channel_id=1, source_target_pairs={{0,16},{4,68},{8,24},{12,76},{16,0},{20,84},{24,8},{28,92},{32,48}... | collective-permute-start | bytes 196616 | tf_op jit(solution)/shard_map/ppermute | solution.py:119
  68.6 0.6 collective-permute-done.17
  69.2 4.0 %collective-permute-done.16 = bf16[64,512]{1,0:T(8,128)(2,1)S(1)} collective-permute-done((bf16[64,512]{1,0:T(8,128)(2,1)S(1)}, bf16[64,512]{1,0:T(8,128)(2,1)S(1)}, u32[]{:S(2)}, u32[]{:S(2)}) %collective-permute-start.16) | collective-permute-done | bytes 65568 | tf_op jit(solution)/shard_map/ppermute | solution.py:119
  73.3 0.8 collective-permute-start.20
  74.1 1.6 %collective-permute-start.19 = (bf16[64,512]{1,0:T(8,128)(2,1)S(1)}, bf16[64,512]{1,0:T(8,128)(2,1)S(1)}, u32[]{:S(2)}, u32[]{:S(2)}) collective-permute-start(bf16[64,512]{1,0:T(8,128)(2,1)S(1)} %add_convert_fusion), channel_id=1, source_target_pairs={{0,64},{4,20},{8,72},{12,28},{16,80},{20,4},{24,88},{28,12},{32,96... | collective-permute-start | bytes 196616 | tf_op jit(solution)/shard_map/ppermute | solution.py:119
  75.7 1.9 %collective-permute-done.20 = bf16[64,512]{1,0:T(8,128)(2,1)S(1)} collective-permute-done((bf16[64,512]{1,0:T(8,128)(2,1)S(1)}, bf16[64,512]{1,0:T(8,128)(2,1)S(1)}, u32[]{:S(2)}, u32[]{:S(2)}) %collective-permute-start.20) | collective-permute-done | bytes 65568 | tf_op jit(solution)/shard_map/ppermute | solution.py:119
  77.6 2.2 %collective-permute-done.19 = bf16[64,512]{1,0:T(8,128)(2,1)S(1)} collective-permute-done((bf16[64,512]{1,0:T(8,128)(2,1)S(1)}, bf16[64,512]{1,0:T(8,128)(2,1)S(1)}, u32[]{:S(2)}, u32[]{:S(2)}) %collective-permute-start.19) | collective-permute-done | bytes 65568 | tf_op jit(solution)/shard_map/ppermute | solution.py:119
  79.8 1.3 %collective-permute-done.18 = bf16[64,512]{1,0:T(8,128)(2,1)S(1)} collective-permute-done((bf16[64,512]{1,0:T(8,128)(2,1)S(1)}, bf16[64,512]{1,0:T(8,128)(2,1)S(1)}, u32[]{:S(2)}, u32[]{:S(2)}) %collective-permute-start.18) | collective-permute-done | bytes 65568 | tf_op jit(solution)/shard_map/ppermute | solution.py:119
  81.3 1.5 %collective-permute-done.21.other = bf16[256,512]{1,0:T(8,128)(2,1)S(1)} collective-permute-done((bf16[256,512]{1,0:T(8,128)(2,1)S(1)}, bf16[256,512]{1,0:T(8,128)(2,1)S(1)}, u32[]{:S(2)}, u32[]{:S(2)}) %collective-permute-start.21) | collective-permute-done | bytes 262176 | tf_op jit(solution)/shard_map/ppermute | solution.py:129
  82.9 0.5 mixer_part.6
  83.4 1.6 %collective-permute-start.23 = (bf16[512,256]{1,0:T(8,128)(2,1)S(1)}, bf16[512,256]{1,0:T(8,128)(2,1)S(1)}, u32[]{:S(2)}, u32[]{:S(2)}) collective-permute-start(bf16[512,256]{1,0:T(8,128)(2,1)S(1)} %get-tuple-element.33), channel_id=1, source_target_pairs={{0,1},{1,2},{2,3},{3,0},{4,5},{5,6},{6,7},{7,4},{8,9},{9,10},{10,1... | collective-permute-start | bytes 786440 | tf_op jit(solution)/shard_map/ppermute | solution.py:327
  84.9 1.7 %collective-permute-start.24 = (bf16[512,256]{1,0:T(8,128)(2,1)S(1)}, bf16[512,256]{1,0:T(8,128)(2,1)S(1)}, u32[]{:S(2)}, u32[]{:S(2)}) collective-permute-start(bf16[512,256]{1,0:T(8,128)(2,1)S(1)} %get-tuple-element.34), channel_id=1, source_target_pairs={{0,3},{1,0},{2,1},{3,2},{4,7},{5,4},{6,5},{7,6},{8,11},{9,8},{10,9... | collective-permute-start | bytes 786440 | tf_op jit(solution)/shard_map/ppermute | solution.py:327
  86.7 0.5 mixer_part.5
  87.1 1.6 %collective-permute-start.22 = (bf16[512,256]{1,0:T(8,128)(2,1)S(1)}, bf16[512,256]{1,0:T(8,128)(2,1)S(1)}, u32[]{:S(2)}, u32[]{:S(2)}) collective-permute-start(bf16[512,256]{1,0:T(8,128)(2,1)S(1)} %get-tuple-element.32), channel_id=1, source_target_pairs={{0,3},{1,0},{2,1},{3,2},{4,7},{5,4},{6,5},{7,6},{8,11},{9,8},{10,9... | collective-permute-start | bytes 786440 | tf_op jit(solution)/shard_map/ppermute | solution.py:327
  88.7 4.2 %collective-permute-done.23.refs_0_ = bf16[512,256]{1,0:T(8,128)(2,1)S(1)} collective-permute-done((bf16[512,256]{1,0:T(8,128)(2,1)S(1)}, bf16[512,256]{1,0:T(8,128)(2,1)S(1)}, u32[]{:S(2)}, u32[]{:S(2)}) %collective-permute-start.23) | collective-permute-done | bytes 262176 | tf_op jit(solution)/shard_map/ppermute | solution.py:327
  93.0 1.1 %collective-permute-done.24.refs_1_ = bf16[512,256]{1,0:T(8,128)(2,1)S(1)} collective-permute-done((bf16[512,256]{1,0:T(8,128)(2,1)S(1)}, bf16[512,256]{1,0:T(8,128)(2,1)S(1)}, u32[]{:S(2)}, u32[]{:S(2)}) %collective-permute-start.24) | collective-permute-done | bytes 262176 | tf_op jit(solution)/shard_map/ppermute | solution.py:327
  94.1 0.5 mixer_part.7
  94.6 1.6 %collective-permute-start.25 = (bf16[512,256]{1,0:T(8,128)(2,1)S(1)}, bf16[512,256]{1,0:T(8,128)(2,1)S(1)}, u32[]{:S(2)}, u32[]{:S(2)}) collective-permute-start(bf16[512,256]{1,0:T(8,128)(2,1)S(1)} %get-tuple-element.35), channel_id=1, source_target_pairs={{0,1},{1,2},{2,3},{3,0},{4,5},{5,6},{6,7},{7,4},{8,9},{9,10},{10,1... | collective-permute-start | bytes 786440 | tf_op jit(solution)/shard_map/ppermute | solution.py:327
  96.1 1.2 %collective-permute-start.27 = (bf16[512,256]{1,0:T(8,128)(2,1)S(1)}, bf16[512,256]{1,0:T(8,128)(2,1)S(1)}, u32[]{:S(2)}, u32[]{:S(2)}) collective-permute-start(bf16[512,256]{1,0:T(8,128)(2,1)S(1)} %get-tuple-element.38), channel_id=1, source_target_pairs={{0,1},{1,2},{2,3},{3,0},{4,5},{5,6},{6,7},{7,4},{8,9},{9,10},{10,1... | collective-permute-start | bytes 786440 | tf_op jit(solution)/shard_map/ppermute | solution.py:327
  97.3 0.5 mixer_part.4
  97.8 3.0 %input_grads.1 = (bf16[2048,512]{1,0:T(8,128)(2,1)}, bf16[2048,512]{1,0:T(8,128)(2,1)}) custom-call(bf16[2048,256]{1,0:T(8,128)(2,1)S(1)} %copy-done.2, bf16[2048,256]{1,0:T(8,128)(2,1)S(1)} %copy-done.3, bf16[256,512]{1,0:T(8,128)(2,1)S(1)} %get-tuple-element.27.dpk, bf16[256,512]{1,0:T(8,128)(2,1)S(1)} %get-tuple-element.28.dpv), custom_call_target="tpu_custom_call" | custom-call | flops 1073741824 | bytes 6291456 | tf_op jit(solution)/shard_map/input_grads/pallas_call | solution.py:312
  100.8 2.0 %collective-permute-start.26 = (bf16[512,256]{1,0:T(8,128)(2,1)S(1)}, bf16[512,256]{1,0:T(8,128)(2,1)S(1)}, u32[]{:S(2)}, u32[]{:S(2)}) collective-permute-start(bf16[512,256]{1,0:T(8,128)(2,1)S(1)} %get-tuple-element.37), channel_id=1, source_target_pairs={{0,3},{1,0},{2,1},{3,2},{4,7},{5,4},{6,5},{7,6},{8,11},{9,8},{10,9... | collective-permute-start | bytes 786440 | tf_op jit(solution)/shard_map/ppermute | solution.py:327
  102.9 2.1 %collective-permute-done.25 = bf16[512,256]{1,0:T(8,128)(2,1)S(1)} collective-permute-done((bf16[512,256]{1,0:T(8,128)(2,1)S(1)}, bf16[512,256]{1,0:T(8,128)(2,1)S(1)}, u32[]{:S(2)}, u32[]{:S(2)}) %collective-permute-start.25) | collective-permute-done | bytes 262176 | tf_op jit(solution)/shard_map/ppermute | solution.py:327
  105.0 0.9 add_add_fusion.1
  105.9 2.0 %collective-permute-done.27 = bf16[512,256]{1,0:T(8,128)(2,1)S(1)} collective-permute-done((bf16[512,256]{1,0:T(8,128)(2,1)S(1)}, bf16[512,256]{1,0:T(8,128)(2,1)S(1)}, u32[]{:S(2)}, u32[]{:S(2)}) %collective-permute-start.27) | collective-permute-done | bytes 262176 | tf_op jit(solution)/shard_map/ppermute | solution.py:327
  107.9 0.9 add_add_fusion
  (40 shorter events, 1.6 us)
Async XLA Ops:
  0.6 38.2 %copy-start.5 = (bf16[1,2048,512]{2,1,0:T(8,128)(2,1)S(1)}, bf16[1,2048,512]{2,1,0:T(8,128)(2,1)}, u32[]{:S(2)}) copy-start(bf16[1,2048,512]{2,1,0:T(8,128)(2,1)} %param.9) | copy-start | bytes 6291460
  4.2 34.7 %copy-start.4 = (bf16[1,2048,512]{2,1,0:T(8,128)(2,1)S(1)}, bf16[1,2048,512]{2,1,0:T(8,128)(2,1)}, u32[]{:S(2)}) copy-start(bf16[1,2048,512]{2,1,0:T(8,128)(2,1)} %param.6) | copy-start | bytes 6291460
  4.2 2.0 %collective-permute-start = (f32[256,512]{1,0:T(8,128)S(1)}, f32[256,512]{1,0:T(8,128)S(1)}, u32[]{:S(2)}, u32[]{:S(2)}) collective-permute-start(f32[256,512]{1,0:T(8,128)S(1)} %get-tuple-element.23), channel_id=1, source_target_pairs={{0,4},{4,0},{1,5},{5,1},{2,6},{6,2},{3,7},{7,3},{8,12},{12,8},{9,1... | collective-permute-start | bytes 1572872 | tf_op jit(solution)/shard_map/ppermute | solution.py:129
  6.3 5.7 %collective-permute-start.3 = (f32[64,512]{1,0:T(8,128)S(1)}, f32[64,512]{1,0:T(8,128)S(1)}, u32[]{:S(2)}, u32[]{:S(2)}) collective-permute-start(f32[64,512]{1,0:T(8,128)S(1)} %get-tuple-element.41), channel_id=1, source_target_pairs={{0,96},{4,28},{8,104},{12,4},{16,112},{20,12},{24,120},{28,20},{32... | collective-permute-start | bytes 393224 | tf_op jit(solution)/shard_map/ppermute | solution.py:119
  9.5 7.6 %collective-permute-start.2 = (f32[64,512]{1,0:T(8,128)S(1)}, f32[64,512]{1,0:T(8,128)S(1)}, u32[]{:S(2)}, u32[]{:S(2)}) collective-permute-start(f32[64,512]{1,0:T(8,128)S(1)} %get-tuple-element.42), channel_id=1, source_target_pairs={{0,32},{4,12},{8,40},{12,20},{16,48},{20,28},{24,56},{28,4},{32,64... | collective-permute-start | bytes 393224 | tf_op jit(solution)/shard_map/ppermute | solution.py:119
  9.5 7.6 %collective-permute-start.1 = (f32[64,512]{1,0:T(8,128)S(1)}, f32[64,512]{1,0:T(8,128)S(1)}, u32[]{:S(2)}, u32[]{:S(2)}) collective-permute-start(f32[64,512]{1,0:T(8,128)S(1)} %get-tuple-element.43), channel_id=1, source_target_pairs={{0,64},{4,20},{8,72},{12,28},{16,80},{20,4},{24,88},{28,12},{32,96... | collective-permute-start | bytes 393224 | tf_op jit(solution)/shard_map/ppermute | solution.py:119
  17.1 6.6 %collective-permute-start.6 = (f32[64,512]{1,0:T(8,128)S(1)}, f32[64,512]{1,0:T(8,128)S(1)}, u32[]{:S(2)}, u32[]{:S(2)}) collective-permute-start(f32[64,512]{1,0:T(8,128)S(1)} %fusion.2), channel_id=1, source_target_pairs={{0,24},{4,100},{8,0},{12,108},{16,8},{20,116},{24,16},{28,124},{32... | collective-permute-start | bytes 393224 | tf_op jit(solution)/shard_map/ppermute | solution.py:119
  21.2 7.6 %collective-permute-start.5 = (f32[64,512]{1,0:T(8,128)S(1)}, f32[64,512]{1,0:T(8,128)S(1)}, u32[]{:S(2)}, u32[]{:S(2)}) collective-permute-start(f32[64,512]{1,0:T(8,128)S(1)} %fusion.2), channel_id=1, source_target_pairs={{0,8},{4,36},{8,16},{12,44},{16,24},{20,52},{24,0},{28,60},{32,40}... | collective-permute-start | bytes 393224 | tf_op jit(solution)/shard_map/ppermute | solution.py:119
  21.2 7.6 %collective-permute-start.4 = (f32[64,512]{1,0:T(8,128)S(1)}, f32[64,512]{1,0:T(8,128)S(1)}, u32[]{:S(2)}, u32[]{:S(2)}) collective-permute-start(f32[64,512]{1,0:T(8,128)S(1)} %fusion.2), channel_id=1, source_target_pairs={{0,16},{4,68},{8,24},{12,76},{16,0},{20,84},{24,8},{28,92},{32,48}... | collective-permute-start | bytes 393224 | tf_op jit(solution)/shard_map/ppermute | solution.py:119
  28.9 4.7 %collective-permute-start.9 = (bf16[64,512]{1,0:T(8,128)(2,1)S(1)}, bf16[64,512]{1,0:T(8,128)(2,1)S(1)}, u32[]{:S(2)}, u32[]{:S(2)}) collective-permute-start(bf16[64,512]{1,0:T(8,128)(2,1)S(1)} %add_convert_fusion.1), channel_id=1, source_target_pairs={{0,96},{4,28},{8,104},{12,4},{16,112},{20,12},{24,120},{28,20},{32... | collective-permute-start | bytes 196616 | tf_op jit(solution)/shard_map/ppermute | solution.py:119
  31.1 5.9 %collective-permute-start.8 = (bf16[64,512]{1,0:T(8,128)(2,1)S(1)}, bf16[64,512]{1,0:T(8,128)(2,1)S(1)}, u32[]{:S(2)}, u32[]{:S(2)}) collective-permute-start(bf16[64,512]{1,0:T(8,128)(2,1)S(1)} %add_convert_fusion.1), channel_id=1, source_target_pairs={{0,64},{4,20},{8,72},{12,28},{16,80},{20,4},{24,88},{28,12},{32,96... | collective-permute-start | bytes 196616 | tf_op jit(solution)/shard_map/ppermute | solution.py:119
  31.1 6.2 %collective-permute-start.7 = (bf16[64,512]{1,0:T(8,128)(2,1)S(1)}, bf16[64,512]{1,0:T(8,128)(2,1)S(1)}, u32[]{:S(2)}, u32[]{:S(2)}) collective-permute-start(bf16[64,512]{1,0:T(8,128)(2,1)S(1)} %add_convert_fusion.1), channel_id=1, source_target_pairs={{0,32},{4,12},{8,40},{12,20},{16,48},{20,28},{24,56},{28,4},{32,64... | collective-permute-start | bytes 196616 | tf_op jit(solution)/shard_map/ppermute | solution.py:119
  37.3 1.6 %collective-permute-start.10 = (bf16[256,512]{1,0:T(8,128)(2,1)S(1)}, bf16[256,512]{1,0:T(8,128)(2,1)S(1)}, u32[]{:S(2)}, u32[]{:S(2)}) collective-permute-start(bf16[256,512]{1,0:T(8,128)(2,1)S(1)} %pad_maximum_fusion.own), channel_id=1, source_target_pairs={{0,4},{4,0},{1,5},{5,1},{2,6},{6,2},{3,7},{7,3},{8,12},{12,8},{9,1... | collective-permute-start | bytes 786440 | tf_op jit(solution)/shard_map/ppermute | solution.py:129
  38.9 44.0 %copy-start.1 = (bf16[1,2048,512]{2,1,0:T(8,128)(2,1)S(1)}, bf16[1,2048,512]{2,1,0:T(8,128)(2,1)}, u32[]{:S(2)}) copy-start(bf16[1,2048,512]{2,1,0:T(8,128)(2,1)} %param.8) | copy-start | bytes 6291460
  55.4 27.4 %copy-start = (bf16[1,2048,512]{2,1,0:T(8,128)(2,1)S(1)}, bf16[1,2048,512]{2,1,0:T(8,128)(2,1)}, u32[]{:S(2)}) copy-start(bf16[1,2048,512]{2,1,0:T(8,128)(2,1)} %param.7) | copy-start | bytes 6291460
  55.4 1.5 %collective-permute-start.11 = (bf16[256,512]{1,0:T(8,128)(2,1)S(1)}, bf16[256,512]{1,0:T(8,128)(2,1)S(1)}, u32[]{:S(2)}, u32[]{:S(2)}) collective-permute-start(bf16[256,512]{1,0:T(8,128)(2,1)S(1)} %get-tuple-element.26), channel_id=1, source_target_pairs={{0,4},{4,0},{1,5},{5,1},{2,6},{6,2},{3,7},{7,3},{8,12},{12,8},{9,1... | collective-permute-start | bytes 786440 | tf_op jit(solution)/shard_map/ppermute | solution.py:129
  57.1 5.8 %collective-permute-start.12 = (bf16[64,512]{1,0:T(8,128)(2,1)S(1)}, bf16[64,512]{1,0:T(8,128)(2,1)S(1)}, u32[]{:S(2)}, u32[]{:S(2)}) collective-permute-start(bf16[64,512]{1,0:T(8,128)(2,1)S(1)} %get-tuple-element.44), channel_id=1, source_target_pairs={{0,64},{4,20},{8,72},{12,28},{16,80},{20,4},{24,88},{28,12},{32,96... | collective-permute-start | bytes 196616 | tf_op jit(solution)/shard_map/ppermute | solution.py:119
  58.8 4.3 %collective-permute-start.14 = (bf16[64,512]{1,0:T(8,128)(2,1)S(1)}, bf16[64,512]{1,0:T(8,128)(2,1)S(1)}, u32[]{:S(2)}, u32[]{:S(2)}) collective-permute-start(bf16[64,512]{1,0:T(8,128)(2,1)S(1)} %get-tuple-element.45), channel_id=1, source_target_pairs={{0,96},{4,28},{8,104},{12,4},{16,112},{20,12},{24,120},{28,20},{32... | collective-permute-start | bytes 196616 | tf_op jit(solution)/shard_map/ppermute | solution.py:119
  59.4 5.5 %collective-permute-start.13 = (bf16[64,512]{1,0:T(8,128)(2,1)S(1)}, bf16[64,512]{1,0:T(8,128)(2,1)S(1)}, u32[]{:S(2)}, u32[]{:S(2)}) collective-permute-start(bf16[64,512]{1,0:T(8,128)(2,1)S(1)} %get-tuple-element.46), channel_id=1, source_target_pairs={{0,32},{4,12},{8,40},{12,20},{16,48},{20,28},{24,56},{28,4},{32,64... | collective-permute-start | bytes 196616 | tf_op jit(solution)/shard_map/ppermute | solution.py:119
  64.9 4.3 %collective-permute-start.17 = (bf16[64,512]{1,0:T(8,128)(2,1)S(1)}, bf16[64,512]{1,0:T(8,128)(2,1)S(1)}, u32[]{:S(2)}, u32[]{:S(2)}) collective-permute-start(bf16[64,512]{1,0:T(8,128)(2,1)S(1)} %fusion.1), channel_id=1, source_target_pairs={{0,24},{4,100},{8,0},{12,108},{16,8},{20,116},{24,16},{28,124},{32... | collective-permute-start | bytes 196616 | tf_op jit(solution)/shard_map/ppermute | solution.py:119
  67.0 6.2 %collective-permute-start.16 = (bf16[64,512]{1,0:T(8,128)(2,1)S(1)}, bf16[64,512]{1,0:T(8,128)(2,1)S(1)}, u32[]{:S(2)}, u32[]{:S(2)}) collective-permute-start(bf16[64,512]{1,0:T(8,128)(2,1)S(1)} %fusion.1), channel_id=1, source_target_pairs={{0,8},{4,36},{8,16},{12,44},{16,24},{20,52},{24,0},{28,60},{32,40}... | collective-permute-start | bytes 196616 | tf_op jit(solution)/shard_map/ppermute | solution.py:119
  67.0 6.2 %collective-permute-start.15 = (bf16[64,512]{1,0:T(8,128)(2,1)S(1)}, bf16[64,512]{1,0:T(8,128)(2,1)S(1)}, u32[]{:S(2)}, u32[]{:S(2)}) collective-permute-start(bf16[64,512]{1,0:T(8,128)(2,1)S(1)} %fusion.1), channel_id=1, source_target_pairs={{0,16},{4,68},{8,24},{12,76},{16,0},{20,84},{24,8},{28,92},{32,48}... | collective-permute-start | bytes 196616 | tf_op jit(solution)/shard_map/ppermute | solution.py:119
  73.3 4.3 %collective-permute-start.20 = (bf16[64,512]{1,0:T(8,128)(2,1)S(1)}, bf16[64,512]{1,0:T(8,128)(2,1)S(1)}, u32[]{:S(2)}, u32[]{:S(2)}) collective-permute-start(bf16[64,512]{1,0:T(8,128)(2,1)S(1)} %add_convert_fusion), channel_id=1, source_target_pairs={{0,96},{4,28},{8,104},{12,4},{16,112},{20,12},{24,120},{28,20},{32... | collective-permute-start | bytes 196616 | tf_op jit(solution)/shard_map/ppermute | solution.py:119
  74.1 5.8 %collective-permute-start.19 = (bf16[64,512]{1,0:T(8,128)(2,1)S(1)}, bf16[64,512]{1,0:T(8,128)(2,1)S(1)}, u32[]{:S(2)}, u32[]{:S(2)}) collective-permute-start(bf16[64,512]{1,0:T(8,128)(2,1)S(1)} %add_convert_fusion), channel_id=1, source_target_pairs={{0,64},{4,20},{8,72},{12,28},{16,80},{20,4},{24,88},{28,12},{32,96... | collective-permute-start | bytes 196616 | tf_op jit(solution)/shard_map/ppermute | solution.py:119
  75.7 5.5 %collective-permute-start.18 = (bf16[64,512]{1,0:T(8,128)(2,1)S(1)}, bf16[64,512]{1,0:T(8,128)(2,1)S(1)}, u32[]{:S(2)}, u32[]{:S(2)}) collective-permute-start(bf16[64,512]{1,0:T(8,128)(2,1)S(1)} %add_convert_fusion), channel_id=1, source_target_pairs={{0,32},{4,12},{8,40},{12,20},{16,48},{20,28},{24,56},{28,4},{32,64... | collective-permute-start | bytes 196616 | tf_op jit(solution)/shard_map/ppermute | solution.py:119
  81.2 1.6 %collective-permute-start.21 = (bf16[256,512]{1,0:T(8,128)(2,1)S(1)}, bf16[256,512]{1,0:T(8,128)(2,1)S(1)}, u32[]{:S(2)}, u32[]{:S(2)}) collective-permute-start(bf16[256,512]{1,0:T(8,128)(2,1)S(1)} %pad_maximum_fusion.1.own), channel_id=1, source_target_pairs={{0,4},{4,0},{1,5},{5,1},{2,6},{6,2},{3,7},{7,3},{8,12},{12,8},{9,1... | collective-permute-start | bytes 786440 | tf_op jit(solution)/shard_map/ppermute | solution.py:129
  83.4 9.6 %collective-permute-start.23 = (bf16[512,256]{1,0:T(8,128)(2,1)S(1)}, bf16[512,256]{1,0:T(8,128)(2,1)S(1)}, u32[]{:S(2)}, u32[]{:S(2)}) collective-permute-start(bf16[512,256]{1,0:T(8,128)(2,1)S(1)} %get-tuple-element.33), channel_id=1, source_target_pairs={{0,1},{1,2},{2,3},{3,0},{4,5},{5,6},{6,7},{7,4},{8,9},{9,10},{10,1... | collective-permute-start | bytes 786440 | tf_op jit(solution)/shard_map/ppermute | solution.py:327
  84.9 9.2 %collective-permute-start.24 = (bf16[512,256]{1,0:T(8,128)(2,1)S(1)}, bf16[512,256]{1,0:T(8,128)(2,1)S(1)}, u32[]{:S(2)}, u32[]{:S(2)}) collective-permute-start(bf16[512,256]{1,0:T(8,128)(2,1)S(1)} %get-tuple-element.34), channel_id=1, source_target_pairs={{0,3},{1,0},{2,1},{3,2},{4,7},{5,4},{6,5},{7,6},{8,11},{9,8},{10,9... | collective-permute-start | bytes 786440 | tf_op jit(solution)/shard_map/ppermute | solution.py:327
  87.1 15.7 %collective-permute-start.22 = (bf16[512,256]{1,0:T(8,128)(2,1)S(1)}, bf16[512,256]{1,0:T(8,128)(2,1)S(1)}, u32[]{:S(2)}, u32[]{:S(2)}) collective-permute-start(bf16[512,256]{1,0:T(8,128)(2,1)S(1)} %get-tuple-element.32), channel_id=1, source_target_pairs={{0,3},{1,0},{2,1},{3,2},{4,7},{5,4},{6,5},{7,6},{8,11},{9,8},{10,9... | collective-permute-start | bytes 786440 | tf_op jit(solution)/shard_map/ppermute | solution.py:327
  94.6 10.5 %collective-permute-start.25 = (bf16[512,256]{1,0:T(8,128)(2,1)S(1)}, bf16[512,256]{1,0:T(8,128)(2,1)S(1)}, u32[]{:S(2)}, u32[]{:S(2)}) collective-permute-start(bf16[512,256]{1,0:T(8,128)(2,1)S(1)} %get-tuple-element.35), channel_id=1, source_target_pairs={{0,1},{1,2},{2,3},{3,0},{4,5},{5,6},{6,7},{7,4},{8,9},{9,10},{10,1... | collective-permute-start | bytes 786440 | tf_op jit(solution)/shard_map/ppermute | solution.py:327
  96.1 1.7 %copy-start.2 = (bf16[2048,256]{1,0:T(8,128)(2,1)S(1)}, bf16[2048,256]{1,0:T(8,128)(2,1)}, u32[]{:S(2)}) copy-start(bf16[2048,256]{1,0:T(8,128)(2,1)} %e_ref.3) | copy-start | bytes 3145732
  96.1 1.7 %copy-start.3 = (bf16[2048,256]{1,0:T(8,128)(2,1)S(1)}, bf16[2048,256]{1,0:T(8,128)(2,1)}, u32[]{:S(2)}) copy-start(bf16[2048,256]{1,0:T(8,128)(2,1)} %f_ref.3) | copy-start | bytes 3145732
  96.1 11.7 %collective-permute-start.27 = (bf16[512,256]{1,0:T(8,128)(2,1)S(1)}, bf16[512,256]{1,0:T(8,128)(2,1)S(1)}, u32[]{:S(2)}, u32[]{:S(2)}) collective-permute-start(bf16[512,256]{1,0:T(8,128)(2,1)S(1)} %get-tuple-element.38), channel_id=1, source_target_pairs={{0,1},{1,2},{2,3},{3,0},{4,5},{5,6},{6,7},{7,4},{8,9},{9,10},{10,1... | collective-permute-start | bytes 786440 | tf_op jit(solution)/shard_map/ppermute | solution.py:327
  100.8 7.0 %collective-permute-start.26 = (bf16[512,256]{1,0:T(8,128)(2,1)S(1)}, bf16[512,256]{1,0:T(8,128)(2,1)S(1)}, u32[]{:S(2)}, u32[]{:S(2)}) collective-permute-start(bf16[512,256]{1,0:T(8,128)(2,1)S(1)} %get-tuple-element.37), channel_id=1, source_target_pairs={{0,3},{1,0},{2,1},{3,2},{4,7},{5,4},{6,5},{7,6},{8,11},{9,8},{10,9... | collective-permute-start | bytes 786440 | tf_op jit(solution)/shard_map/ppermute | solution.py:327

commit v6 on v3

--- a/solution.py
+++ b/solution.py
@@ -61,10 +61,10 @@
                 both[at] = part
             else:
                 both[at] += part
-    for at in range(2):
-        out = slice(at * half, (at + 1) * half)
-        keep[out, :] = both[at, pl.ds(pl.multiple_of(core * half, half), half), :]
-        send[out, :] = both[at, pl.ds(pl.multiple_of((1 - core) * half, half), half), :]
+    for out, side in ((keep, core), (send, 1 - core)):
+        cut = pl.ds(pl.multiple_of(side * half, half), half)
+        for at in range(2):
+            out[at * half : (at + 1) * half, :] = both[at, cut, :]
 
 
 def project(k, v, e, f):
@@ -83,7 +83,7 @@
             pltpu.VMEM((2, KP, width), F32),
             pltpu.SemaphoreType.DMA((4, 4)),
         ],
-        compiler_params=pltpu.CompilerParams(vmem_limit_bytes=58 << 20),
+        compiler_params=pltpu.CompilerParams(vmem_limit_bytes=52 << 20),
         cost_estimate=cost(4 * tokens * width * KP, 6 << 20),
         name="project",
     )(k, v, e, f)
@@ -94,19 +94,8 @@
     out[...] = jnp.broadcast_to(total.astype(out.dtype), out.shape)
 
 
-def swap(value, axis):
-    size = lax.axis_size(axis)
-    return lax.ppermute(value, axis, [(i, (i + 1) % size) for i in range(size)])
-
-
-def total_over_seq(keep, send, wire):
-    chips = ("seq_0", "seq_1")
-    size = lax.axis_size(chips)
-    rows, width = keep.shape
-    part = keep + swap(send, "seq_2").astype(F32)
-    part = part.astype(wire).reshape(size, rows // size, width)
-    got = lax.all_to_all(part, chips, 0, 0, tiled=True)
-    copies = pl.pallas_call(
+def sum_copies(got):
+    return pl.pallas_call(
         sum_copies_kernel,
         in_specs=[VM],
         out_specs=VM,
@@ -115,8 +104,22 @@
         cost_estimate=cost(1 << 20, 1 << 20),
         name="sum_copies",
     )(got)
-    own = lax.all_to_all(copies, chips, 0, 0, tiled=True).reshape(rows, width)
-    return own, swap(own, "seq_2")
+
+
+def swap(value):
+    return lax.ppermute(value, "seq_2", [(0, 1), (1, 0)])
+
+
+def total_over_seq(keep, send, wire):
+    chips = ("seq_0", "seq_1")
+    size = lax.axis_size(chips)
+    rows, width = keep.shape
+    part = (keep + swap(send).astype(F32)).astype(wire)
+    got = lax.all_to_all(
+        part.reshape(size, rows // size, width), chips, 0, 0, tiled=True
+    )
+    own = lax.all_to_all(sum_copies(got), chips, 0, 0, tiled=True).reshape(rows, width)
+    return own, swap(own)
 
 
 def attend_kernel(q_ref, g_ref, own, other, dq_ref, keep, send, sum_k, sum_v):
@@ -207,26 +210,42 @@
     )(q, g, *pieces)
 
 
-def mixer_part_kernel(steps, k_ref, v_ref, own, other, *refs):
-    extra, (de, df) = refs[:-2], refs[-2:]
+def unpack_kernel(own, other, dpk, dpv):
     half = KP // 2
     core = lax.axis_index("seq_2")
+    for piece, side in ((own, core), (other, 1 - core)):
+        cut = pl.ds(pl.multiple_of(side * half, half), half)
+        dpk[cut, :] = piece[:half, :]
+        dpv[cut, :] = piece[half:, :]
+
+
+def unpack(own, other):
+    return pl.pallas_call(
+        unpack_kernel,
+        in_specs=[VM] * 2,
+        out_specs=[VM] * 2,
+        out_shape=[shape_of(*own.shape, BF)] * 2,
+        compiler_params=pltpu.CompilerParams(vmem_limit_bytes=4 << 20),
+        cost_estimate=cost(1 << 20, 1 << 20),
+        name="unpack",
+    )(own, other)
+
+
+def mixer_part_kernel(steps, k_ref, v_ref, dpk, dpv, *refs):
+    extra, (de, df) = refs[:-2], refs[-2:]
     size = lax.axis_size(ACROSS)
     rows = de.shape[0]
-    for at, (data, out) in enumerate(((k_ref, de), (v_ref, df))):
+    for at, (data, grad, out) in enumerate(((k_ref, dpk, de), (v_ref, dpv, df))):
         to = lax.rem(lax.axis_index(ACROSS) + steps[at], size)
-        block = data[pl.ds(pl.multiple_of(to * rows, rows), rows), :]
-        for piece, side in ((own, core), (other, 1 - core)):
-            part = lax.dot_general(
-                block,
-                piece[at * half : (at + 1) * half, :],
-                NT,
-                preferred_element_type=F32,
-            )
-            cols = pl.ds(pl.multiple_of(side * half, half), half)
-            if extra:
-                part += extra[at][:, cols].astype(F32)
-            out[:, cols] = part.astype(out.dtype)
+        part = lax.dot_general(
+            data[pl.ds(pl.multiple_of(to * rows, rows), rows), :],
+            grad[...],
+            NT,
+            preferred_element_type=F32,
+        )
+        if extra:
+            part += extra[at][...].astype(F32)
+        out[...] = part.astype(out.dtype)
 
 
 def mixer_part(steps, k, v, pieces, kind, *extra):
@@ -243,16 +262,7 @@
     )(k, v, *pieces, *extra)
 
 
-def input_grads_kernel(e_ref, f_ref, own, other, dk, dv, dpk, dpv):
-    @pl.when(pl.program_id(0) == 0)
-    def _():
-        half = KP // 2
-        core = lax.axis_index("seq_2")
-        for piece, at in ((own, core), (other, 1 - core)):
-            out = pl.ds(pl.multiple_of(at * half, half), half)
-            dpk[out, :] = piece[:half, :]
-            dpv[out, :] = piece[half:, :]
-
+def input_grads_kernel(e_ref, f_ref, dpk, dpv, dk, dv):
     dk[...] = jnp.dot(e_ref[...], dpk[...], preferred_element_type=F32).astype(BF)
     dv[...] = jnp.dot(f_ref[...], dpv[...], preferred_element_type=F32).astype(BF)
 
@@ -268,7 +278,6 @@
         in_specs=[thin, thin, VM, VM],
         out_specs=[wide, wide],
         out_shape=[shape_of(tokens, width, BF)] * 2,
-        scratch_shapes=[pltpu.VMEM((KP, width), BF)] * 2,
         compiler_params=pltpu.CompilerParams(vmem_limit_bytes=16 << 20),
         cost_estimate=cost(4 * tokens * width * KP, 6 << 20),
         name="input_grads",
@@ -301,7 +310,7 @@
     keep, send = project(k, v, key_mixer, value_mixer)
     pieces = total_over_seq(keep, send, F32)
     query_grad, keep, send = attend(q, g, pieces)
-    pieces = total_over_seq(keep, send, BF)
+    pieces = unpack(*total_over_seq(keep, send, BF))
     mixer_e, mixer_f = mixer_grads(k, v, pieces)
     key_grad, value_grad = input_grads(key_mixer, value_mixer, pieces)
     return (query_grad[None], key_grad[None], value_grad[None], mixer_e, mixer_f)

time: 112 us -> 109 us (0.973)
  the two profiles are of different devices: /device:TPU:6 before, /device:TPU:0 now
where the time goes in v6:
time: 109 us
  blocking collectives  55.6 us (51%)
  Pallas kernels  25.1 us (23%)
  waiting for transfers between devices  15.8 us (14%)
  starting transfers between devices  9.94 us (9%)
  other arithmetic  1.89 us (2%)
    all_to_all x2, blocking collectives, total_over_seq(): lax.all_to_all(part.reshape(size, rows // size, width), chips, 0, 0, tile...  32 us
    all_to_all x2, blocking collectives, total_over_seq(): lax.all_to_all(sum_copies(got), chips, 0, 0, tiled=True)  23.6 us
    pallas_call x1, Pallas kernels, attend(): pl.pallas_call(attend_kernel, grid=(tokens // rows,), in_specs=[wide, wid...  16.6 us
    ppermute x6, starting transfers between devices, along(): return lax.ppermute(value, ACROSS, pairs)  9.71 us
    ppermute x6, waiting for transfers between devices, along(): return lax.ppermute(value, ACROSS, pairs)  9.47 us
    ppermute x4, waiting for transfers between devices, swap(): return lax.ppermute(value, 'seq_2', [(0, 1), (1, 0)])  6.36 us
    pallas_call x1, Pallas kernels, project(): pl.pallas_call(project_kernel, in_specs=[hbm] * 4, out_specs=[VM] * 2, ou...  3.56 us
    pallas_call x1, Pallas kernels, input_grads(): pl.pallas_call(input_grads_kernel, grid=(tokens // rows,), in_specs=[thin...  3.01 us
  transfers between devices with their start and end apart: 10, of which 8 were waited for; matrix products, arithmetic and copies ran while one was open for 1% of the time, Pallas kernels for 4%

profile of v6, /device:TPU:0, one launch (start us, length us, event | category | flops | bytes accessed | tf_op | source)
XLA Modules:
  0.0 109.2 jit_solution(15413005830883396416)
XLA Ops:
  0.6 0.0 copy-start.5
  0.6 3.6 %project.1 = (f32[256,512]{1,0:T(8,128)S(1)}, f32[256,512]{1,0:T(8,128)S(1)}) custom-call(bf16[2048,512]{1,0:T(8,128)(2,1)} %bitcast.11, bf16[2048,512]{1,0:T(8,128)(2,1)} %bitcast.16, bf16[2048,256]{1,0:T(8,128)(2,1)} %e_ref.3, bf16[2048,256]{1,0:T(8,128)(2,1)} %f_ref.3), custom_call_target="tpu_custom_call" | custom-call | flops 1073741824 | bytes 6291456 | tf_op jit(solution)/shard_map/project/pallas_call | solution.py:73
  4.2 0.0 copy-start.4
  4.2 0.1 collective-permute-start
  4.3 1.9 %collective-permute-done = f32[256,512]{1,0:T(8,128)S(1)} collective-permute-done((f32[256,512]{1,0:T(8,128)S(1)}, f32[256,512]{1,0:T(8,128)S(1)}, u32[]{:S(2)}, u32[]{:S(2)}) %collective-permute-start) | collective-permute-done | bytes 524320 | tf_op jit(solution)/shard_map/ppermute | solution.py:110
  6.2 0.1 add.18
  6.3 19.8 %all_to_all.20.got = f32[16,16,512]{2,1,0:T(8,128)S(1)} all-to-all(f32[16,16,512]{2,1,0:T(8,128)S(1)} %bitcast.27), channel_id=1, replica_groups=mesh['seq_0'=4,'seq_1'=4,'seq_2'=2,'head'=2,'rep'=2] {'seq_0','seq_1'}, dimensions={0} | all-to-all | bytes 1048576 | tf_op jit(solution)/shard_map/all_to_all | solution.py:118
  26.1 11.7 %all_to_all.21 = bf16[16,16,512]{2,1,0:T(8,128)(2,1)S(1)} all-to-all(bf16[16,16,512]{2,1,0:T(8,128)(2,1)S(1)} %sum_copies.2), channel_id=1, replica_groups=mesh['seq_0'=4,'seq_1'=4,'seq_2'=2,'head'=2,'rep'=2] {'seq_0','seq_1'}, dimensions={0} | all-to-all | bytes 524288 | tf_op jit(solution)/shard_map/all_to_all | solution.py:121
  37.8 0.0 collective-permute-start.1
  37.8 1.5 %collective-permute-done.1.other = bf16[256,512]{1,0:T(8,128)(2,1)S(1)} collective-permute-done((bf16[256,512]{1,0:T(8,128)(2,1)S(1)}, bf16[256,512]{1,0:T(8,128)(2,1)S(1)}, u32[]{:S(2)}, u32[]{:S(2)}) %collective-permute-start.1) | collective-permute-done | bytes 262176 | tf_op jit(solution)/shard_map/ppermute | solution.py:110
  39.3 0.0 copy-done.5
  39.4 0.0 copy-done.4
  39.4 0.0 copy-start.1
  39.4 16.6 %attend.1 = (bf16[2048,512]{1,0:T(8,128)(2,1)}, f32[256,512]{1,0:T(8,128)S(1)}, bf16[256,512]{1,0:T(8,128)(2,1)S(1)}) custom-call(bf16[2048,512]{1,0:T(8,128)(2,1)S(1)} %bitcast.25, bf16[2048,512]{1,0:T(8,128)(2,1)S(1)} %bitcast.26, bf16[256,512]{1,0:T(8,128)(2,1)S(1)} %bitcast.24, bf16[256,512]{1,0:T(8,128)(2,1)S(1)} %collective-permute-done.1.other), custom_call_target="tpu_custom_call" | custom-call | flops 4294967296 | bytes 8388608 | tf_op jit(solution)/shard_map/attend/pallas_call | solution.py:196
  55.9 0.0 copy-start
  55.9 0.1 collective-permute-start.2
  56.0 1.4 %collective-permute-done.2 = bf16[256,512]{1,0:T(8,128)(2,1)S(1)} collective-permute-done((bf16[256,512]{1,0:T(8,128)(2,1)S(1)}, bf16[256,512]{1,0:T(8,128)(2,1)S(1)}, u32[]{:S(2)}, u32[]{:S(2)}) %collective-permute-start.2) | collective-permute-done | bytes 262176 | tf_op jit(solution)/shard_map/ppermute | solution.py:110
  57.4 0.1 add_convert_fusion
  57.5 12.3 %all_to_all.22.got = bf16[16,16,512]{2,1,0:T(8,128)(2,1)S(1)} all-to-all(bf16[16,16,512]{2,1,0:T(8,128)(2,1)S(1)} %bitcast.28), channel_id=1, replica_groups=mesh['seq_0'=4,'seq_1'=4,'seq_2'=2,'head'=2,'rep'=2] {'seq_0','seq_1'}, dimensions={0} | all-to-all | bytes 524288 | tf_op jit(solution)/shard_map/all_to_all | solution.py:118
  69.9 11.9 %all_to_all.23 = bf16[16,16,512]{2,1,0:T(8,128)(2,1)S(1)} all-to-all(bf16[16,16,512]{2,1,0:T(8,128)(2,1)S(1)} %sum_copies.3), channel_id=1, replica_groups=mesh['seq_0'=4,'seq_1'=4,'seq_2'=2,'head'=2,'rep'=2] {'seq_0','seq_1'}, dimensions={0} | all-to-all | bytes 524288 | tf_op jit(solution)/shard_map/all_to_all | solution.py:121
  81.8 0.0 collective-permute-start.3
  81.8 1.5 %collective-permute-done.3.other = bf16[256,512]{1,0:T(8,128)(2,1)S(1)} collective-permute-done((bf16[256,512]{1,0:T(8,128)(2,1)S(1)}, bf16[256,512]{1,0:T(8,128)(2,1)S(1)}, u32[]{:S(2)}, u32[]{:S(2)}) %collective-permute-start.3) | collective-permute-done | bytes 262176 | tf_op jit(solution)/shard_map/ppermute | solution.py:110
  83.3 0.0 copy-done.1
  83.4 0.0 copy-done
  83.4 0.5 mixer_part.6
  83.8 1.6 %collective-permute-start.5 = (bf16[512,256]{1,0:T(8,128)(2,1)S(1)}, bf16[512,256]{1,0:T(8,128)(2,1)S(1)}, u32[]{:S(2)}, u32[]{:S(2)}) collective-permute-start(bf16[512,256]{1,0:T(8,128)(2,1)S(1)} %get-tuple-element.33), channel_id=1, source_target_pairs={{0,1},{1,2},{2,3},{3,0},{4,5},{5,6},{6,7},{7,4},{8,9},{9,10},{10,1... | collective-permute-start | bytes 786440 | tf_op jit(solution)/shard_map/ppermute | solution.py:290
  85.4 1.7 %collective-permute-start.6 = (bf16[512,256]{1,0:T(8,128)(2,1)S(1)}, bf16[512,256]{1,0:T(8,128)(2,1)S(1)}, u32[]{:S(2)}, u32[]{:S(2)}) collective-permute-start(bf16[512,256]{1,0:T(8,128)(2,1)S(1)} %get-tuple-element.34), channel_id=1, source_target_pairs={{0,3},{1,0},{2,1},{3,2},{4,7},{5,4},{6,5},{7,6},{8,11},{9,8},{10,9... | collective-permute-start | bytes 786440 | tf_op jit(solution)/shard_map/ppermute | solution.py:290
  87.1 0.5 mixer_part.5
  87.6 1.6 %collective-permute-start.4 = (bf16[512,256]{1,0:T(8,128)(2,1)S(1)}, bf16[512,256]{1,0:T(8,128)(2,1)S(1)}, u32[]{:S(2)}, u32[]{:S(2)}) collective-permute-start(bf16[512,256]{1,0:T(8,128)(2,1)S(1)} %get-tuple-element.32), channel_id=1, source_target_pairs={{0,3},{1,0},{2,1},{3,2},{4,7},{5,4},{6,5},{7,6},{8,11},{9,8},{10,9... | collective-permute-start | bytes 786440 | tf_op jit(solution)/shard_map/ppermute | solution.py:290
  89.2 4.2 %collective-permute-done.5.refs_0_ = bf16[512,256]{1,0:T(8,128)(2,1)S(1)} collective-permute-done((bf16[512,256]{1,0:T(8,128)(2,1)S(1)}, bf16[512,256]{1,0:T(8,128)(2,1)S(1)}, u32[]{:S(2)}, u32[]{:S(2)}) %collective-permute-start.5) | collective-permute-done | bytes 262176 | tf_op jit(solution)/shard_map/ppermute | solution.py:290
  93.5 1.1 %collective-permute-done.6.refs_1_ = bf16[512,256]{1,0:T(8,128)(2,1)S(1)} collective-permute-done((bf16[512,256]{1,0:T(8,128)(2,1)S(1)}, bf16[512,256]{1,0:T(8,128)(2,1)S(1)}, u32[]{:S(2)}, u32[]{:S(2)}) %collective-permute-start.6) | collective-permute-done | bytes 262176 | tf_op jit(solution)/shard_map/ppermute | solution.py:290
  94.6 0.5 mixer_part.7
  95.1 1.6 %collective-permute-start.7 = (bf16[512,256]{1,0:T(8,128)(2,1)S(1)}, bf16[512,256]{1,0:T(8,128)(2,1)S(1)}, u32[]{:S(2)}, u32[]{:S(2)}) collective-permute-start(bf16[512,256]{1,0:T(8,128)(2,1)S(1)} %get-tuple-element.35), channel_id=1, source_target_pairs={{0,1},{1,2},{2,3},{3,0},{4,5},{5,6},{6,7},{7,4},{8,9},{9,10},{10,1... | collective-permute-start | bytes 786440 | tf_op jit(solution)/shard_map/ppermute | solution.py:290
  96.6 0.0 copy-start.2
  96.6 0.0 copy-start.3
  96.6 1.2 %collective-permute-start.9 = (bf16[512,256]{1,0:T(8,128)(2,1)S(1)}, bf16[512,256]{1,0:T(8,128)(2,1)S(1)}, u32[]{:S(2)}, u32[]{:S(2)}) collective-permute-start(bf16[512,256]{1,0:T(8,128)(2,1)S(1)} %get-tuple-element.38), channel_id=1, source_target_pairs={{0,1},{1,2},{2,3},{3,0},{4,5},{5,6},{6,7},{7,4},{8,9},{9,10},{10,1... | collective-permute-start | bytes 786440 | tf_op jit(solution)/shard_map/ppermute | solution.py:290
  97.8 0.5 mixer_part.4
  98.3 0.0 copy-done.2
  98.3 0.0 copy-done.3
  98.3 3.0 %input_grads.1 = (bf16[2048,512]{1,0:T(8,128)(2,1)}, bf16[2048,512]{1,0:T(8,128)(2,1)}) custom-call(bf16[2048,256]{1,0:T(8,128)(2,1)S(1)} %copy-done.2, bf16[2048,256]{1,0:T(8,128)(2,1)S(1)} %copy-done.3, bf16[256,512]{1,0:T(8,128)(2,1)S(1)} %get-tuple-element.27.dpk, bf16[256,512]{1,0:T(8,128)(2,1)S(1)} %get-tuple-element.28.dpv), custom_call_target="tpu_custom_call" | custom-call | flops 1073741824 | bytes 6291456 | tf_op jit(solution)/shard_map/input_grads/pallas_call | solution.py:275
  101.3 2.0 %collective-permute-start.8 = (bf16[512,256]{1,0:T(8,128)(2,1)S(1)}, bf16[512,256]{1,0:T(8,128)(2,1)S(1)}, u32[]{:S(2)}, u32[]{:S(2)}) collective-permute-start(bf16[512,256]{1,0:T(8,128)(2,1)S(1)} %get-tuple-element.37), channel_id=1, source_target_pairs={{0,3},{1,0},{2,1},{3,2},{4,7},{5,4},{6,5},{7,6},{8,11},{9,8},{10,9... | collective-permute-start | bytes 786440 | tf_op jit(solution)/shard_map/ppermute | solution.py:290
  103.4 0.0 collective-permute-done.4
  103.4 2.2 %collective-permute-done.7 = bf16[512,256]{1,0:T(8,128)(2,1)S(1)} collective-permute-done((bf16[512,256]{1,0:T(8,128)(2,1)S(1)}, bf16[512,256]{1,0:T(8,128)(2,1)S(1)}, u32[]{:S(2)}, u32[]{:S(2)}) %collective-permute-start.7) | collective-permute-done | bytes 262176 | tf_op jit(solution)/shard_map/ppermute | solution.py:290
  105.5 0.9 add_add_fusion.1
  106.4 2.0 %collective-permute-done.9 = bf16[512,256]{1,0:T(8,128)(2,1)S(1)} collective-permute-done((bf16[512,256]{1,0:T(8,128)(2,1)S(1)}, bf16[512,256]{1,0:T(8,128)(2,1)S(1)}, u32[]{:S(2)}, u32[]{:S(2)}) %collective-permute-start.9) | collective-permute-done | bytes 262176 | tf_op jit(solution)/shard_map/ppermute | solution.py:290
  108.3 0.0 collective-permute-done.8
  108.3 0.9 add_add_fusion
  (3 shorter events, 0.1 us)
Async XLA Ops:
  0.6 38.7 %copy-start.5 = (bf16[1,2048,512]{2,1,0:T(8,128)(2,1)S(1)}, bf16[1,2048,512]{2,1,0:T(8,128)(2,1)}, u32[]{:S(2)}) copy-start(bf16[1,2048,512]{2,1,0:T(8,128)(2,1)} %param.9) | copy-start | bytes 6291460
  4.2 35.1 %copy-start.4 = (bf16[1,2048,512]{2,1,0:T(8,128)(2,1)S(1)}, bf16[1,2048,512]{2,1,0:T(8,128)(2,1)}, u32[]{:S(2)}) copy-start(bf16[1,2048,512]{2,1,0:T(8,128)(2,1)} %param.6) | copy-start | bytes 6291460
  4.2 2.0 %collective-permute-start = (f32[256,512]{1,0:T(8,128)S(1)}, f32[256,512]{1,0:T(8,128)S(1)}, u32[]{:S(2)}, u32[]{:S(2)}) collective-permute-start(f32[256,512]{1,0:T(8,128)S(1)} %get-tuple-element.23), channel_id=1, source_target_pairs={{0,4},{4,0},{1,5},{5,1},{2,6},{6,2},{3,7},{7,3},{8,12},{12,8},{9,1... | collective-permute-start | bytes 1572872 | tf_op jit(solution)/shard_map/ppermute | solution.py:110
  37.8 1.5 %collective-permute-start.1 = (bf16[256,512]{1,0:T(8,128)(2,1)S(1)}, bf16[256,512]{1,0:T(8,128)(2,1)S(1)}, u32[]{:S(2)}, u32[]{:S(2)}) collective-permute-start(bf16[256,512]{1,0:T(8,128)(2,1)S(1)} %bitcast.23), channel_id=1, source_target_pairs={{0,4},{4,0},{1,5},{5,1},{2,6},{6,2},{3,7},{7,3},{8,12},{12,8},{9,1... | collective-permute-start | bytes 786440 | tf_op jit(solution)/shard_map/ppermute | solution.py:110
  39.4 44.0 %copy-start.1 = (bf16[1,2048,512]{2,1,0:T(8,128)(2,1)S(1)}, bf16[1,2048,512]{2,1,0:T(8,128)(2,1)}, u32[]{:S(2)}) copy-start(bf16[1,2048,512]{2,1,0:T(8,128)(2,1)} %param.8) | copy-start | bytes 6291460
  55.9 27.5 %copy-start = (bf16[1,2048,512]{2,1,0:T(8,128)(2,1)S(1)}, bf16[1,2048,512]{2,1,0:T(8,128)(2,1)}, u32[]{:S(2)}) copy-start(bf16[1,2048,512]{2,1,0:T(8,128)(2,1)} %param.7) | copy-start | bytes 6291460
  55.9 1.5 %collective-permute-start.2 = (bf16[256,512]{1,0:T(8,128)(2,1)S(1)}, bf16[256,512]{1,0:T(8,128)(2,1)S(1)}, u32[]{:S(2)}, u32[]{:S(2)}) collective-permute-start(bf16[256,512]{1,0:T(8,128)(2,1)S(1)} %get-tuple-element.26), channel_id=1, source_target_pairs={{0,4},{4,0},{1,5},{5,1},{2,6},{6,2},{3,7},{7,3},{8,12},{12,8},{9,1... | collective-permute-start | bytes 786440 | tf_op jit(solution)/shard_map/ppermute | solution.py:110
  81.8 1.5 %collective-permute-start.3 = (bf16[256,512]{1,0:T(8,128)(2,1)S(1)}, bf16[256,512]{1,0:T(8,128)(2,1)S(1)}, u32[]{:S(2)}, u32[]{:S(2)}) collective-permute-start(bf16[256,512]{1,0:T(8,128)(2,1)S(1)} %bitcast.21), channel_id=1, source_target_pairs={{0,4},{4,0},{1,5},{5,1},{2,6},{6,2},{3,7},{7,3},{8,12},{12,8},{9,1... | collective-permute-start | bytes 786440 | tf_op jit(solution)/shard_map/ppermute | solution.py:110
  83.8 9.6 %collective-permute-start.5 = (bf16[512,256]{1,0:T(8,128)(2,1)S(1)}, bf16[512,256]{1,0:T(8,128)(2,1)S(1)}, u32[]{:S(2)}, u32[]{:S(2)}) collective-permute-start(bf16[512,256]{1,0:T(8,128)(2,1)S(1)} %get-tuple-element.33), channel_id=1, source_target_pairs={{0,1},{1,2},{2,3},{3,0},{4,5},{5,6},{6,7},{7,4},{8,9},{9,10},{10,1... | collective-permute-start | bytes 786440 | tf_op jit(solution)/shard_map/ppermute | solution.py:290
  85.4 9.2 %collective-permute-start.6 = (bf16[512,256]{1,0:T(8,128)(2,1)S(1)}, bf16[512,256]{1,0:T(8,128)(2,1)S(1)}, u32[]{:S(2)}, u32[]{:S(2)}) collective-permute-start(bf16[512,256]{1,0:T(8,128)(2,1)S(1)} %get-tuple-element.34), channel_id=1, source_target_pairs={{0,3},{1,0},{2,1},{3,2},{4,7},{5,4},{6,5},{7,6},{8,11},{9,8},{10,9... | collective-permute-start | bytes 786440 | tf_op jit(solution)/shard_map/ppermute | solution.py:290
  87.6 15.7 %collective-permute-start.4 = (bf16[512,256]{1,0:T(8,128)(2,1)S(1)}, bf16[512,256]{1,0:T(8,128)(2,1)S(1)}, u32[]{:S(2)}, u32[]{:S(2)}) collective-permute-start(bf16[512,256]{1,0:T(8,128)(2,1)S(1)} %get-tuple-element.32), channel_id=1, source_target_pairs={{0,3},{1,0},{2,1},{3,2},{4,7},{5,4},{6,5},{7,6},{8,11},{9,8},{10,9... | collective-permute-start | bytes 786440 | tf_op jit(solution)/shard_map/ppermute | solution.py:290
  95.1 10.5 %collective-permute-start.7 = (bf16[512,256]{1,0:T(8,128)(2,1)S(1)}, bf16[512,256]{1,0:T(8,128)(2,1)S(1)}, u32[]{:S(2)}, u32[]{:S(2)}) collective-permute-start(bf16[512,256]{1,0:T(8,128)(2,1)S(1)} %get-tuple-element.35), channel_id=1, source_target_pairs={{0,1},{1,2},{2,3},{3,0},{4,5},{5,6},{6,7},{7,4},{8,9},{9,10},{10,1... | collective-permute-start | bytes 786440 | tf_op jit(solution)/shard_map/ppermute | solution.py:290
  96.6 1.7 %copy-start.2 = (bf16[2048,256]{1,0:T(8,128)(2,1)S(1)}, bf16[2048,256]{1,0:T(8,128)(2,1)}, u32[]{:S(2)}) copy-start(bf16[2048,256]{1,0:T(8,128)(2,1)} %e_ref.3) | copy-start | bytes 3145732
  96.6 1.7 %copy-start.3 = (bf16[2048,256]{1,0:T(8,128)(2,1)S(1)}, bf16[2048,256]{1,0:T(8,128)(2,1)}, u32[]{:S(2)}) copy-start(bf16[2048,256]{1,0:T(8,128)(2,1)} %f_ref.3) | copy-start | bytes 3145732
  96.6 11.7 %collective-permute-start.9 = (bf16[512,256]{1,0:T(8,128)(2,1)S(1)}, bf16[512,256]{1,0:T(8,128)(2,1)S(1)}, u32[]{:S(2)}, u32[]{:S(2)}) collective-permute-start(bf16[512,256]{1,0:T(8,128)(2,1)S(1)} %get-tuple-element.38), channel_id=1, source_target_pairs={{0,1},{1,2},{2,3},{3,0},{4,5},{5,6},{6,7},{7,4},{8,9},{9,10},{10,1... | collective-permute-start | bytes 786440 | tf_op jit(solution)/shard_map/ppermute | solution.py:290
  101.3 7.0 %collective-permute-start.8 = (bf16[512,256]{1,0:T(8,128)(2,1)S(1)}, bf16[512,256]{1,0:T(8,128)(2,1)S(1)}, u32[]{:S(2)}, u32[]{:S(2)}) collective-permute-start(bf16[512,256]{1,0:T(8,128)(2,1)S(1)} %get-tuple-element.37), channel_id=1, source_target_pairs={{0,3},{1,0},{2,1},{3,2},{4,7},{5,4},{6,5},{7,6},{8,11},{9,8},{10,9... | collective-permute-start | bytes 786440 | tf_op jit(solution)/shard_map/ppermute | solution.py:290

commit v7 on v6

--- a/solution.py
+++ b/solution.py
@@ -127,7 +127,7 @@
     width = q_ref.shape[1]
     half = KP // 2
     scale = 1.0 / DH**0.5
-    heads = 4
+    heads = 2
     lanes = heads * DH
 
     @pl.when(step == 0)
@@ -149,8 +149,8 @@
             out = jnp.where(head_of == h, total[h * KP : (h + 1) * KP], out)
         return out
 
-    def group(j, carry):
-        cols = pl.ds(pl.multiple_of(j * lanes, lanes), lanes)
+    def group(j):
+        cols = slice(j * lanes, (j + 1) * lanes)
         q = q_ref[:, cols]
         g = g_ref[:, cols]
         pk = stacked(jnp.concatenate([own[:half, cols], other[:half, cols]], axis=0))
@@ -176,9 +176,9 @@
         dq_ref[:, cols] = lax.dot_general(
             ds, pk, TN, preferred_element_type=F32
         ).astype(BF)
-        return carry
-
-    lax.fori_loop(0, width // lanes, group, 0)
+
+    for j in range(width // lanes):
+        group(j)
 
     @pl.when(step == pl.num_programs(0) - 1)
     def _():
@@ -190,7 +190,7 @@
 
 def attend(q, g, pieces):
     tokens, width = q.shape
-    rows = 1024
+    rows = 512
     wide = pl.BlockSpec((rows, width), lambda i: (i, 0))
     still = pl.BlockSpec((KP, width), lambda i: (0, 0))
     return pl.pallas_call(
@@ -284,6 +284,11 @@
     )(e, f, *pieces)
 
 
+def mixer_sum_kernel(own_e, down_e, up_e, own_f, down_f, up_f, de, df):
+    for own, down, up, out in ((own_e, down_e, up_e, de), (own_f, down_f, up_f, df)):
+        out[...] = own[...] + (down[...].astype(F32) + up[...].astype(F32))
+
+
 def along(value, step):
     size = lax.axis_size(ACROSS)
     pairs = [(i, (i + step) % size) for i in range(size)]
@@ -298,10 +303,15 @@
     own_e, own_f = mixer_part((0, 0), k, v, pieces, F32)
     up_e, down_f = mixer_part((1, 3), k, v, pieces, BF, far_e, far_f)
     up_e, down_f = along(up_e, 1), along(down_f, -1)
-    return (
-        own_e + (down_e.astype(F32) + up_e.astype(F32)),
-        own_f + (down_f.astype(F32) + up_f.astype(F32)),
-    )
+    return pl.pallas_call(
+        mixer_sum_kernel,
+        in_specs=[VM] * 6,
+        out_specs=[VM] * 2,
+        out_shape=[shape_of(*own_e.shape, F32)] * 2,
+        compiler_params=pltpu.CompilerParams(vmem_limit_bytes=8 << 20),
+        cost_estimate=cost(1 << 20, 3 << 20),
+        name="mixer_sum",
+    )(own_e, down_e, up_e, own_f, down_f, up_f)
 
 
 def on_device(queries, key_states, value_states, out_grad, key_mixer, value_mixer):

time: 109 us -> 106 us (0.972)
  the two profiles are of different devices: /device:TPU:0 before, /device:TPU:3 now
where the time goes in v7:
time: 106 us; the launch traced here: 105 us
  blocking collectives  50.4 us (48%)
  Pallas kernels  26.1 us (25%)
  waiting for transfers between devices  15.2 us (14%)
  starting transfers between devices  11.6 us (11%)
    all_to_all x2, blocking collectives, total_over_seq(): lax.all_to_all(part.reshape(size, rows // size, width), chips, 0, 0, tile...  28.7 us
    all_to_all x2, blocking collectives, total_over_seq(): lax.all_to_all(sum_copies(got), chips, 0, 0, tiled=True)  21.7 us
    pallas_call x1, Pallas kernels, attend(): pl.pallas_call(attend_kernel, grid=(tokens // rows,), in_specs=[wide, wid...  16.5 us
    ppermute x6, waiting for transfers between devices, along(): return lax.ppermute(value, ACROSS, pairs)  10.2 us
    ppermute x4, starting transfers between devices, swap(): return lax.ppermute(value, 'seq_2', [(0, 1), (1, 0)])  7.01 us
    ppermute x4, waiting for transfers between devices, swap(): return lax.ppermute(value, 'seq_2', [(0, 1), (1, 0)])  5.02 us
    ppermute x6, starting transfers between devices, along(): return lax.ppermute(value, ACROSS, pairs)  4.6 us
    pallas_call x1, Pallas kernels, project(): pl.pallas_call(project_kernel, in_specs=[hbm] * 4, out_specs=[VM] * 2, ou...  3.56 us
  transfers between devices with their start and end apart: 10, of which 8 were waited for; matrix products, arithmetic and copies ran while one was open for 0% of the time, Pallas kernels for 4%

profile of v7, /device:TPU:3, one launch (start us, length us, event | category | flops | bytes accessed | tf_op | source)
XLA Modules:
  0.0 104.7 jit_solution(14891465264803397681)
XLA Ops:
  0.6 0.0 copy-start.5
  0.6 3.6 %project.1 = (f32[256,512]{1,0:T(8,128)S(1)}, f32[256,512]{1,0:T(8,128)S(1)}) custom-call(bf16[2048,512]{1,0:T(8,128)(2,1)} %bitcast.11, bf16[2048,512]{1,0:T(8,128)(2,1)} %bitcast.16, bf16[2048,256]{1,0:T(8,128)(2,1)} %e_ref.3, bf16[2048,256]{1,0:T(8,128)(2,1)} %f_ref.3), custom_call_target="tpu_custom_call" | custom-call | flops 1073741824 | bytes 6291456 | tf_op jit(solution)/shard_map/project/pallas_call | solution.py:73
  4.2 0.0 copy-start.4
  4.2 0.8 collective-permute-start
  5.0 1.5 %collective-permute-done = f32[256,512]{1,0:T(8,128)S(1)} collective-permute-done((f32[256,512]{1,0:T(8,128)S(1)}, f32[256,512]{1,0:T(8,128)S(1)}, u32[]{:S(2)}, u32[]{:S(2)}) %collective-permute-start) | collective-permute-done | bytes 524320 | tf_op jit(solution)/shard_map/ppermute | solution.py:110
  6.5 0.1 add.6
  6.6 17.9 %all_to_all.20.got = f32[16,16,512]{2,1,0:T(8,128)S(1)} all-to-all(f32[16,16,512]{2,1,0:T(8,128)S(1)} %bitcast.27), channel_id=1, replica_groups=mesh['seq_0'=4,'seq_1'=4,'seq_2'=2,'head'=2,'rep'=2] {'seq_0','seq_1'}, dimensions={0} | all-to-all | bytes 1048576 | tf_op jit(solution)/shard_map/all_to_all | solution.py:118
  24.6 10.8 %all_to_all.21 = bf16[16,16,512]{2,1,0:T(8,128)(2,1)S(1)} all-to-all(bf16[16,16,512]{2,1,0:T(8,128)(2,1)S(1)} %sum_copies.2), channel_id=1, replica_groups=mesh['seq_0'=4,'seq_1'=4,'seq_2'=2,'head'=2,'rep'=2] {'seq_0','seq_1'}, dimensions={0} | all-to-all | bytes 524288 | tf_op jit(solution)/shard_map/all_to_all | solution.py:121
  35.4 2.9 %collective-permute-start.1 = (bf16[256,512]{1,0:T(8,128)(2,1)S(1)}, bf16[256,512]{1,0:T(8,128)(2,1)S(1)}, u32[]{:S(2)}, u32[]{:S(2)}) collective-permute-start(bf16[256,512]{1,0:T(8,128)(2,1)S(1)} %bitcast.23), channel_id=1, source_target_pairs={{0,4},{4,0},{1,5},{5,1},{2,6},{6,2},{3,7},{7,3},{8,12},{12,8},{9,1... | collective-permute-start | bytes 786440 | tf_op jit(solution)/shard_map/ppermute | solution.py:110
  38.4 1.2 %collective-permute-done.1.other = bf16[256,512]{1,0:T(8,128)(2,1)S(1)} collective-permute-done((bf16[256,512]{1,0:T(8,128)(2,1)S(1)}, bf16[256,512]{1,0:T(8,128)(2,1)S(1)}, u32[]{:S(2)}, u32[]{:S(2)}) %collective-permute-start.1) | collective-permute-done | bytes 262176 | tf_op jit(solution)/shard_map/ppermute | solution.py:110
  39.5 0.0 copy-done.5
  39.5 0.0 copy-done.4
  39.5 0.0 copy-start.1
  39.5 16.5 %attend.1 = (bf16[2048,512]{1,0:T(8,128)(2,1)}, f32[256,512]{1,0:T(8,128)S(1)}, bf16[256,512]{1,0:T(8,128)(2,1)S(1)}) custom-call(bf16[2048,512]{1,0:T(8,128)(2,1)S(1)} %bitcast.25, bf16[2048,512]{1,0:T(8,128)(2,1)S(1)} %bitcast.26, bf16[256,512]{1,0:T(8,128)(2,1)S(1)} %bitcast.24, bf16[256,512]{1,0:T(8,128)(2,1)S(1)} %collective-permute-done.1.other), custom_call_target="tpu_custom_call" | custom-call | flops 4294967296 | bytes 8388608 | tf_op jit(solution)/shard_map/attend/pallas_call | solution.py:196
  56.0 0.0 copy-start
  56.0 0.4 collective-permute-start.2
  56.4 1.2 %collective-permute-done.2 = bf16[256,512]{1,0:T(8,128)(2,1)S(1)} collective-permute-done((bf16[256,512]{1,0:T(8,128)(2,1)S(1)}, bf16[256,512]{1,0:T(8,128)(2,1)S(1)}, u32[]{:S(2)}, u32[]{:S(2)}) %collective-permute-start.2) | collective-permute-done | bytes 262176 | tf_op jit(solution)/shard_map/ppermute | solution.py:110
  57.6 0.1 add_convert_fusion
  57.6 10.8 %all_to_all.22.got = bf16[16,16,512]{2,1,0:T(8,128)(2,1)S(1)} all-to-all(bf16[16,16,512]{2,1,0:T(8,128)(2,1)S(1)} %bitcast.28), channel_id=1, replica_groups=mesh['seq_0'=4,'seq_1'=4,'seq_2'=2,'head'=2,'rep'=2] {'seq_0','seq_1'}, dimensions={0} | all-to-all | bytes 524288 | tf_op jit(solution)/shard_map/all_to_all | solution.py:118
  68.4 10.9 %all_to_all.23 = bf16[16,16,512]{2,1,0:T(8,128)(2,1)S(1)} all-to-all(bf16[16,16,512]{2,1,0:T(8,128)(2,1)S(1)} %sum_copies.3), channel_id=1, replica_groups=mesh['seq_0'=4,'seq_1'=4,'seq_2'=2,'head'=2,'rep'=2] {'seq_0','seq_1'}, dimensions={0} | all-to-all | bytes 524288 | tf_op jit(solution)/shard_map/all_to_all | solution.py:121
  79.3 2.9 %collective-permute-start.3 = (bf16[256,512]{1,0:T(8,128)(2,1)S(1)}, bf16[256,512]{1,0:T(8,128)(2,1)S(1)}, u32[]{:S(2)}, u32[]{:S(2)}) collective-permute-start(bf16[256,512]{1,0:T(8,128)(2,1)S(1)} %bitcast.21), channel_id=1, source_target_pairs={{0,4},{4,0},{1,5},{5,1},{2,6},{6,2},{3,7},{7,3},{8,12},{12,8},{9,1... | collective-permute-start | bytes 786440 | tf_op jit(solution)/shard_map/ppermute | solution.py:110
  82.2 1.2 %collective-permute-done.3.other = bf16[256,512]{1,0:T(8,128)(2,1)S(1)} collective-permute-done((bf16[256,512]{1,0:T(8,128)(2,1)S(1)}, bf16[256,512]{1,0:T(8,128)(2,1)S(1)}, u32[]{:S(2)}, u32[]{:S(2)}) %collective-permute-start.3) | collective-permute-done | bytes 262176 | tf_op jit(solution)/shard_map/ppermute | solution.py:110
  83.5 0.0 copy-done.1
  83.5 0.0 copy-done
  83.5 0.5 mixer_part.6
  84.0 1.3 %collective-permute-start.5 = (bf16[512,256]{1,0:T(8,128)(2,1)S(1)}, bf16[512,256]{1,0:T(8,128)(2,1)S(1)}, u32[]{:S(2)}, u32[]{:S(2)}) collective-permute-start(bf16[512,256]{1,0:T(8,128)(2,1)S(1)} %get-tuple-element.35), channel_id=1, source_target_pairs={{0,1},{1,2},{2,3},{3,0},{4,5},{5,6},{6,7},{7,4},{8,9},{9,10},{10,1... | collective-permute-start | bytes 786440 | tf_op jit(solution)/shard_map/ppermute | solution.py:295
  85.2 0.3 collective-permute-start.6
  85.5 0.5 mixer_part.5
  86.0 1.5 %collective-permute-start.4 = (bf16[512,256]{1,0:T(8,128)(2,1)S(1)}, bf16[512,256]{1,0:T(8,128)(2,1)S(1)}, u32[]{:S(2)}, u32[]{:S(2)}) collective-permute-start(bf16[512,256]{1,0:T(8,128)(2,1)S(1)} %get-tuple-element.34), channel_id=1, source_target_pairs={{0,3},{1,0},{2,1},{3,2},{4,7},{5,4},{6,5},{7,6},{8,11},{9,8},{10,9... | collective-permute-start | bytes 786440 | tf_op jit(solution)/shard_map/ppermute | solution.py:295
  87.5 0.0 collective-permute-start.9
  87.5 4.0 %collective-permute-done.5.refs_0_ = bf16[512,256]{1,0:T(8,128)(2,1)S(1)} collective-permute-done((bf16[512,256]{1,0:T(8,128)(2,1)S(1)}, bf16[512,256]{1,0:T(8,128)(2,1)S(1)}, u32[]{:S(2)}, u32[]{:S(2)}) %collective-permute-start.5) | collective-permute-done | bytes 262176 | tf_op jit(solution)/shard_map/ppermute | solution.py:295
  91.5 0.9 collective-permute-done.6.refs_1_
  92.4 0.5 mixer_part.7
  92.9 1.0 collective-permute-start.7
  93.9 0.0 copy-start.2
  93.9 0.0 copy-start.3
  93.9 0.5 collective-permute-start.8
  94.5 0.5 mixer_part.4
  94.9 0.2 copy-done.2
  95.1 0.3 copy-done.3
  95.5 3.0 %input_grads.1 = (bf16[2048,512]{1,0:T(8,128)(2,1)}, bf16[2048,512]{1,0:T(8,128)(2,1)}) custom-call(bf16[2048,256]{1,0:T(8,128)(2,1)S(1)} %copy-done.2, bf16[2048,256]{1,0:T(8,128)(2,1)S(1)} %copy-done.3, bf16[256,512]{1,0:T(8,128)(2,1)S(1)} %get-tuple-element.29.dpk, bf16[256,512]{1,0:T(8,128)(2,1)S(1)} %get-tuple-element.30.dpv), custom_call_target="tpu_custom_call" | custom-call | flops 1073741824 | bytes 6291456 | tf_op jit(solution)/shard_map/input_grads/pallas_call | solution.py:275
  98.4 0.0 collective-permute-done.4.down_e
  98.4 0.0 collective-permute-done.9.up_f
  98.4 4.3 %collective-permute-done.7.up_e = bf16[512,256]{1,0:T(8,128)(2,1)S(1)} collective-permute-done((bf16[512,256]{1,0:T(8,128)(2,1)S(1)}, bf16[512,256]{1,0:T(8,128)(2,1)S(1)}, u32[]{:S(2)}, u32[]{:S(2)}) %collective-permute-start.7) | collective-permute-done | bytes 262176 | tf_op jit(solution)/shard_map/ppermute | solution.py:295
  102.8 0.9 collective-permute-done.8.down_f
  103.7 1.1 %mixer_sum.1 = (f32[512,256]{1,0:T(8,128)}, f32[512,256]{1,0:T(8,128)}) custom-call(f32[512,256]{1,0:T(8,128)S(1)} %get-tuple-element.33.own_e, bf16[512,256]{1,0:T(8,128)(2,1)S(1)} %collective-permute-done.4.down_e, bf16[512,256]{1,0:T(8,128)(2,1)S(1)} %collective-permute-done.7.up_e, f32[512,256]{1,0:T(8,128)S(1)} %get-tuple-element.38.own_f, ...), custom_call_target="tpu_custom_call" | custom-call | flops 1048576 | bytes 3145728 | tf_op jit(solution)/shard_map/mixer_sum/pallas_call | solution.py:306
  (3 shorter events, 0.1 us)
Async XLA Ops:
  0.6 38.9 %copy-start.5 = (bf16[1,2048,512]{2,1,0:T(8,128)(2,1)S(1)}, bf16[1,2048,512]{2,1,0:T(8,128)(2,1)}, u32[]{:S(2)}) copy-start(bf16[1,2048,512]{2,1,0:T(8,128)(2,1)} %param.9) | copy-start | bytes 6291460
  4.2 35.3 %copy-start.4 = (bf16[1,2048,512]{2,1,0:T(8,128)(2,1)S(1)}, bf16[1,2048,512]{2,1,0:T(8,128)(2,1)}, u32[]{:S(2)}) copy-start(bf16[1,2048,512]{2,1,0:T(8,128)(2,1)} %param.6) | copy-start | bytes 6291460
  4.2 2.3 %collective-permute-start = (f32[256,512]{1,0:T(8,128)S(1)}, f32[256,512]{1,0:T(8,128)S(1)}, u32[]{:S(2)}, u32[]{:S(2)}) collective-permute-start(f32[256,512]{1,0:T(8,128)S(1)} %get-tuple-element.25), channel_id=1, source_target_pairs={{0,4},{4,0},{1,5},{5,1},{2,6},{6,2},{3,7},{7,3},{8,12},{12,8},{9,1... | collective-permute-start | bytes 1572872 | tf_op jit(solution)/shard_map/ppermute | solution.py:110
  35.4 4.1 %collective-permute-start.1 = (bf16[256,512]{1,0:T(8,128)(2,1)S(1)}, bf16[256,512]{1,0:T(8,128)(2,1)S(1)}, u32[]{:S(2)}, u32[]{:S(2)}) collective-permute-start(bf16[256,512]{1,0:T(8,128)(2,1)S(1)} %bitcast.23), channel_id=1, source_target_pairs={{0,4},{4,0},{1,5},{5,1},{2,6},{6,2},{3,7},{7,3},{8,12},{12,8},{9,1... | collective-permute-start | bytes 786440 | tf_op jit(solution)/shard_map/ppermute | solution.py:110
  39.5 43.9 %copy-start.1 = (bf16[1,2048,512]{2,1,0:T(8,128)(2,1)S(1)}, bf16[1,2048,512]{2,1,0:T(8,128)(2,1)}, u32[]{:S(2)}) copy-start(bf16[1,2048,512]{2,1,0:T(8,128)(2,1)} %param.8) | copy-start | bytes 6291460
  56.0 27.4 %copy-start = (bf16[1,2048,512]{2,1,0:T(8,128)(2,1)S(1)}, bf16[1,2048,512]{2,1,0:T(8,128)(2,1)}, u32[]{:S(2)}) copy-start(bf16[1,2048,512]{2,1,0:T(8,128)(2,1)} %param.7) | copy-start | bytes 6291460
  56.0 1.5 %collective-permute-start.2 = (bf16[256,512]{1,0:T(8,128)(2,1)S(1)}, bf16[256,512]{1,0:T(8,128)(2,1)S(1)}, u32[]{:S(2)}, u32[]{:S(2)}) collective-permute-start(bf16[256,512]{1,0:T(8,128)(2,1)S(1)} %get-tuple-element.28), channel_id=1, source_target_pairs={{0,4},{4,0},{1,5},{5,1},{2,6},{6,2},{3,7},{7,3},{8,12},{12,8},{9,1... | collective-permute-start | bytes 786440 | tf_op jit(solution)/shard_map/ppermute | solution.py:110
  79.3 4.1 %collective-permute-start.3 = (bf16[256,512]{1,0:T(8,128)(2,1)S(1)}, bf16[256,512]{1,0:T(8,128)(2,1)S(1)}, u32[]{:S(2)}, u32[]{:S(2)}) collective-permute-start(bf16[256,512]{1,0:T(8,128)(2,1)S(1)} %bitcast.21), channel_id=1, source_target_pairs={{0,4},{4,0},{1,5},{5,1},{2,6},{6,2},{3,7},{7,3},{8,12},{12,8},{9,1... | collective-permute-start | bytes 786440 | tf_op jit(solution)/shard_map/ppermute | solution.py:110
  84.0 7.6 %collective-permute-start.5 = (bf16[512,256]{1,0:T(8,128)(2,1)S(1)}, bf16[512,256]{1,0:T(8,128)(2,1)S(1)}, u32[]{:S(2)}, u32[]{:S(2)}) collective-permute-start(bf16[512,256]{1,0:T(8,128)(2,1)S(1)} %get-tuple-element.35), channel_id=1, source_target_pairs={{0,1},{1,2},{2,3},{3,0},{4,5},{5,6},{6,7},{7,4},{8,9},{9,10},{10,1... | collective-permute-start | bytes 786440 | tf_op jit(solution)/shard_map/ppermute | solution.py:295
  85.2 7.2 %collective-permute-start.6 = (bf16[512,256]{1,0:T(8,128)(2,1)S(1)}, bf16[512,256]{1,0:T(8,128)(2,1)S(1)}, u32[]{:S(2)}, u32[]{:S(2)}) collective-permute-start(bf16[512,256]{1,0:T(8,128)(2,1)S(1)} %get-tuple-element.36), channel_id=1, source_target_pairs={{0,3},{1,0},{2,1},{3,2},{4,7},{5,4},{6,5},{7,6},{8,11},{9,8},{10,9... | collective-permute-start | bytes 786440 | tf_op jit(solution)/shard_map/ppermute | solution.py:295
  86.0 12.5 %collective-permute-start.4 = (bf16[512,256]{1,0:T(8,128)(2,1)S(1)}, bf16[512,256]{1,0:T(8,128)(2,1)S(1)}, u32[]{:S(2)}, u32[]{:S(2)}) collective-permute-start(bf16[512,256]{1,0:T(8,128)(2,1)S(1)} %get-tuple-element.34), channel_id=1, source_target_pairs={{0,3},{1,0},{2,1},{3,2},{4,7},{5,4},{6,5},{7,6},{8,11},{9,8},{10,9... | collective-permute-start | bytes 786440 | tf_op jit(solution)/shard_map/ppermute | solution.py:295
  87.5 10.9 %collective-permute-start.9 = (bf16[512,256]{1,0:T(8,128)(2,1)S(1)}, bf16[512,256]{1,0:T(8,128)(2,1)S(1)}, u32[]{:S(2)}, u32[]{:S(2)}) collective-permute-start(bf16[512,256]{1,0:T(8,128)(2,1)S(1)} %get-tuple-element.40), channel_id=1, source_target_pairs={{0,1},{1,2},{2,3},{3,0},{4,5},{5,6},{6,7},{7,4},{8,9},{9,10},{10,1... | collective-permute-start | bytes 786440 | tf_op jit(solution)/shard_map/ppermute | solution.py:295
  92.9 9.8 %collective-permute-start.7 = (bf16[512,256]{1,0:T(8,128)(2,1)S(1)}, bf16[512,256]{1,0:T(8,128)(2,1)S(1)}, u32[]{:S(2)}, u32[]{:S(2)}) collective-permute-start(bf16[512,256]{1,0:T(8,128)(2,1)S(1)} %get-tuple-element.37), channel_id=1, source_target_pairs={{0,1},{1,2},{2,3},{3,0},{4,5},{5,6},{6,7},{7,4},{8,9},{9,10},{10,1... | collective-permute-start | bytes 786440 | tf_op jit(solution)/shard_map/ppermute | solution.py:295
  93.9 1.2 %copy-start.2 = (bf16[2048,256]{1,0:T(8,128)(2,1)S(1)}, bf16[2048,256]{1,0:T(8,128)(2,1)}, u32[]{:S(2)}) copy-start(bf16[2048,256]{1,0:T(8,128)(2,1)} %e_ref.3) | copy-start | bytes 3145732
  93.9 1.5 %copy-start.3 = (bf16[2048,256]{1,0:T(8,128)(2,1)S(1)}, bf16[2048,256]{1,0:T(8,128)(2,1)}, u32[]{:S(2)}) copy-start(bf16[2048,256]{1,0:T(8,128)(2,1)} %f_ref.3) | copy-start | bytes 3145732
  93.9 9.8 %collective-permute-start.8 = (bf16[512,256]{1,0:T(8,128)(2,1)S(1)}, bf16[512,256]{1,0:T(8,128)(2,1)S(1)}, u32[]{:S(2)}, u32[]{:S(2)}) collective-permute-start(bf16[512,256]{1,0:T(8,128)(2,1)S(1)} %get-tuple-element.39), channel_id=1, source_target_pairs={{0,3},{1,0},{2,1},{3,2},{4,7},{5,4},{6,5},{7,6},{8,11},{9,8},{10,9... | collective-permute-start | bytes 786440 | tf_op jit(solution)/shard_map/ppermute | solution.py:295

commit v8 on v7

--- a/solution.py
+++ b/solution.py
@@ -284,9 +284,26 @@
     )(e, f, *pieces)
 
 
-def mixer_sum_kernel(own_e, down_e, up_e, own_f, down_f, up_f, de, df):
-    for own, down, up, out in ((own_e, down_e, up_e, de), (own_f, down_f, up_f, df)):
-        out[...] = own[...] + (down[...].astype(F32) + up[...].astype(F32))
+def mixer_sum_kernel(own_e, down_e, up_e, own_f, down_f, up_f, de, df, sums, sem):
+    rows = own_e.shape[0] // 2
+    copies = []
+    for at, (own, down, up, out) in enumerate(
+        ((own_e, down_e, up_e, de), (own_f, down_f, up_f, df))
+    ):
+        for part in range(2):
+            cut = slice(part * rows, (part + 1) * rows)
+            sums[at, cut, :] = own[cut, :] + (
+                down[cut, :].astype(F32) + up[cut, :].astype(F32)
+            )
+            copy = pltpu.make_async_copy(
+                sums.at[at, pl.ds(part * rows, rows), :],
+                out.at[pl.ds(part * rows, rows), :],
+                sem.at[at, part],
+            )
+            copy.start()
+            copies.append(copy)
+    for copy in copies:
+        copy.wait()
 
 
 def along(value, step):
@@ -306,8 +323,12 @@
     return pl.pallas_call(
         mixer_sum_kernel,
         in_specs=[VM] * 6,
-        out_specs=[VM] * 2,
+        out_specs=[pl.BlockSpec(memory_space=pltpu.MemorySpace.HBM)] * 2,
         out_shape=[shape_of(*own_e.shape, F32)] * 2,
+        scratch_shapes=[
+            pltpu.VMEM((2, *own_e.shape), F32),
+            pltpu.SemaphoreType.DMA((2, 2)),
+        ],
         compiler_params=pltpu.CompilerParams(vmem_limit_bytes=8 << 20),
         cost_estimate=cost(1 << 20, 3 << 20),
         name="mixer_sum",

time: 106 us -> 106 us (level)
  no operation moved by 1% of the time
where the time goes in v8:
time: 106 us; the launch traced here: 105 us
  blocking collectives  50.4 us (48%)
  Pallas kernels  26.1 us (25%)
  waiting for transfers between devices  15.2 us (14%)
  starting transfers between devices  11.6 us (11%)
    all_to_all x2, blocking collectives, total_over_seq(): lax.all_to_all(part.reshape(size, rows // size, width), chips, 0, 0, tile...  28.7 us
    all_to_all x2, blocking collectives, total_over_seq(): lax.all_to_all(sum_copies(got), chips, 0, 0, tiled=True)  21.7 us
    pallas_call x1, Pallas kernels, attend(): pl.pallas_call(attend_kernel, grid=(tokens // rows,), in_specs=[wide, wid...  16.5 us
    ppermute x6, waiting for transfers between devices, along(): return lax.ppermute(value, ACROSS, pairs)  10.2 us
    ppermute x4, starting transfers between devices, swap(): return lax.ppermute(value, 'seq_2', [(0, 1), (1, 0)])  7.01 us
    ppermute x4, waiting for transfers between devices, swap(): return lax.ppermute(value, 'seq_2', [(0, 1), (1, 0)])  5.02 us
    ppermute x6, starting transfers between devices, along(): return lax.ppermute(value, ACROSS, pairs)  4.6 us
    pallas_call x1, Pallas kernels, project(): pl.pallas_call(project_kernel, in_specs=[hbm] * 4, out_specs=[VM] * 2, ou...  3.56 us
  transfers between devices with their start and end apart: 10, of which 8 were waited for; matrix products, arithmetic and copies ran while one was open for 0% of the time, Pallas kernels for 4%

profile of v8, /device:TPU:3, one launch (start us, length us, event | category | flops | bytes accessed | tf_op | source)
XLA Modules:
  0.0 104.7 jit_solution(11808492383398646524)
XLA Ops:
  0.6 0.0 copy-start.5
  0.6 3.6 %project.1 = (f32[256,512]{1,0:T(8,128)S(1)}, f32[256,512]{1,0:T(8,128)S(1)}) custom-call(bf16[2048,512]{1,0:T(8,128)(2,1)} %bitcast.11, bf16[2048,512]{1,0:T(8,128)(2,1)} %bitcast.16, bf16[2048,256]{1,0:T(8,128)(2,1)} %e_ref.3, bf16[2048,256]{1,0:T(8,128)(2,1)} %f_ref.3), custom_call_target="tpu_custom_call" | custom-call | flops 1073741824 | bytes 6291456 | tf_op jit(solution)/shard_map/project/pallas_call | solution.py:73
  4.2 0.0 copy-start.4
  4.2 0.8 collective-permute-start
  5.0 1.5 %collective-permute-done = f32[256,512]{1,0:T(8,128)S(1)} collective-permute-done((f32[256,512]{1,0:T(8,128)S(1)}, f32[256,512]{1,0:T(8,128)S(1)}, u32[]{:S(2)}, u32[]{:S(2)}) %collective-permute-start) | collective-permute-done | bytes 524320 | tf_op jit(solution)/shard_map/ppermute | solution.py:110
  6.5 0.1 add.6
  6.6 17.9 %all_to_all.20.got = f32[16,16,512]{2,1,0:T(8,128)S(1)} all-to-all(f32[16,16,512]{2,1,0:T(8,128)S(1)} %bitcast.27), channel_id=1, replica_groups=mesh['seq_0'=4,'seq_1'=4,'seq_2'=2,'head'=2,'rep'=2] {'seq_0','seq_1'}, dimensions={0} | all-to-all | bytes 1048576 | tf_op jit(solution)/shard_map/all_to_all | solution.py:118
  24.6 10.8 %all_to_all.21 = bf16[16,16,512]{2,1,0:T(8,128)(2,1)S(1)} all-to-all(bf16[16,16,512]{2,1,0:T(8,128)(2,1)S(1)} %sum_copies.2), channel_id=1, replica_groups=mesh['seq_0'=4,'seq_1'=4,'seq_2'=2,'head'=2,'rep'=2] {'seq_0','seq_1'}, dimensions={0} | all-to-all | bytes 524288 | tf_op jit(solution)/shard_map/all_to_all | solution.py:121
  35.4 2.9 %collective-permute-start.1 = (bf16[256,512]{1,0:T(8,128)(2,1)S(1)}, bf16[256,512]{1,0:T(8,128)(2,1)S(1)}, u32[]{:S(2)}, u32[]{:S(2)}) collective-permute-start(bf16[256,512]{1,0:T(8,128)(2,1)S(1)} %bitcast.23), channel_id=1, source_target_pairs={{0,4},{4,0},{1,5},{5,1},{2,6},{6,2},{3,7},{7,3},{8,12},{12,8},{9,1... | collective-permute-start | bytes 786440 | tf_op jit(solution)/shard_map/ppermute | solution.py:110
  38.4 1.2 %collective-permute-done.1.other = bf16[256,512]{1,0:T(8,128)(2,1)S(1)} collective-permute-done((bf16[256,512]{1,0:T(8,128)(2,1)S(1)}, bf16[256,512]{1,0:T(8,128)(2,1)S(1)}, u32[]{:S(2)}, u32[]{:S(2)}) %collective-permute-start.1) | collective-permute-done | bytes 262176 | tf_op jit(solution)/shard_map/ppermute | solution.py:110
  39.5 0.0 copy-done.5
  39.5 0.0 copy-done.4
  39.5 0.0 copy-start.1
  39.5 16.5 %attend.1 = (bf16[2048,512]{1,0:T(8,128)(2,1)}, f32[256,512]{1,0:T(8,128)S(1)}, bf16[256,512]{1,0:T(8,128)(2,1)S(1)}) custom-call(bf16[2048,512]{1,0:T(8,128)(2,1)S(1)} %bitcast.25, bf16[2048,512]{1,0:T(8,128)(2,1)S(1)} %bitcast.26, bf16[256,512]{1,0:T(8,128)(2,1)S(1)} %bitcast.24, bf16[256,512]{1,0:T(8,128)(2,1)S(1)} %collective-permute-done.1.other), custom_call_target="tpu_custom_call" | custom-call | flops 4294967296 | bytes 8388608 | tf_op jit(solution)/shard_map/attend/pallas_call | solution.py:196
  56.0 0.0 copy-start
  56.0 0.4 collective-permute-start.2
  56.4 1.2 %collective-permute-done.2 = bf16[256,512]{1,0:T(8,128)(2,1)S(1)} collective-permute-done((bf16[256,512]{1,0:T(8,128)(2,1)S(1)}, bf16[256,512]{1,0:T(8,128)(2,1)S(1)}, u32[]{:S(2)}, u32[]{:S(2)}) %collective-permute-start.2) | collective-permute-done | bytes 262176 | tf_op jit(solution)/shard_map/ppermute | solution.py:110
  57.6 0.1 add_convert_fusion
  57.6 10.8 %all_to_all.22.got = bf16[16,16,512]{2,1,0:T(8,128)(2,1)S(1)} all-to-all(bf16[16,16,512]{2,1,0:T(8,128)(2,1)S(1)} %bitcast.28), channel_id=1, replica_groups=mesh['seq_0'=4,'seq_1'=4,'seq_2'=2,'head'=2,'rep'=2] {'seq_0','seq_1'}, dimensions={0} | all-to-all | bytes 524288 | tf_op jit(solution)/shard_map/all_to_all | solution.py:118
  68.4 10.9 %all_to_all.23 = bf16[16,16,512]{2,1,0:T(8,128)(2,1)S(1)} all-to-all(bf16[16,16,512]{2,1,0:T(8,128)(2,1)S(1)} %sum_copies.3), channel_id=1, replica_groups=mesh['seq_0'=4,'seq_1'=4,'seq_2'=2,'head'=2,'rep'=2] {'seq_0','seq_1'}, dimensions={0} | all-to-all | bytes 524288 | tf_op jit(solution)/shard_map/all_to_all | solution.py:121
  79.3 2.9 %collective-permute-start.3 = (bf16[256,512]{1,0:T(8,128)(2,1)S(1)}, bf16[256,512]{1,0:T(8,128)(2,1)S(1)}, u32[]{:S(2)}, u32[]{:S(2)}) collective-permute-start(bf16[256,512]{1,0:T(8,128)(2,1)S(1)} %bitcast.21), channel_id=1, source_target_pairs={{0,4},{4,0},{1,5},{5,1},{2,6},{6,2},{3,7},{7,3},{8,12},{12,8},{9,1... | collective-permute-start | bytes 786440 | tf_op jit(solution)/shard_map/ppermute | solution.py:110
  82.2 1.2 %collective-permute-done.3.other = bf16[256,512]{1,0:T(8,128)(2,1)S(1)} collective-permute-done((bf16[256,512]{1,0:T(8,128)(2,1)S(1)}, bf16[256,512]{1,0:T(8,128)(2,1)S(1)}, u32[]{:S(2)}, u32[]{:S(2)}) %collective-permute-start.3) | collective-permute-done | bytes 262176 | tf_op jit(solution)/shard_map/ppermute | solution.py:110
  83.5 0.0 copy-done.1
  83.5 0.0 copy-done
  83.5 0.5 mixer_part.6
  84.0 1.3 %collective-permute-start.5 = (bf16[512,256]{1,0:T(8,128)(2,1)S(1)}, bf16[512,256]{1,0:T(8,128)(2,1)S(1)}, u32[]{:S(2)}, u32[]{:S(2)}) collective-permute-start(bf16[512,256]{1,0:T(8,128)(2,1)S(1)} %get-tuple-element.35), channel_id=1, source_target_pairs={{0,1},{1,2},{2,3},{3,0},{4,5},{5,6},{6,7},{7,4},{8,9},{9,10},{10,1... | collective-permute-start | bytes 786440 | tf_op jit(solution)/shard_map/ppermute | solution.py:312
  85.2 0.3 collective-permute-start.6
  85.5 0.5 mixer_part.5
  86.0 1.5 %collective-permute-start.4 = (bf16[512,256]{1,0:T(8,128)(2,1)S(1)}, bf16[512,256]{1,0:T(8,128)(2,1)S(1)}, u32[]{:S(2)}, u32[]{:S(2)}) collective-permute-start(bf16[512,256]{1,0:T(8,128)(2,1)S(1)} %get-tuple-element.34), channel_id=1, source_target_pairs={{0,3},{1,0},{2,1},{3,2},{4,7},{5,4},{6,5},{7,6},{8,11},{9,8},{10,9... | collective-permute-start | bytes 786440 | tf_op jit(solution)/shard_map/ppermute | solution.py:312
  87.5 0.0 collective-permute-start.9
  87.5 4.0 %collective-permute-done.5.refs_0_ = bf16[512,256]{1,0:T(8,128)(2,1)S(1)} collective-permute-done((bf16[512,256]{1,0:T(8,128)(2,1)S(1)}, bf16[512,256]{1,0:T(8,128)(2,1)S(1)}, u32[]{:S(2)}, u32[]{:S(2)}) %collective-permute-start.5) | collective-permute-done | bytes 262176 | tf_op jit(solution)/shard_map/ppermute | solution.py:312
  91.5 0.9 collective-permute-done.6.refs_1_
  92.4 0.5 mixer_part.7
  92.9 1.0 collective-permute-start.7
  93.9 0.0 copy-start.2
  93.9 0.0 copy-start.3
  93.9 0.5 collective-permute-start.8
  94.5 0.5 mixer_part.4
  94.9 0.2 copy-done.2
  95.1 0.3 copy-done.3
  95.5 3.0 %input_grads.1 = (bf16[2048,512]{1,0:T(8,128)(2,1)}, bf16[2048,512]{1,0:T(8,128)(2,1)}) custom-call(bf16[2048,256]{1,0:T(8,128)(2,1)S(1)} %copy-done.2, bf16[2048,256]{1,0:T(8,128)(2,1)S(1)} %copy-done.3, bf16[256,512]{1,0:T(8,128)(2,1)S(1)} %get-tuple-element.29.dpk, bf16[256,512]{1,0:T(8,128)(2,1)S(1)} %get-tuple-element.30.dpv), custom_call_target="tpu_custom_call" | custom-call | flops 1073741824 | bytes 6291456 | tf_op jit(solution)/shard_map/input_grads/pallas_call | solution.py:275
  98.4 0.0 collective-permute-done.4.down_e
  98.4 0.0 collective-permute-done.9.up_f
  98.4 4.3 %collective-permute-done.7.up_e = bf16[512,256]{1,0:T(8,128)(2,1)S(1)} collective-permute-done((bf16[512,256]{1,0:T(8,128)(2,1)S(1)}, bf16[512,256]{1,0:T(8,128)(2,1)S(1)}, u32[]{:S(2)}, u32[]{:S(2)}) %collective-permute-start.7) | collective-permute-done | bytes 262176 | tf_op jit(solution)/shard_map/ppermute | solution.py:312
  102.8 0.9 collective-permute-done.8.down_f
  103.7 1.0 mixer_sum.1
  (3 shorter events, 0.1 us)
Async XLA Ops:
  0.6 38.9 %copy-start.5 = (bf16[1,2048,512]{2,1,0:T(8,128)(2,1)S(1)}, bf16[1,2048,512]{2,1,0:T(8,128)(2,1)}, u32[]{:S(2)}) copy-start(bf16[1,2048,512]{2,1,0:T(8,128)(2,1)} %param.9) | copy-start | bytes 6291460
  4.2 35.3 %copy-start.4 = (bf16[1,2048,512]{2,1,0:T(8,128)(2,1)S(1)}, bf16[1,2048,512]{2,1,0:T(8,128)(2,1)}, u32[]{:S(2)}) copy-start(bf16[1,2048,512]{2,1,0:T(8,128)(2,1)} %param.6) | copy-start | bytes 6291460
  4.2 2.3 %collective-permute-start = (f32[256,512]{1,0:T(8,128)S(1)}, f32[256,512]{1,0:T(8,128)S(1)}, u32[]{:S(2)}, u32[]{:S(2)}) collective-permute-start(f32[256,512]{1,0:T(8,128)S(1)} %get-tuple-element.25), channel_id=1, source_target_pairs={{0,4},{4,0},{1,5},{5,1},{2,6},{6,2},{3,7},{7,3},{8,12},{12,8},{9,1... | collective-permute-start | bytes 1572872 | tf_op jit(solution)/shard_map/ppermute | solution.py:110
  35.4 4.1 %collective-permute-start.1 = (bf16[256,512]{1,0:T(8,128)(2,1)S(1)}, bf16[256,512]{1,0:T(8,128)(2,1)S(1)}, u32[]{:S(2)}, u32[]{:S(2)}) collective-permute-start(bf16[256,512]{1,0:T(8,128)(2,1)S(1)} %bitcast.23), channel_id=1, source_target_pairs={{0,4},{4,0},{1,5},{5,1},{2,6},{6,2},{3,7},{7,3},{8,12},{12,8},{9,1... | collective-permute-start | bytes 786440 | tf_op jit(solution)/shard_map/ppermute | solution.py:110
  39.5 43.9 %copy-start.1 = (bf16[1,2048,512]{2,1,0:T(8,128)(2,1)S(1)}, bf16[1,2048,512]{2,1,0:T(8,128)(2,1)}, u32[]{:S(2)}) copy-start(bf16[1,2048,512]{2,1,0:T(8,128)(2,1)} %param.8) | copy-start | bytes 6291460
  56.0 27.4 %copy-start = (bf16[1,2048,512]{2,1,0:T(8,128)(2,1)S(1)}, bf16[1,2048,512]{2,1,0:T(8,128)(2,1)}, u32[]{:S(2)}) copy-start(bf16[1,2048,512]{2,1,0:T(8,128)(2,1)} %param.7) | copy-start | bytes 6291460
  56.0 1.5 %collective-permute-start.2 = (bf16[256,512]{1,0:T(8,128)(2,1)S(1)}, bf16[256,512]{1,0:T(8,128)(2,1)S(1)}, u32[]{:S(2)}, u32[]{:S(2)}) collective-permute-start(bf16[256,512]{1,0:T(8,128)(2,1)S(1)} %get-tuple-element.28), channel_id=1, source_target_pairs={{0,4},{4,0},{1,5},{5,1},{2,6},{6,2},{3,7},{7,3},{8,12},{12,8},{9,1... | collective-permute-start | bytes 786440 | tf_op jit(solution)/shard_map/ppermute | solution.py:110
  79.3 4.1 %collective-permute-start.3 = (bf16[256,512]{1,0:T(8,128)(2,1)S(1)}, bf16[256,512]{1,0:T(8,128)(2,1)S(1)}, u32[]{:S(2)}, u32[]{:S(2)}) collective-permute-start(bf16[256,512]{1,0:T(8,128)(2,1)S(1)} %bitcast.21), channel_id=1, source_target_pairs={{0,4},{4,0},{1,5},{5,1},{2,6},{6,2},{3,7},{7,3},{8,12},{12,8},{9,1... | collective-permute-start | bytes 786440 | tf_op jit(solution)/shard_map/ppermute | solution.py:110
  84.0 7.6 %collective-permute-start.5 = (bf16[512,256]{1,0:T(8,128)(2,1)S(1)}, bf16[512,256]{1,0:T(8,128)(2,1)S(1)}, u32[]{:S(2)}, u32[]{:S(2)}) collective-permute-start(bf16[512,256]{1,0:T(8,128)(2,1)S(1)} %get-tuple-element.35), channel_id=1, source_target_pairs={{0,1},{1,2},{2,3},{3,0},{4,5},{5,6},{6,7},{7,4},{8,9},{9,10},{10,1... | collective-permute-start | bytes 786440 | tf_op jit(solution)/shard_map/ppermute | solution.py:312
  85.2 7.2 %collective-permute-start.6 = (bf16[512,256]{1,0:T(8,128)(2,1)S(1)}, bf16[512,256]{1,0:T(8,128)(2,1)S(1)}, u32[]{:S(2)}, u32[]{:S(2)}) collective-permute-start(bf16[512,256]{1,0:T(8,128)(2,1)S(1)} %get-tuple-element.36), channel_id=1, source_target_pairs={{0,3},{1,0},{2,1},{3,2},{4,7},{5,4},{6,5},{7,6},{8,11},{9,8},{10,9... | collective-permute-start | bytes 786440 | tf_op jit(solution)/shard_map/ppermute | solution.py:312
  86.0 12.5 %collective-permute-start.4 = (bf16[512,256]{1,0:T(8,128)(2,1)S(1)}, bf16[512,256]{1,0:T(8,128)(2,1)S(1)}, u32[]{:S(2)}, u32[]{:S(2)}) collective-permute-start(bf16[512,256]{1,0:T(8,128)(2,1)S(1)} %get-tuple-element.34), channel_id=1, source_target_pairs={{0,3},{1,0},{2,1},{3,2},{4,7},{5,4},{6,5},{7,6},{8,11},{9,8},{10,9... | collective-permute-start | bytes 786440 | tf_op jit(solution)/shard_map/ppermute | solution.py:312
  87.5 10.9 %collective-permute-start.9 = (bf16[512,256]{1,0:T(8,128)(2,1)S(1)}, bf16[512,256]{1,0:T(8,128)(2,1)S(1)}, u32[]{:S(2)}, u32[]{:S(2)}) collective-permute-start(bf16[512,256]{1,0:T(8,128)(2,1)S(1)} %get-tuple-element.40), channel_id=1, source_target_pairs={{0,1},{1,2},{2,3},{3,0},{4,5},{5,6},{6,7},{7,4},{8,9},{9,10},{10,1... | collective-permute-start | bytes 786440 | tf_op jit(solution)/shard_map/ppermute | solution.py:312
  92.9 9.8 %collective-permute-start.7 = (bf16[512,256]{1,0:T(8,128)(2,1)S(1)}, bf16[512,256]{1,0:T(8,128)(2,1)S(1)}, u32[]{:S(2)}, u32[]{:S(2)}) collective-permute-start(bf16[512,256]{1,0:T(8,128)(2,1)S(1)} %get-tuple-element.37), channel_id=1, source_target_pairs={{0,1},{1,2},{2,3},{3,0},{4,5},{5,6},{6,7},{7,4},{8,9},{9,10},{10,1... | collective-permute-start | bytes 786440 | tf_op jit(solution)/shard_map/ppermute | solution.py:312
  93.9 1.2 %copy-start.2 = (bf16[2048,256]{1,0:T(8,128)(2,1)S(1)}, bf16[2048,256]{1,0:T(8,128)(2,1)}, u32[]{:S(2)}) copy-start(bf16[2048,256]{1,0:T(8,128)(2,1)} %e_ref.3) | copy-start | bytes 3145732
  93.9 1.5 %copy-start.3 = (bf16[2048,256]{1,0:T(8,128)(2,1)S(1)}, bf16[2048,256]{1,0:T(8,128)(2,1)}, u32[]{:S(2)}) copy-start(bf16[2048,256]{1,0:T(8,128)(2,1)} %f_ref.3) | copy-start | bytes 3145732
  93.9 9.8 %collective-permute-start.8 = (bf16[512,256]{1,0:T(8,128)(2,1)S(1)}, bf16[512,256]{1,0:T(8,128)(2,1)S(1)}, u32[]{:S(2)}, u32[]{:S(2)}) collective-permute-start(bf16[512,256]{1,0:T(8,128)(2,1)S(1)} %get-tuple-element.39), channel_id=1, source_target_pairs={{0,3},{1,0},{2,1},{3,2},{4,7},{5,4},{6,5},{7,6},{8,11},{9,8},{10,9... | collective-permute-start | bytes 786440 | tf_op jit(solution)/shard_map/ppermute | solution.py:312
